TPU v7x, 32 devices: a whole 2x2x4 slice. The times are simulated.
32 devices in a mesh: dp: 32 (over z, y, x, core).
Axes of the slice: x: 2, y: 2, z: 4, core: 2. Of those that a mesh axis runs over, the one named last changes fastest.
Arguments:
- block_in: bfloat16 [131072, 384], P('dp'), may hold values from -6 to 6
- out_grad: bfloat16 [131072, 384], P('dp'), may hold values from -6 to 6
- live_counts: int32 [32], P('dp'), may hold values from 4 to 16, as said below
- qkv_weight: float32 [384, 1152], P(None, 'dp'), may hold values from -0.3125 to 0.3125
- proj_weight: float32 [384, 384], P(None, 'dp'), may hold values from -1.25 to 1.25
- up_weight: float32 [384, 1536], P(None, 'dp'), may hold values from -0.3125 to 0.3125
- down_weight: float32 [384, 1536], P(None, 'dp'), may hold values from -0.15625 to 0.15625
- feature_vectors: float32 [8, 384], replicated, may hold values from -0.6 to 1.5, as said below
- up_bias: float32 [1536], replicated, may hold values from -3 to 3
- qkv_moment: float32 [384, 1152], P(None, 'dp'), may hold values from -320 to 320
- proj_moment: float32 [384, 384], P(None, 'dp'), may hold values from -112 to 112
- up_moment: float32 [384, 1536], P(None, 'dp'), may hold values from -320 to 320
- down_moment: float32 [384, 1536], P(None, 'dp'), may hold values from -640 to 640
Outputs:
- block_out: float32 [131072, 384], P('dp')
- input_gradient: float32 [131072, 384], P('dp')
- qkv_gradient: float32 [384, 1152], P(None, 'dp')
- proj_gradient: float32 [384, 384], P(None, 'dp')
- up_gradient: float32 [384, 1536], P(None, 'dp')
- down_gradient: float32 [384, 1536], P(None, 'dp')
- vector_gradient: float32 [8, 384], replicated
- bias_gradient: float32 [1536], replicated
- qkv_updated: float32 [384, 1152], P(None, 'dp')
- proj_updated: float32 [384, 384], P(None, 'dp')
- up_updated: float32 [384, 1536], P(None, 'dp')
- down_updated: float32 [384, 1536], P(None, 'dp')
- qkv_state: float32 [384, 1152], P(None, 'dp')
- proj_state: float32 [384, 384], P(None, 'dp')
- up_state: float32 [384, 1536], P(None, 'dp')
- down_state: float32 [384, 1536], P(None, 'dp')
- vectors_updated: float32 [8, 384], replicated
- bias_updated: float32 [1536], replicated
Inputs may be any that keep to these rules, and one draw needn't show every extreme that they name: The first live_counts[p] of the 16 image slots of index p are live; some index has all 16 live. `feature_vectors`: rows 0 and 5 lie in 0.5 to 1.5.
All inputs are finite; a program needn't handle non-finite values.
Results may differ from a plain program's by a relative error of at most 0.011.
Values may be sent and summed in bfloat16 or wider, within the bound.
No kernel may reach another device: no remote copies, remote signals or barrier semaphores. Data moves between devices by JAX's collectives and lax.ppermute only.
A program may use at most 192 MiB of HBM per device.

v0:
```python
import math

import jax
import jax.numpy as jnp
from jax import lax
from jax.sharding import PartitionSpec as P

HEAD_DIM = 64
SEQ = 256
ATT_BLK = 2


norm_eps = 1e-06
newton_a = 3.4445
newton_b = -4.775
newton_c = 2.0315
momentum_decay = 0.9
matrix_rate = 0.15
vector_rate = 0.2


def layer_norm(inputs, gain, shift):
    center = inputs - jnp.mean(inputs, axis=-1, keepdims=True)
    scale = lax.rsqrt(jnp.mean(center * center, axis=-1, keepdims=True) + norm_eps)
    normed = center * scale
    return (normed, scale, normed * gain + shift)


def norm_back(upstream, normed, scale, gain):
    inner = upstream * gain
    return scale * (
        inner
        - jnp.mean(inner, axis=-1, keepdims=True)
        - normed * jnp.mean(inner * normed, axis=-1, keepdims=True)
    )


def gelu_exact(values):
    return 0.5 * values * (1.0 + lax.erf(values * (1.0 / math.sqrt(2.0))))


def gelu_slope(values):
    return 0.5 * (1.0 + lax.erf(values * (1.0 / math.sqrt(2.0)))) + values * jnp.exp(
        -0.5 * values * values
    ) * (1.0 / math.sqrt(2.0 * math.pi))


def contract_rows(left, right):
    return lax.dot_general(
        left, right, (((0,), (0,)), ((), ())), preferred_element_type=jnp.float32
    )


def contract_cols(left, right):
    return lax.dot_general(
        left, right, (((1,), (1,)), ((), ())), preferred_element_type=jnp.float32
    )


def block_pass(inputs, cotangent, alive, qkv_b, proj_b, up_b, down_b, vectors, up_bias):
    count = inputs.shape[0]
    width = inputs.shape[2]
    rows = count * SEQ
    heads = width // HEAD_DIM
    scale_qk = 1.0 / math.sqrt(HEAD_DIM)

    def split(array):
        return array.reshape(count, SEQ, heads, HEAD_DIM)

    residual = inputs.reshape(rows, width).astype(jnp.float32)
    row_alive = jnp.repeat(alive, SEQ)[:, None]
    normed_one, scale_one, mixed_one = layer_norm(residual, vectors[0], vectors[1])
    normal_one = mixed_one.astype(jnp.bfloat16)
    projected = jnp.dot(normal_one, qkv_b, preferred_element_type=jnp.float32)
    query = (projected[:, :width] + vectors[2]).astype(jnp.bfloat16)
    keys = projected[:, width : 2 * width].astype(jnp.bfloat16)
    values = (projected[:, 2 * width :] + vectors[3]).astype(jnp.bfloat16)
    query_h = split(query)
    keys_h = split(keys)
    values_h = split(values)
    scores = (
        jnp.einsum("nqhd,nkhd->nhqk", query_h, keys_h, preferred_element_type=jnp.float32)
        * scale_qk
    )
    top = jnp.max(scores, axis=-1, keepdims=True)
    log_total = top + jnp.log(jnp.sum(jnp.exp(scores - top), axis=-1, keepdims=True))
    attend_b = jnp.exp(scores - log_total).astype(jnp.bfloat16)
    heads_out = jnp.einsum(
        "nhqk,nkhd->nqhd", attend_b, values_h, preferred_element_type=jnp.float32
    )
    attn_b = heads_out.reshape(rows, width).astype(jnp.bfloat16)
    hidden_one = residual + jnp.dot(attn_b, proj_b, preferred_element_type=jnp.float32) + vectors[4]
    normed_two, scale_two, mixed_two = layer_norm(hidden_one, vectors[5], vectors[6])
    normal_two = mixed_two.astype(jnp.bfloat16)
    pre_act = jnp.dot(normal_two, up_b, preferred_element_type=jnp.float32) + up_bias
    active = gelu_exact(pre_act).astype(jnp.bfloat16)
    down_out = contract_cols(active, down_b)
    result = (hidden_one + down_out + vectors[7]) * row_alive
    cot_b = jnp.where(row_alive > 0.5, cotangent.reshape(rows, width), jnp.zeros((), jnp.bfloat16))
    cot_f = cot_b.astype(jnp.float32)
    down_grad = contract_rows(cot_b, active)
    pre_grad = jnp.dot(cot_b, down_b, preferred_element_type=jnp.float32) * gelu_slope(pre_act)
    pre_grad_b = pre_grad.astype(jnp.bfloat16)
    up_grad = contract_rows(normal_two, pre_grad_b)
    mixed_two_grad = contract_cols(pre_grad_b, up_b)
    hidden_grad = norm_back(mixed_two_grad, normed_two, scale_two, vectors[5]) + cot_f
    hidden_grad_b = hidden_grad.astype(jnp.bfloat16)
    proj_grad = contract_rows(attn_b, hidden_grad_b)
    attn_grad_b = contract_cols(hidden_grad_b, proj_b).astype(jnp.bfloat16)
    attn_grad_h = split(attn_grad_b)
    delta = jnp.sum(attn_grad_h.astype(jnp.float32) * split(attn_b).astype(jnp.float32), axis=-1)
    delta = jnp.transpose(delta, (0, 2, 1))[..., None]
    scores = (
        jnp.einsum("nqhd,nkhd->nhqk", query_h, keys_h, preferred_element_type=jnp.float32)
        * scale_qk
    )
    attend = jnp.exp(scores - log_total)
    values_grad = jnp.einsum(
        "nhqk,nqhd->nkhd", attend_b, attn_grad_h, preferred_element_type=jnp.float32
    )
    attend_grad = jnp.einsum(
        "nqhd,nkhd->nhqk", attn_grad_h, values_h, preferred_element_type=jnp.float32
    )
    score_grad = (attend * (attend_grad - delta) * scale_qk).astype(jnp.bfloat16)
    query_grad = jnp.einsum(
        "nhqk,nkhd->nqhd", score_grad, keys_h, preferred_element_type=jnp.float32
    ).reshape(rows, width)
    keys_grad = jnp.einsum(
        "nhqk,nqhd->nkhd", score_grad, query_h, preferred_element_type=jnp.float32
    ).reshape(rows, width)
    values_grad = values_grad.reshape(rows, width)
    packed_grad = jnp.concatenate([query_grad, keys_grad, values_grad], axis=1).astype(jnp.bfloat16)
    qkv_grad = contract_rows(normal_one, packed_grad)
    mixed_one_grad = contract_cols(packed_grad, qkv_b)
    input_grad = norm_back(mixed_one_grad, normed_one, scale_one, vectors[0]) + hidden_grad
    vector_grad = jnp.stack(
        [
            jnp.sum(mixed_one_grad * normed_one, axis=0),
            jnp.sum(mixed_one_grad, axis=0),
            jnp.sum(query_grad, axis=0),
            jnp.sum(values_grad, axis=0),
            jnp.sum(hidden_grad, axis=0),
            jnp.sum(mixed_two_grad * normed_two, axis=0),
            jnp.sum(mixed_two_grad, axis=0),
            jnp.sum(cot_f, axis=0),
        ]
    )
    bias_grad = jnp.sum(pre_grad, axis=0)
    return (result, input_grad, (qkv_grad, proj_grad, up_grad, down_grad, vector_grad, bias_grad))


def newton_step(ortho, gram):
    poly = newton_b * gram + newton_c * jnp.dot(gram, gram, precision=lax.Precision.HIGHEST)
    return newton_a * ortho + jnp.dot(poly, ortho, precision=lax.Precision.HIGHEST)


def self_gram(ortho):
    return jnp.dot(ortho, ortho.T, precision=lax.Precision.HIGHEST)


def orthogonalize(moment):
    ortho = moment * lax.rsqrt(jnp.sum(moment * moment) + norm_eps)
    for turn in range(5):
        ortho = newton_step(ortho, self_gram(ortho))
    return ortho


def normalized_step(param, gradient):
    return param - vector_rate * gradient * lax.rsqrt(
        jnp.mean(gradient * gradient, axis=-1, keepdims=True) + norm_eps
    )


def owner_worker(columns, devices, widest):

    def worker(received):
        rows = received.shape[1]
        whole = jnp.transpose(received[:, :, :columns], (1, 0, 2)).reshape(rows, devices * columns)
        result = orthogonalize(whole).reshape(rows, devices, columns)
        result = jnp.transpose(result, (1, 0, 2))
        return jnp.pad(result, ((0, 0), (0, 0), (0, widest - columns)))

    return worker


def body(
    block_in,
    out_grad,
    live_counts,
    qkv_weight,
    proj_weight,
    up_weight,
    down_weight,
    feature_vectors,
    up_bias,
    qkv_moment,
    proj_moment,
    up_moment,
    down_moment,
):
    gathered = (
        lax.all_gather(qkv_weight.astype(jnp.bfloat16), "dp", axis=1, tiled=True),
        lax.all_gather(proj_weight.astype(jnp.bfloat16), "dp", axis=1, tiled=True),
        lax.all_gather(up_weight.astype(jnp.bfloat16), "dp", axis=1, tiled=True),
        lax.all_gather(down_weight.astype(jnp.bfloat16), "dp", axis=1, tiled=True),
    )
    width = block_in.shape[1]
    slots = block_in.shape[0] // SEQ
    blocks = slots // ATT_BLK
    block_rows = ATT_BLK * SEQ
    alive = (
        (jnp.arange(slots, dtype=jnp.int32) < live_counts[0])
        .astype(jnp.float32)
        .reshape(blocks, ATT_BLK)
    )
    inputs = block_in.reshape(blocks, ATT_BLK, SEQ, width)
    cotangents = out_grad.reshape(blocks, ATT_BLK, SEQ, width)
    initial = tuple((jnp.zeros(matrix.shape, jnp.float32) for matrix in gathered)) + (
        jnp.zeros(feature_vectors.shape, jnp.float32),
        jnp.zeros(up_bias.shape, jnp.float32),
    )

    def working(operands):
        return block_pass(
            operands[0],
            operands[1],
            operands[2],
            gathered[0],
            gathered[1],
            gathered[2],
            gathered[3],
            feature_vectors,
            up_bias,
        )

    def resting(operands):
        empty = jnp.zeros((block_rows, width), jnp.float32)
        return (empty, empty, initial)

    def visit(carry, piece):
        result, input_grad, grads = lax.cond(jnp.max(piece[2]) > 0.5, working, resting, piece)
        return (tuple((total + grad for total, grad in zip(carry, grads))), (result, input_grad))

    totals, (results, input_grads) = lax.scan(visit, initial, (inputs, cotangents, alive))
    shards = (
        lax.psum_scatter(totals[0], "dp", scatter_dimension=1, tiled=True),
        lax.psum_scatter(totals[1], "dp", scatter_dimension=1, tiled=True),
        lax.psum_scatter(totals[2], "dp", scatter_dimension=1, tiled=True),
        lax.psum_scatter(totals[3], "dp", scatter_dimension=1, tiled=True),
    )
    vector_grad, bias_grad = lax.psum((totals[4], totals[5]), "dp")
    matrices = (qkv_weight, proj_weight, up_weight, down_weight)
    moments = (qkv_moment, proj_moment, up_moment, down_moment)
    states = [momentum_decay * moments[index] + shards[index] for index in range(4)]
    devices = lax.axis_size("dp")
    stride = devices // 4
    local_cols = [states[index].shape[1] for index in range(4)]
    widest = max(local_cols)
    rows = states[0].shape[0]
    outgoing = jnp.zeros((devices, rows, widest), jnp.float32)
    for index in range(4):
        padded = jnp.pad(states[index], ((0, 0), (0, widest - local_cols[index])))
        outgoing = outgoing.at[index * stride].set(padded)
    incoming = lax.all_to_all(outgoing, "dp", split_axis=0, concat_axis=0, tiled=True)
    position = lax.axis_index("dp")
    owned = jnp.where(position % stride == 0, position // stride, 4)
    workers = [owner_worker(local_cols[index], devices, widest) for index in range(4)]
    workers.append(jnp.zeros_like)
    finished = lax.switch(owned, workers, incoming)
    returned = lax.all_to_all(finished, "dp", split_axis=0, concat_axis=0, tiled=True)
    orthos = [returned[index * stride][:, : local_cols[index]] for index in range(4)]
    updated = []
    for index in range(4):
        columns = matrices[index].shape[1] * devices
        updated.append(matrices[index] - matrix_rate * 0.2 * math.sqrt(columns) * orthos[index])
    return (
        results.reshape(block_in.shape),
        input_grads.reshape(block_in.shape),
        shards[0],
        shards[1],
        shards[2],
        shards[3],
        vector_grad,
        bias_grad,
        updated[0],
        updated[1],
        updated[2],
        updated[3],
        states[0],
        states[1],
        states[2],
        states[3],
        normalized_step(feature_vectors, vector_grad),
        normalized_step(up_bias, bias_grad),
    )


def solution(mesh):
    in_specs = (
        P("dp", None),
        P("dp", None),
        P("dp"),
        P(None, "dp"),
        P(None, "dp"),
        P(None, "dp"),
        P(None, "dp"),
        P(),
        P(),
        P(None, "dp"),
        P(None, "dp"),
        P(None, "dp"),
        P(None, "dp"),
    )
    out_specs = (
        P("dp", None),
        P("dp", None),
        P(None, "dp"),
        P(None, "dp"),
        P(None, "dp"),
        P(None, "dp"),
        P(),
        P(),
        P(None, "dp"),
        P(None, "dp"),
        P(None, "dp"),
        P(None, "dp"),
        P(None, "dp"),
        P(None, "dp"),
        P(None, "dp"),
        P(None, "dp"),
        P(),
        P(),
    )
    return jax.shard_map(body, mesh=mesh, in_specs=in_specs, out_specs=out_specs, check_vma=False)
```

profile of v0, /device:TPU:0, one launch (start us, length us, event | category | flops | bytes accessed | tf_op | source)
XLA Modules:
  0.0 1286.5 jit_solution(2561273813920063409)
XLA Ops:
  11.1 8.7 copy.144
  19.8 46.6 %all-gather = bf16[32,36,384]{2,1,0:T(8,128)(2,1)S(1)} all-gather(bf16[1,36,384]{2,1,0:T(8,128)(2,1)S(1)} %convert_bitcast_fusion), channel_id=1, replica_groups=mesh['dp'=32] {'dp'}, dimensions={0}, use_global_device_ids=true | all-gather | bytes 912384 | tf_op jit(solution)/shard_map/all_gather | solution.py:202
  68.1 38.0 %all-gather.1 = bf16[32,12,384]{2,1,0:T(8,128)(2,1)S(1)} all-gather(bf16[1,12,384]{2,1,0:T(8,128)(2,1)S(1)} %convert_bitcast_fusion.1), channel_id=1, replica_groups=mesh['dp'=32] {'dp'}, dimensions={0}, use_global_device_ids=true | all-gather | bytes 304128 | tf_op jit(solution)/shard_map/all_gather | solution.py:203
  107.0 8.8 copy.147
  118.8 6.9 all-gather.7.cloned.1.call-done
  128.2 486.1 %while.29 = (s32[]{:T(128)}, f32[384,1152]{1,0:T(8,128)}, f32[384,384]{1,0:T(8,128)}, f32[384,1536]{1,0:T(8,128)}, f32[384,1536]{1,0:T(8,128)}, /*index=5*/f32[8...) while((s32[]{:T(128)}, f32[384,1152]{1,0:T(8,128)}, ...), condition=%wide.region_24.25_spmd.clone, body=%wide.region_0.24_spmd.clone.sunk | while | flops 6088752640 | bytes 248980560 | solution.py:244
  146.0 67.5 %conditional.5 = (f32[384,1152]{1,0:T(8,128)}, f32[384,384]{1,0:T(8,128)}, f32[384,1536]{1,0:T(8,128)}, f32[384,1536]{1,0:T(8,128)}, f32[8,384]{1,0:T(8,128)}, /...) conditional(s32[]{:T(128)} %convert_element_type.186, () %tuple.125, ...), branch_computations={%region_2.2_spmd, %region_3.23_spmd} | conditional | flops 6085204480 | bytes 178784192 | solution.py:241
  218.5 4.0 select_add_fusion.13
  233.5 67.5 %conditional.5 = (f32[384,1152]{1,0:T(8,128)}, f32[384,384]{1,0:T(8,128)}, f32[384,1536]{1,0:T(8,128)}, f32[384,1536]{1,0:T(8,128)}, f32[8,384]{1,0:T(8,128)}, /...) conditional(s32[]{:T(128)} %convert_element_type.186, () %tuple.125, ...), branch_computations={%region_2.2_spmd, %region_3.23_spmd} | conditional | flops 6085204480 | bytes 178784192 | solution.py:241
  306.6 4.0 select_add_fusion.13
  321.6 67.5 %conditional.5 = (f32[384,1152]{1,0:T(8,128)}, f32[384,384]{1,0:T(8,128)}, f32[384,1536]{1,0:T(8,128)}, f32[384,1536]{1,0:T(8,128)}, f32[8,384]{1,0:T(8,128)}, /...) conditional(s32[]{:T(128)} %convert_element_type.186, () %tuple.125, ...), branch_computations={%region_2.2_spmd, %region_3.23_spmd} | conditional | flops 6085204480 | bytes 178784192 | solution.py:241
  394.7 4.0 select_add_fusion.13
  409.6 67.5 %conditional.5 = (f32[384,1152]{1,0:T(8,128)}, f32[384,384]{1,0:T(8,128)}, f32[384,1536]{1,0:T(8,128)}, f32[384,1536]{1,0:T(8,128)}, f32[8,384]{1,0:T(8,128)}, /...) conditional(s32[]{:T(128)} %convert_element_type.186, () %tuple.125, ...), branch_computations={%region_2.2_spmd, %region_3.23_spmd} | conditional | flops 6085204480 | bytes 178784192 | solution.py:241
  482.7 4.0 select_add_fusion.13
  497.7 8.9 conditional.5
  512.3 4.0 select_add_fusion.13
  527.2 8.9 conditional.5
  541.8 4.0 select_add_fusion.13
  556.8 8.9 conditional.5
  571.3 4.0 select_add_fusion.13
  586.3 8.9 conditional.5
  600.9 4.0 select_add_fusion.13
  624.5 309.3 %fusion.82 = (f32[384,48]{0,1:T(8,128)S(1)}, f32[384,16]{0,1:T(8,128)S(1)}) fusion(f32[384,1152]{0,1:T(8,128)} %copy.152, f32[384,384]{0,1:T(8,128)S(1)} %copy.153), kind=kCustom, calls=%all-reduce-scatter.2 | all-reduce-scatter fusion | flops 786434 | bytes 2457600
  940.3 8.3 collective-permute-start.5
  958.5 5.2 collective-permute-start.4
  979.9 78.7 %reduce-scatter.9.cloned.1.call-done = f32[384,48]{0,1:T(8,128)} async-done(((f32[384,1536]{0,1:T(8,128)}), f32[384,48]{0,1:T(8,128)}) %reduce-scatter.9.cloned.1.call-update) | async-done | bytes 73744 | tf_op jit(solution)/shard_map/reduce_scatter | solution.py:249
  1065.3 54.4 %all-to-all-done = f32[32,384,48]{1,2,0:T(8,128)S(1)} async-done(((f32[32,384,48]{1,2,0:T(8,128)}), f32[32,384,48]{1,2,0:T(8,128)S(1)}, u32[]{:S(2)}, u32[]{:S(2)}) %all-to-all-start) | async-done | bytes 2359328 | tf_op jit(solution)/shard_map/all_to_all | solution.py:264
  1119.6 73.0 %conditional.2 = (f32[32,384,48]{1,2,0:T(8,128)}) conditional(s32[]{:T(128)} %clamp.3, f32[32,384,48]{1,2,0:T(8,128)S(1)} %all-to-all-done, f32[32,384,48]{1,2,0:T(8,128)S(1)} %all-to-all-done, f32[32,384,48]{1,2,0:T(8,128)S(1)} %all-to-all-done, f32[32,384,48]{1,2,0:T(8,128)S(1)} %all-to-all-done, () %tuple.60), branch_computations={%region_31.33_spmd, %region_33.35_spmd, %region_35.37_spmd, %regio... | conditional | flops 30586355712 | bytes 84934744 | solution.py:269
  1130.0 4.4 convolution_add_fusion.4
  1154.6 3.6 convolution_add_fusion.1
  1192.7 6.5 all-to-all-start.1
  1199.3 75.1 %all-reduce.9 = (f32[8,384]{1,0:T(8,128)S(1)}, f32[1536]{0:T(1024)S(1)}) all-reduce(f32[8,384]{1,0:T(8,128)S(1)} %copy-done.61, f32[1536]{0:T(1024)S(1)} %copy-done.66), channel_id=1, replica_groups=mesh['dp'=32] {'dp'}, use_global_device_ids=true, to_apply=%region_29.30 | all-reduce | flops 4608 | bytes 36864 | tf_op jit(solution)/shard_map/psum | solution.py:251
  (1189 shorter events, 535.8 us)
Async XLA Ops:
  7.2 109.2 %all-gather.5.cloned.1.call-start = ((), (), s32[]{:S(2)}) async-start(), calls=%async_computation.4 | async-start | bytes 1216512 | tf_op jit(solution)/shard_map/all_gather | solution.py:205
  8.8 117.0 %all-gather.7.cloned.1.call-start = ((), (), s32[]{:S(2)}) async-start(), calls=%async_computation.5 | async-start | bytes 1216512 | tf_op jit(solution)/shard_map/all_gather | solution.py:204
  10.3 968.0 %reduce-scatter.7.cloned.1.call-start = ((), (), s32[]{:S(2)}) async-start(), calls=%async_computation.6 | async-start | bytes 2433024 | tf_op jit(solution)/shard_map/reduce_scatter | solution.py:248
  19.8 48.3 %copy-start.80 = (f32[384,12]{0,1:T(8,128)S(1)}, f32[384,12]{0,1:T(8,128)}, u32[]{:S(2)}) copy-start(f32[384,12]{0,1:T(8,128)} %param.34) | copy-start | bytes 55300
  617.4 441.3 %reduce-scatter.9.cloned.1.call-start = ((), (), s32[]{:S(2)}) async-start(), calls=%async_computation.7 | async-start | bytes 2433024 | tf_op jit(solution)/shard_map/reduce_scatter | solution.py:249
  624.2 350.5 %copy-start.92 = (f32[384,12]{0,1:T(8,128)S(1)}, f32[384,12]{0,1:T(8,128)}, u32[]{:S(2)}) copy-start(f32[384,12]{0,1:T(8,128)} %param.40) | copy-start | bytes 55300
  624.5 352.5 %copy-start.85 = (f32[384,36]{0,1:T(8,128)S(1)}, f32[384,36]{0,1:T(8,128)}, u32[]{:S(2)}) copy-start(f32[384,36]{0,1:T(8,128)} %param.39) | copy-start | bytes 165892
  933.8 6.5 collective-permute-start.15
  935.1 13.5 %collective-permute-start.14 = (f32[384,16]{0,1:T(8,128)S(1)}, f32[384,16]{0,1:T(8,128)S(1)}, u32[]{:S(2)}, u32[]{:S(2)}) collective-permute-start(f32[384,16]{0,1:T(8,128)S(1)} %get-tuple-element.431), channel_id=1, source_target_pairs={{0,7},{1,8},{2,9},{3,10},{4,11},{5,12},{6,13},{7,14},{8,15},{9,16}... | collective-permute-start | bytes 73736
  936.4 13.5 %collective-permute-start.13 = (f32[384,16]{0,1:T(8,128)S(1)}, f32[384,16]{0,1:T(8,128)S(1)}, u32[]{:S(2)}, u32[]{:S(2)}) collective-permute-start(f32[384,16]{0,1:T(8,128)S(1)} %get-tuple-element.431), channel_id=1, source_target_pairs={{0,6},{1,7},{2,8},{3,9},{4,10},{5,11},{6,12},{7,13},{8,14},{9,15},... | collective-permute-start | bytes 73736
  937.7 14.2 %collective-permute-start.12 = (f32[384,16]{0,1:T(8,128)S(1)}, f32[384,16]{0,1:T(8,128)S(1)}, u32[]{:S(2)}, u32[]{:S(2)}) collective-permute-start(f32[384,16]{0,1:T(8,128)S(1)} %get-tuple-element.431), channel_id=1, source_target_pairs={{0,5},{1,6},{2,7},{3,8},{4,9},{5,10},{6,11},{7,12},{8,13},{9,14},{... | collective-permute-start | bytes 73736
  939.0 31.1 %collective-permute-start.6 = (f32[384,48]{0,1:T(8,128)S(1)}, f32[384,48]{0,1:T(8,128)S(1)}, u32[]{:S(2)}, u32[]{:S(2)}) collective-permute-start(f32[384,48]{0,1:T(8,128)S(1)} %get-tuple-element.430), channel_id=1, source_target_pairs={{0,7},{1,8},{2,9},{3,10},{4,11},{5,12},{6,13},{7,14},{8,15},{9,16}... | collective-permute-start | bytes 221192
  940.3 32.4 %collective-permute-start.5 = (f32[384,48]{0,1:T(8,128)S(1)}, f32[384,48]{0,1:T(8,128)S(1)}, u32[]{:S(2)}, u32[]{:S(2)}) collective-permute-start(f32[384,48]{0,1:T(8,128)S(1)} %get-tuple-element.430), channel_id=1, source_target_pairs={{0,6},{1,7},{2,8},{3,9},{4,10},{5,11},{6,12},{7,13},{8,14},{9,15},... | collective-permute-start | bytes 221192
  948.7 18.5 %collective-permute-start.7 = (f32[384,36]{0,1:T(8,128)S(1)}, f32[384,36]{0,1:T(8,128)S(1)}, u32[]{:S(2)}, u32[]{:S(2)}) collective-permute-start(f32[384,36]{0,1:T(8,128)S(1)} %slice.176), channel_id=1, source_target_pairs={{0,8},{1,9},{2,10},{3,11},{4,12},{5,13},{6,14},{7,15},{8,16},{9,17... | collective-permute-start | bytes 165896
  950.0 3.9 collective-permute-start.11
  951.9 4.8 collective-permute-start.10
  953.8 4.6 collective-permute-start.9
  956.7 7.0 collective-permute-start.8
  958.5 16.9 %collective-permute-start.4 = (f32[384,48]{0,1:T(8,128)S(1)}, f32[384,48]{0,1:T(8,128)S(1)}, u32[]{:S(2)}, u32[]{:S(2)}) collective-permute-start(f32[384,48]{0,1:T(8,128)S(1)} %get-tuple-element.430), channel_id=1, source_target_pairs={{0,5},{1,6},{2,7},{3,8},{4,9},{5,10},{6,11},{7,12},{8,13},{9,14},{... | collective-permute-start | bytes 221192
  963.7 11.7 collective-permute-start.3
  967.2 91.5 %copy-start.84 = (f32[384,48]{0,1:T(8,128)S(1)}, f32[384,48]{0,1:T(8,128)}, u32[]{:S(2)}) copy-start(f32[384,48]{0,1:T(8,128)} %param.42) | copy-start | bytes 221188
  967.2 8.2 collective-permute-start.2
  970.1 5.3 collective-permute-start.1
  972.7 2.9 collective-permute-start
  975.4 84.8 %copy-start.82 = (f32[384,12]{0,1:T(8,128)}, f32[384,12]{0,1:T(8,128)S(1)}, u32[]{:S(2)}) copy-start(f32[384,12]{0,1:T(8,128)S(1)} %get-tuple-element.442) | copy-start | bytes 55300
  1061.6 58.0 %all-to-all-start = ((f32[32,384,48]{1,2,0:T(8,128)}), f32[32,384,48]{1,2,0:T(8,128)S(1)}, u32[]{:S(2)}, u32[]{:S(2)}) async-start(f32[32,384,48]{1,2,0:T(8,128)} %copy-done.35), calls=%async_computation.2 | async-start | bytes 4718592 | tf_op jit(solution)/shard_map/all_to_all | solution.py:264
  1192.7 83.1 %copy-start.94 = (f32[1536]{0:T(1024)S(1)}, f32[1536]{0:T(1024)}, u32[]{:S(2)}) copy-start(f32[1536]{0:T(1024)} %get-tuple-element.748) | copy-start | bytes 18436
  1192.7 85.1 %copy-start.70 = (f32[384,36]{0,1:T(8,128)S(1)}, f32[384,36]{0,1:T(8,128)}, u32[]{:S(2)}) copy-start(f32[384,36]{0,1:T(8,128)} %param.33) | copy-start | bytes 165892
  1192.7 85.8 %copy-start.81 = (f32[384,12]{0,1:T(8,128)S(1)}, f32[384,12]{0,1:T(8,128)}, u32[]{:S(2)}) copy-start(f32[384,12]{0,1:T(8,128)} %param.34) | copy-start | bytes 55300
  1192.7 86.4 %copy-start.67 = (f32[384,48]{0,1:T(8,128)S(1)}, f32[384,48]{0,1:T(8,128)}, u32[]{:S(2)}) copy-start(f32[384,48]{0,1:T(8,128)} %param.36) | copy-start | bytes 221188
  1192.7 86.4 %copy-start.68 = (f32[384,48]{0,1:T(8,128)S(1)}, f32[384,48]{0,1:T(8,128)}, u32[]{:S(2)}) copy-start(f32[384,48]{0,1:T(8,128)} %param.35) | copy-start | bytes 221188
  1192.7 85.1 %all-to-all-start.1 = ((f32[32,384,48]{1,2,0:T(8,128)}), f32[32,384,48]{1,2,0:T(8,128)S(1)}, u32[]{:S(2)}, u32[]{:S(2)}) async-start(f32[32,384,48]{1,2,0:T(8,128)} %get-tuple-element.695), calls=%async_computation.3 | async-start | bytes 4718592 | tf_op jit(solution)/shard_map/all_to_all | solution.py:270
  (328 other events, 1174.2 us)
Sparse Core Ops, SparseCore 0:
  11.5 57.7 all-gather.4
  72.8 52.9 all-gather.6
  617.5 336.6 reduce-scatter.6
  959.9 98.6 reduce-scatter.8
where the time goes:
time: 1290 us
  blocking collectives  469 us (36%)
  local copies, waits for them, and re-layouts  218 us (17%)
  matrix products  175 us (14%)
  other arithmetic  170 us (13%)
  waiting for transfers between devices  140 us (11%)
  starting transfers between devices  49.9 us (4%)
  loops' own time  48.1 us (4%)
  between operations  16 us (1%)
    unnamed x1, blocking collectives  309 us
    add x40, other arithmetic, visit(): total + grad  81.6 us
    reduce_scatter x1, waiting for transfers between devices, body(): lax.psum_scatter(totals[3], 'dp', scatter_dimension=1, tiled=True)  78.7 us
    psum x1, blocking collectives, body(): vector_grad, bias_grad = lax.psum((totals[4], totals[5]), 'dp')  75.1 us
    all_to_all x1, waiting for transfers between devices, body(): lax.all_to_all(outgoing, 'dp', split_axis=0, concat_axis=0, tiled=True)  54.4 us
    dynamic_update_slice x24, local copies, waits for them, and re-layouts, body(): lax.scan(visit, initial, (inputs, cotangents, alive))  48.6 us
    all_gather x1, blocking collectives, body(): lax.all_gather(qkv_weight.astype(jnp.bfloat16), 'dp', axis=1, tiled=True)  46.6 us
    dot_general x16, matrix products, contract_cols(): lax.dot_general(left, right, (((1,), (1,)), ((), ())), preferred_element_...  41 us
  transfers between devices with their start and end apart: 22, of which 4 were waited for; matrix products, arithmetic and copies ran while one was open for 27% of the time, Pallas kernels for 0%

commit v1 on v0

v1 whole, which is shorter than its diff:
```python
import functools
import math

import jax
import jax.numpy as jnp
from jax import lax
from jax.experimental import pallas as pl
from jax.experimental.pallas import tpu as pltpu
from jax.sharding import PartitionSpec as P

HEAD_DIM = 64
SEQ = 256
GROUP = 2
LANES = 128

norm_eps = 1e-06
newton_a = 3.4445
newton_b = -4.775
newton_c = 2.0315
momentum_decay = 0.9
matrix_rate = 0.15
vector_rate = 0.2

f32 = jnp.float32
bf16 = jnp.bfloat16


def nn(a, b):
    return lax.dot_general(a, b, (((1,), (0,)), ((), ())), preferred_element_type=f32)


def nt(a, b):
    return lax.dot_general(a, b, (((1,), (1,)), ((), ())), preferred_element_type=f32)


def tn(a, b):
    return lax.dot_general(a, b, (((0,), (0,)), ((), ())), preferred_element_type=f32)


def cols(index):
    return slice(index * LANES, (index + 1) * LANES)


def norm_parts(chunk):
    width = chunk.shape[0]
    center = chunk - jnp.sum(chunk, axis=0, keepdims=True) * (1.0 / width)
    scale = lax.rsqrt(jnp.sum(center * center, axis=0, keepdims=True) * (1.0 / width) + norm_eps)
    return center * scale, scale


def norm_back(inner, normed, scale):
    width = inner.shape[0]
    mean = jnp.sum(inner, axis=0, keepdims=True) * (1.0 / width)
    cross = jnp.sum(inner * normed, axis=0, keepdims=True) * (1.0 / width)
    return scale * (inner - mean - normed * cross)


def normal_parts(u):
    size = jnp.abs(u)
    density = jnp.exp(u * u * (-0.5))
    t = 1.0 / (1.0 + (0.3275911 / math.sqrt(2.0)) * size)
    poly = t * (
        0.5 * 0.254829592
        + t
        * (
            0.5 * -0.284496736
            + t * (0.5 * 1.421413741 + t * (0.5 * -1.453152027 + t * (0.5 * 1.061405429)))
        )
    )
    tail = poly * density
    return jnp.where(u >= 0.0, 1.0 - tail, tail), density * (1.0 / math.sqrt(2.0 * math.pi))


def split3(x):
    high = x.astype(bf16)
    return high, (x - high.astype(f32)).astype(bf16)


def mul3(a, b):
    ah, al = split3(a)
    bh, bl = split3(b)
    return nn(ah, bh) + (nn(ah, bl) + nn(al, bh))


def assemble(par, own_ref, other_ref, first, count, stage):
    for shard in range(2 * own_ref.shape[0]):
        mine = own_ref[shard // 2, first : first + count, :].astype(f32)
        theirs = other_ref[shard // 2, first : first + count, :].astype(f32)
        stage[shard * count : (shard + 1) * count, :] = jnp.where(par == shard % 2, mine, theirs)


def emit(par, pieces, vector, keep_ref, send_ref, stage):
    count = 2 * keep_ref.shape[0]
    sizes = [piece.shape[0] // count for piece in pieces]
    rows = sum(sizes)
    width = pieces[0].shape[1]
    stage[...] = jnp.zeros_like(stage)
    base = rows * (width // LANES)
    for index, row in enumerate(vector):
        stage[base + index : base + index + 1, :] = row.astype(bf16).astype(f32)
    for shard in range(count):
        for c in range(width // LANES):
            low = c * rows
            for piece, size in zip(pieces, sizes):
                stage[low : low + size, :] = piece[shard * size : (shard + 1) * size, cols(c)]
                low += size

        @pl.when(par == shard % 2)
        def _():
            keep_ref[shard // 2] = stage[...]

        @pl.when(par != shard % 2)
        def _():
            send_ref[shard // 2] = stage[...].astype(bf16)


def lane_rows(acc):
    out = []
    for c in range(acc.shape[0] // LANES):
        out.append(jnp.sum(acc[cols(c), :].T, axis=0, keepdims=True))
    return out


def prep_kernel(wq_ref, wp_ref, wu_ref, wd_ref, first_ref, second_ref):
    first = wq_ref[...].T.astype(bf16)
    second = jnp.concatenate([wu_ref[...].T, wd_ref[...].T, wp_ref[...].T], axis=0).astype(bf16)
    for index in range(first_ref.shape[0]):
        first_ref[index] = first
        second_ref[index] = second


def attend_kernel(
    info, x_ref, own_ref, other_ref, vec_ref, qkv_ref, att_ref, out_ref, wq_ref, z_scr, stage
):
    width, lanes = z_scr.shape
    heads = width // HEAD_DIM

    @pl.when(pl.program_id(0) == 0)
    def _():
        assemble(info[1], own_ref, other_ref, 0, own_ref.shape[1], stage)
        wq_ref[...] = stage[...].astype(bf16)

    @pl.when(pl.program_id(0) * GROUP < info[0])
    def _():
        for c in range(lanes // LANES):
            chunk = x_ref[cols(c), :].astype(f32).T
            normed, _ = norm_parts(chunk)
            z_scr[:, cols(c)] = (normed * vec_ref[0] + vec_ref[1]).astype(bf16)
        for part in range(3):
            rows = slice(part * width, (part + 1) * width)
            made = nn(wq_ref[rows, :], z_scr[...])
            for c in range(lanes // LANES):
                piece = made[:, cols(c)]
                if part == 0:
                    piece = (piece + vec_ref[2]) * (1.0 / math.sqrt(HEAD_DIM))
                elif part == 2:
                    piece = piece + vec_ref[3]
                qkv_ref[rows, cols(c)] = piece.astype(bf16)
        for image in range(lanes // SEQ):
            span = slice(image * SEQ, (image + 1) * SEQ)
            for head in range(heads):
                low = head * HEAD_DIM
                query = qkv_ref[low : low + HEAD_DIM, span]
                keys = qkv_ref[width + low : width + low + HEAD_DIM, span]
                values = qkv_ref[2 * width + low : 2 * width + low + HEAD_DIM, span]
                scores = tn(keys, query)
                top = jnp.max(scores, axis=0, keepdims=True)
                raised = jnp.exp(scores - top)
                total = jnp.sum(raised, axis=0, keepdims=True)
                attend = (raised * (1.0 / total)).astype(bf16)
                base = (image * heads + head) * SEQ
                att_ref[base : base + SEQ, :] = attend
                out_ref[low : low + HEAD_DIM, span] = nn(values, attend).astype(bf16)


def mlp_kernel(
    info, x_ref, cot_ref, att_ref, own_ref, other_ref, vec_ref, ub_ref,
    out_ref, dh_ref, gp_ref, wpn_ref, keep_ref, send_ref,
    wun_scr, wdn_scr, wp_scr, wu_scr, wd_scr, gu_scr, gd_scr, rows_scr, bias_scr,
    h_scr, n_scr, z_scr, m_scr, act_scr, du_scr, dhb_scr, s_scr, stage, wide,
):
    width, lanes = z_scr.shape
    ff = wu_scr.shape[0]
    devices = 2 * own_ref.shape[0]
    step = pl.program_id(0)
    block = 256

    @pl.when(step == 0)
    def _():
        gp_ref[...] = jnp.zeros_like(gp_ref)
        gu_scr[...] = jnp.zeros_like(gu_scr)
        gd_scr[...] = jnp.zeros_like(gd_scr)
        rows_scr[...] = jnp.zeros_like(rows_scr)
        bias_scr[...] = jnp.zeros_like(bias_scr)
        part = ff // devices
        assemble(info[1], own_ref, other_ref, 2 * part, width // devices, wide.at[:width])
        wp_scr[...] = wide[:width, :].astype(bf16)
        wpn_ref[...] = wide[:width, :].T.astype(bf16)
        assemble(info[1], own_ref, other_ref, 0, part, wide)
        wu_scr[...] = wide[...].astype(bf16)
        for c in range(ff // block):
            rows = slice(c * block, (c + 1) * block)
            wun_scr[:, rows] = wide[rows, :].T.astype(bf16)
        assemble(info[1], own_ref, other_ref, part, part, wide)
        wd_scr[...] = wide[...].astype(bf16)
        for c in range(ff // block):
            rows = slice(c * block, (c + 1) * block)
            wdn_scr[:, rows] = wide[rows, :].T.astype(bf16)

    @pl.when(step * GROUP >= info[0])
    def _():
        out_ref[...] = jnp.zeros_like(out_ref)

    @pl.when(step * GROUP < info[0])
    def _():
        made = nn(wp_scr[...], att_ref[...])
        total7 = jnp.zeros((width, LANES), f32)
        for c in range(lanes // LANES):
            chunk = x_ref[cols(c), :].astype(f32).T + made[:, cols(c)] + vec_ref[4]
            h_scr[:, cols(c)] = chunk
            normed, scale = norm_parts(chunk)
            n_scr[:, cols(c)] = normed
            s_scr[:, cols(c)] = scale
            z_scr[:, cols(c)] = (normed * vec_ref[5] + vec_ref[6]).astype(bf16)
            image = step * GROUP + c * LANES // SEQ
            cot = jnp.where(image < info[0], cot_ref[cols(c), :].astype(f32), 0.0).T
            m_scr[:, cols(c)] = cot.astype(bf16)
            total7 += cot
        rows_scr[3] += total7
        for c in range(ff // block):
            rows = slice(c * block, (c + 1) * block)
            u_all = nn(wu_scr[rows, :], z_scr[...])
            d_all = nn(wd_scr[rows, :], m_scr[...])
            bias = jnp.zeros((block, LANES), f32)
            for k in range(lanes // LANES):
                u = u_all[:, cols(k)] + ub_ref[rows, :]
                cdf, density = normal_parts(u)
                act_scr[rows, cols(k)] = (u * cdf).astype(bf16)
                du = d_all[:, cols(k)] * (cdf + u * density)
                du_scr[rows, cols(k)] = du.astype(bf16)
                bias += du
            bias_scr[rows, :] += bias
            gu_scr[rows, :] += nt(du_scr[rows, :], z_scr[...])
            gd_scr[rows, :] += nt(act_scr[rows, :], m_scr[...])
        down = nn(wdn_scr[...], act_scr[...])
        for c in range(lanes // LANES):
            image = step * GROUP + c * LANES // SEQ
            whole = down[:, cols(c)] + h_scr[:, cols(c)] + vec_ref[7]
            out_ref[cols(c), :] = jnp.where(image < info[0], whole, 0.0).T
        dz = nn(wun_scr[...], du_scr[...])
        total4 = jnp.zeros((width, LANES), f32)
        total5 = jnp.zeros((width, LANES), f32)
        total6 = jnp.zeros((width, LANES), f32)
        for c in range(lanes // LANES):
            piece = dz[:, cols(c)]
            normed = n_scr[:, cols(c)]
            dh = norm_back(piece * vec_ref[5], normed, s_scr[:, cols(c)]) + m_scr[:, cols(c)].astype(f32)
            dh_ref[:, cols(c)] = dh
            dhb_scr[:, cols(c)] = dh.astype(bf16)
            total4 += dh
            total5 += piece * normed
            total6 += piece
        rows_scr[0] += total4
        rows_scr[1] += total5
        rows_scr[2] += total6
        gp_ref[...] += nt(dhb_scr[...], att_ref[...])

    @pl.when(step == pl.num_programs(0) - 1)
    def _():
        vector = []
        for index in range(4):
            vector += lane_rows(rows_scr[index])
        vector += lane_rows(bias_scr)
        emit(info[1], (gu_scr, gd_scr), vector, keep_ref, send_ref, stage)


def back_kernel(
    info, x_ref, qkv_ref, att_ref, dh_ref, wpn_ref, wq_ref, gp_ref, vec_ref,
    out_ref, keep_ref, send_ref,
    wqn_scr, n_scr, z_scr, s_scr, da_scr, dqkv_scr, gq_scr, rows_scr, stage,
):
    width, lanes = z_scr.shape
    heads = width // HEAD_DIM
    step = pl.program_id(0)

    @pl.when(step == 0)
    def _():
        gq_scr[...] = jnp.zeros_like(gq_scr)
        rows_scr[...] = jnp.zeros_like(rows_scr)
        for c in range(3):
            rows = slice(c * width, (c + 1) * width)
            wqn_scr[:, rows] = wq_ref[rows, :].T

    @pl.when(step * GROUP >= info[0])
    def _():
        out_ref[...] = jnp.zeros_like(out_ref)

    @pl.when(step * GROUP < info[0])
    def _():
        da_scr[...] = nn(wpn_ref[...], dh_ref[...].astype(bf16)).astype(bf16)
        for c in range(lanes // LANES):
            chunk = x_ref[cols(c), :].astype(f32).T
            normed, scale = norm_parts(chunk)
            n_scr[:, cols(c)] = normed
            s_scr[:, cols(c)] = scale
            z_scr[:, cols(c)] = (normed * vec_ref[0] + vec_ref[1]).astype(bf16)
        for image in range(lanes // SEQ):
            span = slice(image * SEQ, (image + 1) * SEQ)
            for head in range(heads):
                low = head * HEAD_DIM
                high = low + HEAD_DIM
                query = qkv_ref[low:high, span]
                keys = qkv_ref[width + low : width + high, span]
                values = qkv_ref[2 * width + low : 2 * width + high, span]
                grad = da_scr[low:high, span]
                base = (image * heads + head) * SEQ
                attend = att_ref[base : base + SEQ, :]
                attend_f = attend.astype(f32)
                upstream = tn(values, grad)
                delta = jnp.sum(attend_f * upstream, axis=0, keepdims=True)
                dscore = (attend_f * (upstream - delta)).astype(bf16)
                dquery = nn(keys, dscore) * (1.0 / math.sqrt(HEAD_DIM))
                dkey = nt(query, dscore)
                dvalue = nt(grad, attend)
                dqkv_scr[low:high, span] = dquery.astype(bf16)
                dqkv_scr[width + low : width + high, span] = dkey.astype(bf16)
                dqkv_scr[2 * width + low : 2 * width + high, span] = dvalue.astype(bf16)
                rows_scr[2, low:high, :] += dquery[:, :LANES] + dquery[:, LANES:]
                rows_scr[3, low:high, :] += dvalue[:, :LANES] + dvalue[:, LANES:]
        for part in range(3):
            rows = slice(part * width, (part + 1) * width)
            gq_scr[rows, :] += nt(dqkv_scr[rows, :], z_scr[...])
        dz = nn(wqn_scr[...], dqkv_scr[...])
        total0 = jnp.zeros((width, LANES), f32)
        total1 = jnp.zeros((width, LANES), f32)
        for c in range(lanes // LANES):
            piece = dz[:, cols(c)]
            normed = n_scr[:, cols(c)]
            dx = norm_back(piece * vec_ref[0], normed, s_scr[:, cols(c)]) + dh_ref[:, cols(c)]
            out_ref[cols(c), :] = dx.T
            total0 += piece * normed
            total1 += piece
        rows_scr[0] += total0
        rows_scr[1] += total1

    @pl.when(step == pl.num_programs(0) - 1)
    def _():
        vector = []
        for index in range(4):
            vector += lane_rows(rows_scr[index])
        emit(info[1], (gq_scr, gp_ref), vector, keep_ref, send_ref, stage)


def state_kernel(got_ref, ma_ref, mb_ref, ga_ref, gb_ref, sa_ref, sb_ref, spread_ref, state_ref, vec_ref):
    width, first = ma_ref.shape
    second = mb_ref.shape[1]
    rows = first + second
    total = got_ref[0].astype(f32)
    for index in range(1, got_ref.shape[0]):
        total += got_ref[index].astype(f32)
    blocks = width // LANES
    grad = jnp.concatenate([total[c * rows : (c + 1) * rows] for c in range(blocks)], axis=1)
    vec_ref[...] = total[blocks * rows : blocks * rows + vec_ref.shape[0]]
    natural = grad.T
    ga_ref[...] = natural[:, :first]
    gb_ref[...] = natural[:, first:]
    state_a = momentum_decay * ma_ref[...] + natural[:, :first]
    state_b = momentum_decay * mb_ref[...] + natural[:, first:]
    sa_ref[...] = state_a
    sb_ref[...] = state_b
    state = jnp.concatenate([state_a, state_b], axis=1).T
    state_ref[...] = state
    for index in range(spread_ref.shape[0]):
        spread_ref[index] = state.astype(bf16)


def newton_kernel(columns, own_ref, other_ref, state_ref, wa_ref, wb_ref, ua_ref, ub_ref):
    count, rows, width = own_ref.shape
    first = wa_ref.shape[1]
    spans = ((0, first), (first, rows))
    grams = []
    for low, high in spans:
        gram = jnp.zeros((width, width), f32)
        for ref in (own_ref, other_ref):
            part = jnp.concatenate(
                [ref[index, low:high, :].astype(f32) for index in range(count)], axis=0
            ).astype(bf16)
            gram += tn(part, part)
        grams.append(gram)
    eye = (
        lax.broadcasted_iota(jnp.int32, (width, width), 0)
        == lax.broadcasted_iota(jnp.int32, (width, width), 1)
    ).astype(f32)
    for gram, (low, high), w_ref, u_ref, wide in zip(
        grams, spans, (wa_ref, wb_ref), (ua_ref, ub_ref), columns
    ):
        norm = lax.rsqrt(jnp.sum(gram * eye) + norm_eps)
        gram = gram * (norm * norm)
        whole = None
        for turn in range(5):
            poly = newton_a * eye + newton_b * gram + newton_c * mul3(gram, gram)
            whole = poly if whole is None else mul3(poly, whole)
            if turn < 4:
                gram = mul3(mul3(poly, gram), poly)
        sh, sl = split3(state_ref[low:high, :] * norm)
        ph, pl_ = split3(whole)
        ortho = nt(ph, sh) + (nt(ph, sl) + nt(pl_, sh))
        u_ref[...] = w_ref[...] - (matrix_rate * 0.2 * math.sqrt(wide)) * ortho


def fixed(shape):
    return pl.BlockSpec(shape, lambda i, info: (0,) * len(shape))


def params(grid=True):
    return pltpu.CompilerParams(
        dimension_semantics=("arbitrary",) if grid else None, vmem_limit_bytes=60 * 1024 * 1024
    )


def shape_of(shape, dtype):
    return jax.ShapeDtypeStruct(shape, dtype)


def small_call(kernel, outs, name):
    return pl.pallas_call(
        kernel,
        out_shape=[shape_of(*out) for out in outs],
        compiler_params=params(False),
        name=name,
    )


def padded(rows):
    return -(-rows // 16) * 16


def body(
    block_in,
    out_grad,
    live_counts,
    qkv_weight,
    proj_weight,
    up_weight,
    down_weight,
    feature_vectors,
    up_bias,
    qkv_moment,
    proj_moment,
    up_moment,
    down_moment,
):
    devices = lax.axis_size("dp")
    half = devices // 2
    par = lax.axis_index("dp") % 2
    width = block_in.shape[1]
    heads = width // HEAD_DIM
    slots = block_in.shape[0] // SEQ
    groups = slots // GROUP
    lanes = GROUP * SEQ
    cq, cp, cu, cd = (w.shape[1] for w in (qkv_weight, proj_weight, up_weight, down_weight))
    ff = cu * devices
    blocks = width // LANES
    pairs = [(i, i ^ 1) for i in range(devices)]
    planes = [[2 * i + c for i in range(half)] for c in range(2)]
    info = jnp.stack([live_counts[0], par.astype(jnp.int32)])
    vec = jnp.broadcast_to(feature_vectors[:, :, None], feature_vectors.shape + (LANES,))
    ub = jnp.broadcast_to(up_bias[:, None], up_bias.shape + (LANES,))

    def exchange(x):
        return lax.all_to_all(x, "dp", 0, 0, axis_index_groups=planes, tiled=True)

    def swap(x):
        return lax.ppermute(x, "dp", pairs)

    first, second = small_call(
        prep_kernel,
        [((half, cq, width), bf16), ((half, cu + cd + cp, width), bf16)],
        "prep",
    )(qkv_weight, proj_weight, up_weight, down_weight)
    wq_own = exchange(first)
    wq_other = swap(wq_own)
    second, wq_own = lax.optimization_barrier((second, wq_own))
    rest_own = exchange(second)
    rest_other = swap(rest_own)

    tokens = lambda i, info: (i, 0)
    deep = lambda i, info: (i, 0, 0)
    token_spec = pl.BlockSpec((lanes, width), tokens)
    deep_spec = pl.BlockSpec((None, width, lanes), deep)
    qkv_spec = pl.BlockSpec((None, 3 * width, lanes), deep)
    att_spec = pl.BlockSpec((None, GROUP * heads * SEQ, SEQ), deep)

    qkv, att, attn, wq = pl.pallas_call(
        attend_kernel,
        grid_spec=pltpu.PrefetchScalarGridSpec(
            num_scalar_prefetch=1,
            grid=(groups,),
            in_specs=[token_spec, fixed(wq_own.shape), fixed(wq_own.shape), fixed(vec.shape)],
            out_specs=[qkv_spec, att_spec, deep_spec, fixed((3 * width, width))],
            scratch_shapes=[pltpu.VMEM((width, lanes), bf16), pltpu.VMEM((3 * width, width), f32)],
        ),
        out_shape=[
            shape_of((groups, 3 * width, lanes), bf16),
            shape_of((groups, GROUP * heads * SEQ, SEQ), bf16),
            shape_of((groups, width, lanes), bf16),
            shape_of((3 * width, width), bf16),
        ],
        compiler_params=params(),
        cost_estimate=pl.CostEstimate(flops=40_000_000_000, bytes_accessed=30_000_000, transcendentals=0),
        name="attend",
    )(info, block_in, wq_own, wq_other, vec)

    rows_b = padded(blocks * (cu + cd) + 4 * blocks + ff // LANES)
    out, dh, gp, wpn, keep_b, send_b = pl.pallas_call(
        mlp_kernel,
        grid_spec=pltpu.PrefetchScalarGridSpec(
            num_scalar_prefetch=1,
            grid=(groups,),
            in_specs=[
                token_spec, token_spec, deep_spec,
                fixed(rest_own.shape), fixed(rest_own.shape), fixed(vec.shape), fixed(ub.shape),
            ],
            out_specs=[
                token_spec, deep_spec, fixed((width, width)), fixed((width, width)),
                fixed((half, rows_b, LANES)), fixed((half, rows_b, LANES)),
            ],
            scratch_shapes=[
                pltpu.VMEM((width, ff), bf16),
                pltpu.VMEM((width, ff), bf16),
                pltpu.VMEM((width, width), bf16),
                pltpu.VMEM((ff, width), bf16),
                pltpu.VMEM((ff, width), bf16),
                pltpu.VMEM((ff, width), f32),
                pltpu.VMEM((ff, width), f32),
                pltpu.VMEM((4, width, LANES), f32),
                pltpu.VMEM((ff, LANES), f32),
                pltpu.VMEM((width, lanes), f32),
                pltpu.VMEM((width, lanes), f32),
                pltpu.VMEM((width, lanes), bf16),
                pltpu.VMEM((width, lanes), bf16),
                pltpu.VMEM((ff, lanes), bf16),
                pltpu.VMEM((ff, lanes), bf16),
                pltpu.VMEM((width, lanes), bf16),
                pltpu.VMEM((1, lanes), f32),
                pltpu.VMEM((rows_b, LANES), f32),
                pltpu.VMEM((ff, width), f32),
            ],
        ),
        out_shape=[
            shape_of(block_in.shape, f32),
            shape_of((groups, width, lanes), f32),
            shape_of((width, width), f32),
            shape_of((width, width), bf16),
            shape_of((half, rows_b, LANES), f32),
            shape_of((half, rows_b, LANES), bf16),
        ],
        compiler_params=params(),
        cost_estimate=pl.CostEstimate(flops=80_000_000_000, bytes_accessed=30_000_000, transcendentals=0),
        name="mlp",
    )(info, block_in, out_grad, attn, rest_own, rest_other, vec, ub)

    def gather_sums(keep, send):
        return exchange((keep + swap(send).astype(f32)).astype(bf16))

    got_b = gather_sums(keep_b, send_b)

    rows_a = padded(blocks * (cq + cp) + 4 * blocks)
    dx, keep_a, send_a = pl.pallas_call(
        back_kernel,
        grid_spec=pltpu.PrefetchScalarGridSpec(
            num_scalar_prefetch=1,
            grid=(groups,),
            in_specs=[
                token_spec, qkv_spec, att_spec, deep_spec,
                fixed(wpn.shape), fixed(wq.shape), fixed(gp.shape), fixed(vec.shape),
            ],
            out_specs=[token_spec, fixed((half, rows_a, LANES)), fixed((half, rows_a, LANES))],
            scratch_shapes=[
                pltpu.VMEM((width, 3 * width), bf16),
                pltpu.VMEM((width, lanes), f32),
                pltpu.VMEM((width, lanes), bf16),
                pltpu.VMEM((1, lanes), f32),
                pltpu.VMEM((width, lanes), bf16),
                pltpu.VMEM((3 * width, lanes), bf16),
                pltpu.VMEM((3 * width, width), f32),
                pltpu.VMEM((4, width, LANES), f32),
                pltpu.VMEM((rows_a, LANES), f32),
            ],
        ),
        out_shape=[
            shape_of(block_in.shape, f32),
            shape_of((half, rows_a, LANES), f32),
            shape_of((half, rows_a, LANES), bf16),
        ],
        compiler_params=params(),
        cost_estimate=pl.CostEstimate(flops=60_000_000_000, bytes_accessed=40_000_000, transcendentals=0),
        name="back",
    )(info, block_in, qkv, att, dh, wpn, wq, gp, vec)
    got_a = gather_sums(keep_a, send_a)

    def muon(got, moment_a, moment_b, weight_a, weight_b, vectors, name):
        ca, cb = moment_a.shape[1], moment_b.shape[1]
        ga, gb, sa, sb, spread, state, vector = small_call(
            state_kernel,
            [
                (moment_a.shape, f32), (moment_b.shape, f32), (moment_a.shape, f32), (moment_b.shape, f32),
                ((half, ca + cb, width), bf16), ((ca + cb, width), f32), ((vectors, LANES), f32),
            ],
            name + "_state",
        )(got, moment_a, moment_b)
        own = exchange(spread)
        other = swap(own)
        ua, ub_ = small_call(
            functools.partial(newton_kernel, (ca * devices, cb * devices)),
            [(moment_a.shape, f32), (moment_b.shape, f32)],
            name + "_newton",
        )(own, other, state, weight_a, weight_b)
        return ga, gb, sa, sb, ua, ub_, vector

    gu, gd, su, sd, uu, ud, vector_b = muon(
        got_b, up_moment, down_moment, up_weight, down_weight, 4 * blocks + ff // LANES, "mlp"
    )
    gq, gpr, sq, sp, uq, up, vector_a = muon(
        got_a, qkv_moment, proj_moment, qkv_weight, proj_weight, 4 * blocks, "att"
    )
    vector_grad = jnp.concatenate(
        [vector_a.reshape(4, width), vector_b[: 4 * blocks].reshape(4, width)], axis=0
    )
    bias_grad = vector_b[4 * blocks :].reshape(ff)

    def normalized_step(param, gradient):
        return param - vector_rate * gradient * lax.rsqrt(
            jnp.mean(gradient * gradient, axis=-1, keepdims=True) + norm_eps
        )

    return (
        out, dx, gq, gpr, gu, gd, vector_grad, bias_grad, uq, up, uu, ud, sq, sp, su, sd,
        normalized_step(feature_vectors, vector_grad),
        normalized_step(up_bias, bias_grad),
    )


def solution(mesh):
    rows, columns, whole = P("dp", None), P(None, "dp"), P()
    return jax.shard_map(
        body,
        mesh=mesh,
        in_specs=(rows, rows, P("dp")) + (columns,) * 4 + (whole,) * 2 + (columns,) * 4,
        out_specs=(rows, rows) + (columns,) * 4 + (whole,) * 2 + (columns,) * 8 + (whole,) * 2,
        check_vma=False,
    )
```

time: 1290 us -> 450 us (0.35)
  blocking collectives: 469 us -> 22.8 us
  Pallas kernels: 0 us -> 240 us
  local copies, waits for them, and re-layouts: 218 us -> 35.4 us
  matrix products: 175 us -> 0 us
  other arithmetic: 170 us -> 8.58 us
  loops' own time: 48.1 us -> 0 us
  waiting for transfers between devices: 140 us -> 106 us
  starting transfers between devices: 49.9 us -> 26.4 us
  between operations: 16 us -> 2.42 us
    unnamed x1 -> x0, blocking collectives: 309 us -> none
    pallas_call x0 -> x8, Pallas kernels: none -> 240 us  [the longest x1 79.5 us: body(): pl.pallas_call(mlp_kernel, grid_spec=pltpu.PrefetchScalarGridSpec(num_sca...]
    dot_general x87 -> x0, matrix products: 175 us -> none  [the longest x16 41 us: contract_cols(): lax.dot_general(left, right, (((1,), (1,)), ((), ())), preferred_element_...]
    add x46 -> x0, other arithmetic: 86 us -> none  [the longest x40 81.6 us: visit(): total + grad]
    all_gather x2 -> x0, blocking collectives: 84.5 us -> none  [the longest x1 46.6 us: body(): lax.all_gather(qkv_weight.astype(jnp.bfloat16), 'dp', axis=1, tiled=True)]
    reduce_scatter x2 -> x0, waiting for transfers between devices: 78.7 us -> none  [the longest x1 78.7 us: body(): lax.psum_scatter(totals[3], 'dp', scatter_dimension=1, tiled=True)]
    psum x1 -> x0, blocking collectives: 75.1 us -> none  [body(): vector_grad, bias_grad = lax.psum((totals[4], totals[5]), 'dp')]
    all_to_all x2 -> x5, waiting for transfers between devices: 54.4 us -> 105 us  [exchange(): return lax.all_to_all(x, 'dp', 0, 0, axis_index_groups=planes, tiled=True)]
  transfers between devices with their start and end apart: 22 -> 11, of which waited for: 4 -> 6; matrix products, arithmetic and copies ran while one was open for 27% -> 7% of each run, Pallas kernels for 0% -> 17%
where the time goes in v1:
time: 450 us; the launch traced here: 442 us
  Pallas kernels  240 us (53%)
  waiting for transfers between devices  106 us (24%)
  local copies, waits for them, and re-layouts  35.4 us (8%)
  starting transfers between devices  26.4 us (6%)
  blocking collectives  22.8 us (5%)
  other arithmetic  8.58 us (2%)
    all_to_all x5, waiting for transfers between devices, exchange(): return lax.all_to_all(x, 'dp', 0, 0, axis_index_groups=planes, tiled=True)  105 us
    pallas_call x1, Pallas kernels, body(): pl.pallas_call(mlp_kernel, grid_spec=pltpu.PrefetchScalarGridSpec(num_sca...  79.5 us
    pallas_call x1, Pallas kernels, body(): pl.pallas_call(back_kernel, grid_spec=pltpu.PrefetchScalarGridSpec(num_sc...  54.2 us
    pallas_call x2, Pallas kernels, muon(): small_call(functools.partial(newton_kernel, (ca * devices, cb * devices))...  53.9 us
    pallas_call x1, Pallas kernels, body(): pl.pallas_call(attend_kernel, grid_spec=pltpu.PrefetchScalarGridSpec(num_...  44.7 us
    unnamed x68, local copies, waits for them, and re-layouts  29 us
    all_to_all x5, starting transfers between devices, exchange(): return lax.all_to_all(x, 'dp', 0, 0, axis_index_groups=planes, tiled=True)  25.7 us
    all_to_all x1, blocking collectives, exchange(): return lax.all_to_all(x, 'dp', 0, 0, axis_index_groups=planes, tiled=True)  22.8 us
  transfers between devices with their start and end apart: 11, of which 6 were waited for; matrix products, arithmetic and copies ran while one was open for 7% of the time, Pallas kernels for 17%

profile of v1, /device:TPU:0, one launch (start us, length us, event | category | flops | bytes accessed | tf_op | source)
XLA Modules:
  0.0 442.5 jit_solution(14852106302546478447)
XLA Ops:
  3.8 1.7 copy.57.wu_ref.wa_ref
  5.5 1.7 copy.58.wd_ref.wb_ref
  7.3 2.6 prep.1
  9.8 22.8 %all_to_all.30.own_ref = bf16[16,36,384]{2,1,0:T(8,128)(2,1)S(1)} all-to-all(bf16[16,36,384]{2,1,0:T(8,128)(2,1)} %get-tuple-element.54), channel_id=1, replica_groups={{0,2,4,6,8,10,12,14,16,18,20,22,24,26,28,30},{1,3,5,7,9,11,13,15,17,19,..., dimensions={0} | all-to-all | bytes 884736 | tf_op jit(solution)/shard_map/all_to_all | solution.py:471
  32.7 3.8 all-to-all-start.1
  37.8 28.7 %all-to-all-done.1.own_ref = bf16[16,108,384]{2,1,0:T(8,128)(2,1)S(1)} async-done(((bf16[16,108,384]{2,1,0:T(8,128)(2,1)}), bf16[16,108,384]{2,1,0:T(8,128)(2,1)S(1)}, u32[]{:S(2)}, u32[]{:S(2)}) %all-to-all-start.1) | async-done | bytes 1327136 | tf_op jit(solution)/shard_map/all_to_all | solution.py:471
  69.7 44.7 %attend.1 = (bf16[8,1152,512]{2,1,0:T(8,128)(2,1)}, bf16[8,3072,256]{2,1,0:T(8,128)(2,1)}, bf16[8,384,512]{2,1,0:T(8,128)(2,1)}, bf16[1152,384]{1,0:T(8,128)(2,1)}) custom-call(s32[2]{0:T(128)} %pad_add_fusion.info, bf16[4096,384]{1,0:T(8,128)(2,1)} %x_ref.5, bf16[16,36,384]{2,1,0:T(8,128)(2,1)} %copy-done.8, ...), custom_call_target="tpu_custom_call" | custom-call | flops 40000000000 | bytes 30000000 | tf_op jit(solution)/shard_map/attend/pallas_call | solution.py:494
  117.0 79.5 %mlp.1 = (f32[4096,384]{1,0:T(8,128)}, f32[8,384,512]{2,1,0:T(8,128)}, f32[384,384]{1,0:T(8,128)}, bf16[384,384]{1,0:T(8,128)(2,1)}, f32[16,320,128]{2,1,0:T(8,128)}, /*index=5*/bf16[16,320,128]{2,1,0:T(8,128)(2,1)}) custom-call(s32[2]{0:T(128)} %pad_add_fusion.info, bf16[4096,384]{1,0:T(8,128)(2,1)} %x_ref.5, bf16[4096,384]{1,0:T(8,128)(2,1)} %cot_ref.1, ...), custom_call_target="tpu_custom_call" | custom-call | flops 80000000000 | bytes 30000000 | tf_op jit(solution)/shard_map/mlp/pallas_call | solution.py:515
  196.5 54.2 %back.1 = (f32[4096,384]{1,0:T(8,128)}, f32[16,160,128]{2,1,0:T(8,128)}, bf16[16,160,128]{2,1,0:T(8,128)(2,1)}) custom-call(s32[2]{0:T(128)} %pad_add_fusion.info, bf16[4096,384]{1,0:T(8,128)(2,1)} %x_ref.5, bf16[8,1152,512]{2,1,0:T(8,128)(2,1)} %get-tuple-element.59.qkv_ref, bf16[8,3072,256]{2,1,0:T(8,128)(2,1)} %get-tuple-element.60.att_ref, ...), custom_call_target="tpu_custom_call" | custom-call | flops 60000002048 | bytes 40000000 | tf_op jit(solution)/shard_map/back/pallas_call | solution.py:569
  251.3 1.8 collective-permute-done.2
  253.1 2.5 add_convert_fusion.1
  255.5 6.6 %all-to-all-start.2 = ((bf16[16,160,128]{2,1,0:T(8,128)(2,1)}), bf16[16,160,128]{2,1,0:T(8,128)(2,1)S(1)}, u32[]{:S(2)}, u32[]{:S(2)}) async-start(bf16[16,160,128]{2,1,0:T(8,128)(2,1)} %add_convert_fusion.1), calls=%async_computation.2 | async-start | bytes 1310720 | tf_op jit(solution)/shard_map/all_to_all | solution.py:471
  262.2 2.7 add_convert_fusion
  264.9 15.0 %all-to-all-done.2.got_ref = bf16[16,160,128]{2,1,0:T(8,128)(2,1)S(1)} async-done(((bf16[16,160,128]{2,1,0:T(8,128)(2,1)}), bf16[16,160,128]{2,1,0:T(8,128)(2,1)S(1)}, u32[]{:S(2)}, u32[]{:S(2)}) %all-to-all-start.2) | async-done | bytes 655392 | tf_op jit(solution)/shard_map/all_to_all | solution.py:471
  279.9 4.6 %all-to-all-start.3 = ((bf16[16,320,128]{2,1,0:T(8,128)(2,1)}), bf16[16,320,128]{2,1,0:T(8,128)(2,1)S(1)}, u32[]{:S(2)}, u32[]{:S(2)}) async-start(bf16[16,320,128]{2,1,0:T(8,128)(2,1)} %add_convert_fusion), calls=%async_computation.3 | async-start | bytes 2621440 | tf_op jit(solution)/shard_map/all_to_all | solution.py:471
  286.2 2.5 att_state.1
  288.8 24.4 %all-to-all-done.3.got_ref = bf16[16,320,128]{2,1,0:T(8,128)(2,1)S(1)} async-done(((bf16[16,320,128]{2,1,0:T(8,128)(2,1)}), bf16[16,320,128]{2,1,0:T(8,128)(2,1)S(1)}, u32[]{:S(2)}, u32[]{:S(2)}) %all-to-all-start.3) | async-done | bytes 1310752 | tf_op jit(solution)/shard_map/all_to_all | solution.py:471
  313.1 6.4 %all-to-all-start.4 = ((bf16[16,48,384]{2,1,0:T(8,128)(2,1)}), bf16[16,48,384]{2,1,0:T(8,128)(2,1)S(1)}, u32[]{:S(2)}, u32[]{:S(2)}) async-start(bf16[16,48,384]{2,1,0:T(8,128)(2,1)} %get-tuple-element.76), calls=%async_computation.4 | async-start | bytes 1179648 | tf_op jit(solution)/shard_map/all_to_all | solution.py:471
  321.2 3.1 mlp_state.1
  324.3 10.7 %all-to-all-done.4.own_ref = bf16[16,48,384]{2,1,0:T(8,128)(2,1)S(1)} async-done(((bf16[16,48,384]{2,1,0:T(8,128)(2,1)}), bf16[16,48,384]{2,1,0:T(8,128)(2,1)S(1)}, u32[]{:S(2)}, u32[]{:S(2)}) %all-to-all-start.4) | async-done | bytes 589856 | tf_op jit(solution)/shard_map/all_to_all | solution.py:471
  335.0 4.2 all-to-all-start.5
  339.3 25.8 %all-to-all-done.5.own_ref = bf16[16,96,384]{2,1,0:T(8,128)(2,1)S(1)} async-done(((bf16[16,96,384]{2,1,0:T(8,128)(2,1)}), bf16[16,96,384]{2,1,0:T(8,128)(2,1)S(1)}, u32[]{:S(2)}, u32[]{:S(2)}) %all-to-all-start.5) | async-done | bytes 1179680 | tf_op jit(solution)/shard_map/all_to_all | solution.py:471
  365.8 1.7 copy.69
  367.4 1.7 copy.77
  369.1 1.6 copy.70
  373.2 26.3 %att_newton.1 = (f32[384,36]{1,0:T(8,128)}, f32[384,12]{1,0:T(8,128)}) custom-call(bf16[16,48,384]{2,1,0:T(8,128)(2,1)} %copy-done.5, bf16[16,48,384]{2,1,0:T(8,128)(2,1)} %copy-done.7, f32[48,384]{1,0:T(8,128)} %get-tuple-element.77.state_ref, f32[384,36]{1,0:T(8,128)} %copy.55.wq_ref.wa_ref, f32[384,12]{1,0:T(8,128)} %copy.56.wp_ref.wb_ref), custom_call_target="tpu_custom_call" | custom-call | tf_op jit(solution)/shard_map/att_newton/pallas_call | solution.py:614
  399.5 1.7 copy.73
  401.2 1.6 copy.74
  405.0 1.7 copy.71
  411.4 27.6 %mlp_newton.1 = (f32[384,48]{1,0:T(8,128)}, f32[384,48]{1,0:T(8,128)}) custom-call(bf16[16,96,384]{2,1,0:T(8,128)(2,1)} %copy-done.2, bf16[16,96,384]{2,1,0:T(8,128)(2,1)} %copy-done.6, f32[96,384]{1,0:T(8,128)} %get-tuple-element.81.state_ref, f32[384,48]{1,0:T(8,128)} %copy.57.wu_ref.wa_ref, f32[384,48]{1,0:T(8,128)} %copy.58.wd_ref.wb_ref), custom_call_target="tpu_custom_call" | custom-call | tf_op jit(solution)/shard_map/mlp_newton/pallas_call | solution.py:614
  439.0 1.7 copy.75
  440.6 1.7 copy.76
  (81 shorter events, 22.7 us)
Async XLA Ops:
  32.7 3.8 copy-start.8
  32.7 33.9 %all-to-all-start.1 = ((bf16[16,108,384]{2,1,0:T(8,128)(2,1)}), bf16[16,108,384]{2,1,0:T(8,128)(2,1)S(1)}, u32[]{:S(2)}, u32[]{:S(2)}) async-start(bf16[16,108,384]{2,1,0:T(8,128)(2,1)} %get-tuple-element.57), calls=%async_computation.1 | async-start | bytes 2752512 | tf_op jit(solution)/shard_map/all_to_all | solution.py:471
  36.5 31.6 %copy-start.15 = (f32[8,384]{1,0:T(8,128)S(1)}, f32[8,384]{1,0:T(8,128)}, u32[]{:S(2)}) copy-start(f32[8,384]{1,0:T(8,128)} %param.20) | copy-start | bytes 36868
  36.5 31.6 %collective-permute-start = (bf16[16,36,384]{2,1,0:T(8,128)(2,1)S(1)}, bf16[16,36,384]{2,1,0:T(8,128)(2,1)}, u32[]{:S(2)}, u32[]{:S(2)}) collective-permute-start(bf16[16,36,384]{2,1,0:T(8,128)(2,1)S(1)} %all_to_all.30.own_ref), channel_id=1, source_target_pairs={{0,1},{1,0},{2,3},{3,2},{4,5},{5,4},{6,7},{7,6},{8,9},{9,8},{10,11... | collective-permute-start | bytes 1327112 | tf_op jit(solution)/shard_map/ppermute | solution.py:474
  66.6 3.2 copy-start
  68.1 46.4 %collective-permute-start.1 = (bf16[16,108,384]{2,0,1:T(8,128)(2,1)}, bf16[16,108,384]{2,0,1:T(8,128)(2,1)S(1)}, u32[]{:S(2)}, u32[]{:S(2)}) collective-permute-start(bf16[16,108,384]{2,0,1:T(8,128)(2,1)} %copy.59), channel_id=1, source_target_pairs={{0,1},{1,0},{2,3},{3,2},{4,5},{5,4},{6,7},{7,6},{8,9},{9,8},{10,11... | collective-permute-start | bytes 3981320 | tf_op jit(solution)/shard_map/ppermute | solution.py:474
  250.7 2.4 collective-permute-start.2
  250.8 11.4 %collective-permute-start.3 = (bf16[16,320,128]{2,1,0:T(8,128)(2,1)}, bf16[16,320,128]{2,1,0:T(8,128)(2,1)}, u32[]{:S(2)}, u32[]{:S(2)}) collective-permute-start(bf16[16,320,128]{2,1,0:T(8,128)(2,1)} %get-tuple-element.71), channel_id=1, source_target_pairs={{0,1},{1,0},{2,3},{3,2},{4,5},{5,4},{6,7},{7,6},{8,9},{9,8},{10,11... | collective-permute-start | bytes 3932168 | tf_op jit(solution)/shard_map/ppermute | solution.py:474
  253.1 9.1 %copy-start.3 = (f32[16,320,128]{2,1,0:T(8,128)S(1)}, f32[16,320,128]{2,1,0:T(8,128)}, u32[]{:S(2)}) copy-start(f32[16,320,128]{2,1,0:T(8,128)} %get-tuple-element.70) | copy-start | bytes 7864324
  255.5 24.4 %all-to-all-start.2 = ((bf16[16,160,128]{2,1,0:T(8,128)(2,1)}), bf16[16,160,128]{2,1,0:T(8,128)(2,1)S(1)}, u32[]{:S(2)}, u32[]{:S(2)}) async-start(bf16[16,160,128]{2,1,0:T(8,128)(2,1)} %add_convert_fusion.1), calls=%async_computation.2 | async-start | bytes 1310720 | tf_op jit(solution)/shard_map/all_to_all | solution.py:471
  264.9 19.6 %copy-start.14 = (f32[384,36]{0,1:T(8,128)S(1)}, f32[384,36]{0,1:T(8,128)}, u32[]{:S(2)}) copy-start(f32[384,36]{0,1:T(8,128)} %param.22) | copy-start | bytes 165892
  264.9 20.5 %copy-start.21 = (f32[384,12]{0,1:T(8,128)S(1)}, f32[384,12]{0,1:T(8,128)}, u32[]{:S(2)}) copy-start(f32[384,12]{0,1:T(8,128)} %param.23) | copy-start | bytes 55300
  279.9 5.5 %copy-start.4 = (bf16[16,160,128]{2,1,0:T(8,128)(2,1)}, bf16[16,160,128]{2,1,0:T(8,128)(2,1)S(1)}, u32[]{:S(2)}) copy-start(bf16[16,160,128]{2,1,0:T(8,128)(2,1)S(1)} %all-to-all-done.2.got_ref) | copy-start | bytes 1966084
  279.9 33.2 %all-to-all-start.3 = ((bf16[16,320,128]{2,1,0:T(8,128)(2,1)}), bf16[16,320,128]{2,1,0:T(8,128)(2,1)S(1)}, u32[]{:S(2)}, u32[]{:S(2)}) async-start(bf16[16,320,128]{2,1,0:T(8,128)(2,1)} %add_convert_fusion), calls=%async_computation.3 | async-start | bytes 2621440 | tf_op jit(solution)/shard_map/all_to_all | solution.py:471
  284.6 35.0 %copy-start.12 = (f32[384,48]{0,1:T(8,128)S(1)}, f32[384,48]{0,1:T(8,128)}, u32[]{:S(2)}) copy-start(f32[384,48]{0,1:T(8,128)} %param.24) | copy-start | bytes 221188
  285.4 35.0 %copy-start.13 = (f32[384,48]{0,1:T(8,128)S(1)}, f32[384,48]{0,1:T(8,128)}, u32[]{:S(2)}) copy-start(f32[384,48]{0,1:T(8,128)} %param.25) | copy-start | bytes 221188
  313.1 8.1 %copy-start.1 = (bf16[16,320,128]{2,1,0:T(8,128)(2,1)}, bf16[16,320,128]{2,1,0:T(8,128)(2,1)S(1)}, u32[]{:S(2)}) copy-start(bf16[16,320,128]{2,1,0:T(8,128)(2,1)S(1)} %all-to-all-done.3.got_ref) | copy-start | bytes 3932164
  313.1 21.9 %all-to-all-start.4 = ((bf16[16,48,384]{2,1,0:T(8,128)(2,1)}), bf16[16,48,384]{2,1,0:T(8,128)(2,1)S(1)}, u32[]{:S(2)}, u32[]{:S(2)}) async-start(bf16[16,48,384]{2,1,0:T(8,128)(2,1)} %get-tuple-element.76), calls=%async_computation.4 | async-start | bytes 1179648 | tf_op jit(solution)/shard_map/all_to_all | solution.py:471
  324.3 40.8 %copy-start.23 = (f32[12,128]{1,0:T(8,128)S(1)}, f32[12,128]{1,0:T(8,128)}, u32[]{:S(2)}) copy-start(f32[12,128]{1,0:T(8,128)} %get-tuple-element.74) | copy-start | bytes 18436
  335.0 34.1 %copy-start.5 = (bf16[16,48,384]{2,1,0:T(8,128)(2,1)}, bf16[16,48,384]{2,1,0:T(8,128)(2,1)S(1)}, u32[]{:S(2)}) copy-start(bf16[16,48,384]{2,1,0:T(8,128)(2,1)S(1)} %all-to-all-done.4.own_ref) | copy-start | bytes 1769476
  335.0 30.1 %all-to-all-start.5 = ((bf16[16,96,384]{2,1,0:T(8,128)(2,1)}), bf16[16,96,384]{2,1,0:T(8,128)(2,1)S(1)}, u32[]{:S(2)}, u32[]{:S(2)}) async-start(bf16[16,96,384]{2,1,0:T(8,128)(2,1)} %get-tuple-element.80), calls=%async_computation.5 | async-start | bytes 2359296 | tf_op jit(solution)/shard_map/all_to_all | solution.py:471
  339.2 33.2 %collective-permute-start.4 = (bf16[16,48,384]{2,1,0:T(8,128)(2,1)S(1)}, bf16[16,48,384]{2,1,0:T(8,128)(2,1)S(1)}, u32[]{:S(2)}, u32[]{:S(2)}) collective-permute-start(bf16[16,48,384]{2,1,0:T(8,128)(2,1)S(1)} %all-to-all-done.4.own_ref), channel_id=1, source_target_pairs={{0,1},{1,0},{2,3},{3,2},{4,5},{5,4},{6,7},{7,6},{8,9},{9,8},{10,11... | collective-permute-start | bytes 1769480 | tf_op jit(solution)/shard_map/ppermute | solution.py:474
  365.1 36.1 %copy-start.2 = (bf16[16,96,384]{2,1,0:T(8,128)(2,1)}, bf16[16,96,384]{2,1,0:T(8,128)(2,1)S(1)}, u32[]{:S(2)}) copy-start(bf16[16,96,384]{2,1,0:T(8,128)(2,1)S(1)} %all-to-all-done.5.own_ref) | copy-start | bytes 3538948
  365.1 45.2 %collective-permute-start.5 = (bf16[16,96,384]{2,1,0:T(8,128)(2,1)S(1)}, bf16[16,96,384]{2,1,0:T(8,128)(2,1)S(1)}, u32[]{:S(2)}, u32[]{:S(2)}) collective-permute-start(bf16[16,96,384]{2,1,0:T(8,128)(2,1)S(1)} %all-to-all-done.5.own_ref), channel_id=1, source_target_pairs={{0,1},{1,0},{2,3},{3,2},{4,5},{5,4},{6,7},{7,6},{8,9},{9,8},{10,11... | collective-permute-start | bytes 3538952 | tf_op jit(solution)/shard_map/ppermute | solution.py:474
  372.4 34.2 %copy-start.11 = (f32[384,48]{1,0:T(8,128)S(1)}, f32[384,48]{1,0:T(8,128)}, u32[]{:S(2)}) copy-start(f32[384,48]{1,0:T(8,128)} %get-tuple-element.111) | copy-start | bytes 221188
  372.4 35.0 %copy-start.10 = (f32[384,48]{1,0:T(8,128)S(1)}, f32[384,48]{1,0:T(8,128)}, u32[]{:S(2)}) copy-start(f32[384,48]{1,0:T(8,128)} %get-tuple-element.120) | copy-start | bytes 221188
  373.2 34.9 %copy-start.9 = (f32[384,48]{1,0:T(8,128)S(1)}, f32[384,48]{1,0:T(8,128)}, u32[]{:S(2)}) copy-start(f32[384,48]{1,0:T(8,128)} %get-tuple-element.121) | copy-start | bytes 221188
  373.2 36.4 %copy-start.16 = (f32[8,384]{1,0:T(8,128)S(1)}, f32[8,384]{1,0:T(8,128)}, u32[]{:S(2)}) copy-start(f32[8,384]{1,0:T(8,128)} %param.20) | copy-start | bytes 36868
  399.5 9.4 %copy-start.22 = (f32[4,384]{1,0:T(4,128)S(1)}, f32[4,384]{1,0:T(4,128)}, u32[]{:S(2)}) copy-start(f32[4,384]{1,0:T(4,128)} %reshape.65) | copy-start | bytes 18436
  399.5 9.5 %copy-start.18 = (f32[24,128]{1,0:T(8,128)S(1)}, f32[24,128]{1,0:T(8,128)}, u32[]{:S(2)}) copy-start(f32[24,128]{1,0:T(8,128)} %get-tuple-element.75) | copy-start | bytes 36868
  399.5 9.5 %copy-start.20 = (f32[1536]{0:T(1024)S(1)}, f32[1536]{0:T(1024)}, u32[]{:S(2)}) copy-start(f32[1536]{0:T(1024)} %param.21) | copy-start | bytes 18436
  409.0 30.0 %copy-start.17 = (f32[8,384]{1,0:T(8,128)}, f32[8,384]{1,0:T(8,128)S(1)}, u32[]{:S(2)}) copy-start(f32[8,384]{1,0:T(8,128)S(1)} %get-tuple-element.127) | copy-start | bytes 36868
  (3 other events, 3.3 us)

commit v2 on v1

v2 whole, which is shorter than its diff:
```python
import functools
import math

import jax
import jax.numpy as jnp
from jax import lax
from jax.experimental import pallas as pl
from jax.experimental.pallas import tpu as pltpu
from jax.sharding import PartitionSpec as P

HEAD_DIM = 64
SEQ = 256
GROUP = 2
LANES = 128

norm_eps = 1e-06
newton_a = 3.4445
newton_b = -4.775
newton_c = 2.0315
momentum_decay = 0.9
matrix_rate = 0.15
vector_rate = 0.2

f32 = jnp.float32
bf16 = jnp.bfloat16


def nn(a, b):
    return lax.dot_general(a, b, (((1,), (0,)), ((), ())), preferred_element_type=f32)


def nt(a, b):
    return lax.dot_general(a, b, (((1,), (1,)), ((), ())), preferred_element_type=f32)


def tn(a, b):
    return lax.dot_general(a, b, (((0,), (0,)), ((), ())), preferred_element_type=f32)


def cols(index):
    return slice(index * LANES, (index + 1) * LANES)


def norm_parts(chunk):
    width = chunk.shape[0]
    center = chunk - jnp.sum(chunk, axis=0, keepdims=True) * (1.0 / width)
    scale = lax.rsqrt(jnp.sum(center * center, axis=0, keepdims=True) * (1.0 / width) + norm_eps)
    return center * scale, scale


def norm_back(inner, normed, scale):
    width = inner.shape[0]
    mean = jnp.sum(inner, axis=0, keepdims=True) * (1.0 / width)
    cross = jnp.sum(inner * normed, axis=0, keepdims=True) * (1.0 / width)
    return scale * (inner - mean - normed * cross)


def split_parts(x):
    high = x.astype(bf16)
    return high, (x - high.astype(f32)).astype(bf16)


def shard_rows(par, shard, own_ref, other_ref, first, count):
    span = slice(first, first + count)
    return jnp.where(par == shard % 2, own_ref[shard // 2, span, :], other_ref[shard // 2, span, :])


def lane_rows(acc):
    return [jnp.sum(acc[cols(c), :].T, axis=0, keepdims=True) for c in range(acc.shape[0] // LANES)]


def wide_rows(acc, width):
    rows = lane_rows(acc)
    per = width // LANES
    return [jnp.concatenate(rows[i : i + per], axis=1) for i in range(0, len(rows), per)]


def rounded(x):
    return x.astype(bf16).astype(f32)


def prep_kernel(wq_ref, wp_ref, wu_ref, wd_ref, first_ref, second_ref):
    first = wq_ref[...].astype(bf16)
    second = jnp.concatenate([wu_ref[...], wd_ref[...], wp_ref[...]], axis=0).astype(bf16)
    for index in range(first_ref.shape[0]):
        first_ref[index] = first
        second_ref[index, : second.shape[0], :] = second
        second_ref[index, second.shape[0] :, :] = jnp.zeros_like(second_ref[index, second.shape[0] :, :])


def attend_kernel(start, info, x_ref, vec_ref, *refs):
    if start == 0:
        own_ref, other_ref, qkv_ref, att_ref, out_ref, wq_ref, z_scr, qkv_scr, s_scr, p_scr, stage = refs
    else:
        wq_ref, _, _, _, qkv_ref, att_ref, out_ref, z_scr, qkv_scr, s_scr, p_scr = refs
    width, lanes = z_scr.shape
    heads = width // HEAD_DIM
    group = start + pl.program_id(0)

    if start == 0:

        @pl.when(pl.program_id(0) == 0)
        def _():
            count = own_ref.shape[1]
            for shard in range(2 * own_ref.shape[0]):
                rows = shard_rows(info[1], shard, own_ref, other_ref, 0, count)
                stage[shard * count : (shard + 1) * count, :] = rows.astype(f32)
            wq_ref[...] = stage[...].astype(bf16)

    @pl.when(group * GROUP < info[0])
    def _():
        for c in range(lanes // LANES):
            chunk = x_ref[cols(c), :].astype(f32).T
            normed, _ = norm_parts(chunk)
            z_scr[:, cols(c)] = (normed * vec_ref[0] + vec_ref[1]).astype(bf16)
        for part in range(3):
            rows = slice(part * width, (part + 1) * width)
            made = nn(wq_ref[rows, :], z_scr[...])
            for c in range(lanes // LANES):
                piece = made[:, cols(c)]
                if part == 0:
                    piece = (piece + vec_ref[2]) * (1.0 / math.sqrt(HEAD_DIM))
                elif part == 2:
                    piece = piece + vec_ref[3]
                piece = piece.astype(bf16)
                qkv_scr[rows, cols(c)] = piece
                qkv_ref[rows, cols(c)] = piece
        for image in range(lanes // SEQ):
            span = slice(image * SEQ, (image + 1) * SEQ)
            for head in range(heads):
                low = head * HEAD_DIM
                query = qkv_scr[low : low + HEAD_DIM, span]
                keys = qkv_scr[width + low : width + low + HEAD_DIM, span]
                s_scr[image * heads + head] = tn(keys, query)
        for image in range(lanes // SEQ):
            span = slice(image * SEQ, (image + 1) * SEQ)
            for head in range(heads):
                low = head * HEAD_DIM
                slot = image * heads + head
                for c in range(SEQ // LANES):
                    scores = s_scr[slot, :, cols(c)]
                    top = jnp.max(scores, axis=0, keepdims=True)
                    raised = jnp.exp(scores - top)
                    total = jnp.sum(raised, axis=0, keepdims=True)
                    attend = (raised * (1.0 / total)).astype(bf16)
                    p_scr[slot, :, cols(c)] = attend
                    att_ref[slot * SEQ : (slot + 1) * SEQ, cols(c)] = attend
                values = qkv_scr[2 * width + low : 2 * width + low + HEAD_DIM, span]
                out_ref[low : low + HEAD_DIM, span] = nn(values, p_scr[slot]).astype(bf16)


def mlp_kernel(
    info, x_ref, cot_ref, att_ref, own_ref, other_ref, vec_ref, ub_ref,
    out_ref, dh_ref, gp_ref, wpn_ref, keep_ref, send_ref,
    wun_scr, wdn_scr, wp_scr, wu_scr, wd_scr, gu_scr, gd_scr, rows_scr, bias_scr,
    h_scr, n_scr, z_scr, m_scr, act_scr, du_scr, dhb_scr, s_scr, stage, u_scr, d_scr,
):
    width, lanes = z_scr.shape
    ff = wu_scr.shape[0]
    half = own_ref.shape[0]
    part = ff // (2 * half)
    step = pl.program_id(0)
    block = u_scr.shape[1]

    @pl.when(step == 0)
    def _():
        gp_ref[...] = jnp.zeros_like(gp_ref)
        gu_scr[...] = jnp.zeros_like(gu_scr)
        gd_scr[...] = jnp.zeros_like(gd_scr)
        rows_scr[...] = jnp.zeros_like(rows_scr)
        bias_scr[...] = jnp.zeros_like(bias_scr)
        count = width // (2 * half)
        for shard in range(2 * half):
            rows = shard_rows(info[1], shard, own_ref, other_ref, 2 * part, count)
            stage[shard * count : (shard + 1) * count, :] = rows.astype(f32)
        wp_scr[...] = stage[:width, :].astype(bf16)
        wpn_ref[...] = stage[:width, :].T.astype(bf16)
        for low, wide_scr in ((0, wu_scr), (part, wd_scr)):
            if part % 16 == 0:
                for side, ref in enumerate((own_ref, other_ref)):
                    for index in range(half):
                        at = (side * half + index) * part
                        wide_scr[at : at + part, :] = ref[index, low : low + part, :]
            else:
                for side, ref in enumerate((own_ref, other_ref)):
                    for index in range(half):
                        at = (side * half + index) * part
                        stage[at : at + part, :] = ref[index, low : low + part, :].astype(f32)
                wide_scr[...] = stage[...].astype(bf16)
        for c in range(ff // block):
            rows = slice(c * block, (c + 1) * block)
            wun_scr[:, rows] = wu_scr[rows, :].T
            wdn_scr[:, rows] = wd_scr[rows, :].T

    @pl.when(step * GROUP >= info[0])
    def _():
        out_ref[...] = jnp.zeros_like(out_ref)

    @pl.when(step * GROUP < info[0])
    def _():
        made = nn(wp_scr[...], att_ref[...])
        total7 = jnp.zeros((width, LANES), f32)
        for c in range(lanes // LANES):
            chunk = x_ref[cols(c), :].astype(f32).T + made[:, cols(c)] + vec_ref[4]
            h_scr[:, cols(c)] = chunk
            normed, scale = norm_parts(chunk)
            n_scr[:, cols(c)] = normed
            s_scr[:, cols(c)] = scale
            z_scr[:, cols(c)] = (normed * vec_ref[5] + vec_ref[6]).astype(bf16)
            image = step * GROUP + c * LANES // SEQ
            cot = jnp.where(image < info[0], cot_ref[cols(c), :].astype(f32), 0.0).T
            m_scr[:, cols(c)] = cot.astype(bf16)
            total7 += cot
        rows_scr[3] += total7

        def first(c):
            rows = slice(c * block, (c + 1) * block)
            u_scr[c % 2] = nn(wu_scr[rows, :], z_scr[...])
            d_scr[c % 2] = nn(wd_scr[rows, :], m_scr[...])

        def second(c):
            for low in range(c * block, (c + 1) * block, 128):
                rows = slice(low, low + 128)
                here = slice(low - c * block, low - c * block + 128)
                bias = jnp.zeros((128, LANES), f32)
                for k in range(lanes // LANES):
                    u = u_scr[c % 2, here, cols(k)] + ub_ref[rows, :]
                    v = u * (1.0 / math.sqrt(2.0))
                    cdf = 0.5 + 0.5 * lax.erf(v)
                    act_scr[rows, cols(k)] = (u * cdf).astype(bf16)
                    slope = cdf + (v * (1.0 / math.sqrt(math.pi))) * jnp.exp(-(v * v))
                    du = d_scr[c % 2, here, cols(k)] * slope
                    du_scr[rows, cols(k)] = du.astype(bf16)
                    bias += du
                bias_scr[rows, :] += bias

        def third(c):
            rows = slice(c * block, (c + 1) * block)
            gu_scr[rows, :] += nt(du_scr[rows, :], z_scr[...])
            gd_scr[rows, :] += nt(act_scr[rows, :], m_scr[...])

        chunks = ff // block
        first(0)
        for c in range(chunks):
            if c + 1 < chunks:
                first(c + 1)
            second(c)
            third(c)
        down = nn(wdn_scr[...], act_scr[...])
        for c in range(lanes // LANES):
            image = step * GROUP + c * LANES // SEQ
            whole = down[:, cols(c)] + h_scr[:, cols(c)] + vec_ref[7]
            out_ref[cols(c), :] = jnp.where(image < info[0], whole, 0.0).T
        dz = nn(wun_scr[...], du_scr[...])
        total4 = jnp.zeros((width, LANES), f32)
        total5 = jnp.zeros((width, LANES), f32)
        total6 = jnp.zeros((width, LANES), f32)
        for c in range(lanes // LANES):
            piece = dz[:, cols(c)]
            normed = n_scr[:, cols(c)]
            dh = norm_back(piece * vec_ref[5], normed, s_scr[:, cols(c)]) + m_scr[:, cols(c)].astype(f32)
            dh_ref[:, cols(c)] = dh
            dhb_scr[:, cols(c)] = dh.astype(bf16)
            total4 += dh
            total5 += piece * normed
            total6 += piece
        rows_scr[0] += total4
        rows_scr[1] += total5
        rows_scr[2] += total6
        gp_ref[...] += nt(dhb_scr[...], att_ref[...])

    @pl.when(step == pl.num_programs(0) - 1)
    def _():
        vector = []
        for index in range(4):
            vector += wide_rows(rows_scr[index], width)
        hidden = wide_rows(bias_scr, width)
        side = len(hidden) // 2
        for index in range(len(hidden)):
            swapped = hidden[(index + side) % len(hidden)]
            vector.append(jnp.where(info[1] == 0, hidden[index], swapped))
        vector = jnp.concatenate(vector, axis=0)
        total = 2 * part + vector.shape[0]
        for index in range(half):
            keep_ref[index, :part, :] = gu_scr[index * part : (index + 1) * part, :]
            keep_ref[index, part : 2 * part, :] = gd_scr[index * part : (index + 1) * part, :]
            keep_ref[index, 2 * part : total, :] = rounded(vector)
            at = half * part + index * part
            if part % 16 == 0:
                send_ref[index, :part, :] = gu_scr[at : at + part, :].astype(bf16)
                send_ref[index, part : 2 * part, :] = gd_scr[at : at + part, :].astype(bf16)
                send_ref[index, 2 * part : total, :] = vector.astype(bf16)
            else:
                stage[:part, :] = gu_scr[at : at + part, :]
                stage[part : 2 * part, :] = gd_scr[at : at + part, :]
                stage[2 * part : total, :] = vector
                send_ref[index] = stage[: send_ref.shape[1], :].astype(bf16)


def back_kernel(start, last, info, x_ref, qkv_ref, att_ref, dh_ref, wpn_ref, wq_ref, gp_ref, vec_ref, *refs):
    if start:
        _, gq_in, rows_in = refs[:3]
        refs = refs[3:]
    if last:
        out_ref, keep_ref, send_ref, gq_ref, rows_ref, stage = refs[:6]
        refs = refs[6:]
    else:
        out_ref, gq_ref, rows_ref = refs[:3]
        refs = refs[3:]
    wqn_scr, n_scr, z_scr, s_scr, da_scr, dqkv_scr, up_scr, ds_scr = refs
    width, lanes = z_scr.shape
    heads = width // HEAD_DIM
    step = pl.program_id(0)
    group = start + step

    @pl.when(step == 0)
    def _():
        if start == 0:
            gq_ref[...] = jnp.zeros_like(gq_ref)
            rows_ref[...] = jnp.zeros_like(rows_ref)
        else:
            gq_ref[...] = gq_in[...]
            rows_ref[...] = rows_in[...]
        for c in range(3):
            rows = slice(c * width, (c + 1) * width)
            wqn_scr[:, rows] = wq_ref[rows, :].T

    @pl.when(group * GROUP >= info[0])
    def _():
        out_ref[...] = jnp.zeros_like(out_ref)

    @pl.when(group * GROUP < info[0])
    def _():
        da_scr[...] = nn(wpn_ref[...], dh_ref[...].astype(bf16)).astype(bf16)
        for image in range(lanes // SEQ):
            span = slice(image * SEQ, (image + 1) * SEQ)
            for head in range(heads):
                low = head * HEAD_DIM
                values = qkv_ref[2 * width + low : 2 * width + low + HEAD_DIM, span]
                up_scr[image * heads + head] = tn(values, da_scr[low : low + HEAD_DIM, span])
        for c in range(lanes // LANES):
            chunk = x_ref[cols(c), :].astype(f32).T
            normed, scale = norm_parts(chunk)
            n_scr[:, cols(c)] = normed
            s_scr[:, cols(c)] = scale
            z_scr[:, cols(c)] = (normed * vec_ref[0] + vec_ref[1]).astype(bf16)
        for image in range(lanes // SEQ):
            span = slice(image * SEQ, (image + 1) * SEQ)
            for head in range(heads):
                low = head * HEAD_DIM
                high = low + HEAD_DIM
                slot = image * heads + head
                base = slot * SEQ
                for c in range(SEQ // LANES):
                    attend = att_ref[base : base + SEQ, cols(c)].astype(f32)
                    upstream = up_scr[slot, :, cols(c)]
                    delta = jnp.sum(attend * upstream, axis=0, keepdims=True)
                    ds_scr[slot, :, cols(c)] = (attend * (upstream - delta)).astype(bf16)
                query = qkv_ref[low:high, span]
                keys = qkv_ref[width + low : width + high, span]
                dscore = ds_scr[slot]
                dquery = nn(keys, dscore) * (1.0 / math.sqrt(HEAD_DIM))
                dkey = nt(query, dscore)
                dvalue = nt(da_scr[low:high, span], att_ref[base : base + SEQ, :])
                dqkv_scr[low:high, span] = dquery.astype(bf16)
                dqkv_scr[width + low : width + high, span] = dkey.astype(bf16)
                dqkv_scr[2 * width + low : 2 * width + high, span] = dvalue.astype(bf16)
                rows_ref[2, low:high, :] += dquery[:, :LANES] + dquery[:, LANES:]
                rows_ref[3, low:high, :] += dvalue[:, :LANES] + dvalue[:, LANES:]
        for part in range(3):
            rows = slice(part * width, (part + 1) * width)
            gq_ref[rows, :] += nt(dqkv_scr[rows, :], z_scr[...])
        dz = nn(wqn_scr[...], dqkv_scr[...])
        total0 = jnp.zeros((width, LANES), f32)
        total1 = jnp.zeros((width, LANES), f32)
        for c in range(lanes // LANES):
            piece = dz[:, cols(c)]
            normed = n_scr[:, cols(c)]
            dx = norm_back(piece * vec_ref[0], normed, s_scr[:, cols(c)]) + dh_ref[:, cols(c)]
            out_ref[cols(c), :] = dx.T
            total0 += piece * normed
            total1 += piece
        rows_ref[0] += total0
        rows_ref[1] += total1

    if not last:
        return

    @pl.when(step == pl.num_programs(0) - 1)
    def _():
        count = 2 * keep_ref.shape[0]
        blocks = width // LANES
        sizes = (3 * width // count, width // count)
        rows = sum(sizes)
        stage[...] = jnp.zeros_like(stage)
        vector = []
        for index in range(4):
            vector += lane_rows(rows_ref[index])
        for index, row in enumerate(vector):
            stage[blocks * rows + index : blocks * rows + index + 1, :] = rounded(row)
        for shard in range(count):
            for c in range(blocks):
                low = c * rows
                for piece, size in zip((gq_ref, gp_ref), sizes):
                    stage[low : low + size, :] = piece[shard * size : (shard + 1) * size, cols(c)]
                    low += size

            @pl.when(info[1] == shard % 2)
            def _():
                keep_ref[shard // 2] = stage[...]

            @pl.when(info[1] != shard % 2)
            def _():
                send_ref[shard // 2] = stage[...].astype(bf16)


def unpack_att(total, rows, width, vectors):
    blocks = width // LANES
    grad = jnp.concatenate([total[c * rows : (c + 1) * rows] for c in range(blocks)], axis=1)
    return grad, total[blocks * rows : blocks * rows + vectors]


def state_kernel(got_ref, ma_ref, mb_ref, ga_ref, gb_ref, sa_ref, sb_ref, spread_ref, state_ref, vec_ref):
    first, width = ma_ref.shape
    rows = first + mb_ref.shape[0]
    total = got_ref[0].astype(f32)
    for index in range(1, got_ref.shape[0]):
        total += got_ref[index].astype(f32)
    if got_ref.shape[2] == width:
        grad, vec_ref[...] = total[:rows], total[rows : rows + vec_ref.shape[0]]
    else:
        grad, vec_ref[...] = unpack_att(total, rows, width, vec_ref.shape[0])
    ga_ref[...] = grad[:first]
    gb_ref[...] = grad[first:]
    state = grad + momentum_decay * jnp.concatenate([ma_ref[...], mb_ref[...]], axis=0)
    sa_ref[...] = state[:first]
    sb_ref[...] = state[first:]
    state_ref[...] = state
    for index in range(spread_ref.shape[0]):
        spread_ref[index] = state.astype(bf16)


def store_parts(x, left_ref, right_ref):
    width = x.shape[0]
    high, low = split_parts(x)
    left_ref[:, :width] = high
    left_ref[:, width : 2 * width] = high
    left_ref[:, 2 * width :] = low
    right_ref[:, :width] = high
    right_ref[:, width : 2 * width] = low
    right_ref[:, 2 * width :] = high


def newton_kernel(info, own_ref, other_ref, out_ref, whole_ref, gram_scr, poly_scr, pa, pb, sa, sb):
    count, rows, width = own_ref.shape
    first = info[1]
    eye = (
        lax.broadcasted_iota(jnp.int32, (width, width), 0)
        == lax.broadcasted_iota(jnp.int32, (width, width), 1)
    ).astype(f32)
    gram = jnp.zeros((width, width), f32)
    place = lax.broadcasted_iota(jnp.int32, (rows, width), 0)
    mine = (place < first) == (info[0] == 0)
    for ref in (own_ref, other_ref):
        part = jnp.concatenate(
            [jnp.where(mine, ref[index].astype(f32), 0.0) for index in range(count)], axis=0
        ).astype(bf16)
        gram += tn(part, part)
    norm = lax.rsqrt(jnp.sum(gram * eye) + norm_eps)
    out_ref[width:, :] = jnp.full((8, width), norm, f32)
    gram_scr[...] = gram * (norm * norm)
    whole_ref[...] = eye

    def turn(index, carry):
        store_parts(gram_scr[...], sa, sb)
        gram = gram_scr[...]
        poly = newton_a * eye + newton_b * gram + newton_c * nt(sa[...], sb[...])
        store_parts(poly, pa, pb)
        poly_scr[...] = nt(pa[...], sb[...])
        store_parts(whole_ref[...], sa, sb)
        whole_ref[...] = nt(pa[...], sb[...])

        @pl.when(index < 4)
        def _():
            store_parts(poly_scr[...], sa, sb)
            gram_scr[...] = nt(sa[...], pb[...])

        return carry

    lax.fori_loop(0, 5, turn, 0)
    out_ref[:width, :] = whole_ref[...]


def update_kernel(
    wide, info, mine_ref, theirs_ref, state_ref, wa_ref, wb_ref, ua_ref, ub_ref
):
    first = wa_ref.shape[0]
    rows = state_ref.shape[0]
    ours = info[0] == 0
    for low, high, w_ref, u_ref, columns, is_first in (
        (0, first, wa_ref, ua_ref, wide[0], True),
        (first, rows, wb_ref, ub_ref, wide[1], False),
    ):
        pick = ours if is_first else jnp.logical_not(ours)
        width = mine_ref.shape[1]
        whole = jnp.where(pick, mine_ref[:width, :], theirs_ref[:width, :])
        norm = jnp.where(pick, mine_ref[width : width + 1, :], theirs_ref[width : width + 1, :])
        state = state_ref[low:high, :] * norm
        sh, sl = split_parts(state)
        ph, pl_ = split_parts(whole)
        ortho = nt(sh, ph) + (nt(sl, ph) + nt(sh, pl_))
        u_ref[...] = w_ref[...] - (matrix_rate * 0.2 * math.sqrt(columns)) * ortho


def fixed(shape):
    return pl.BlockSpec(shape, lambda i, info: (0,) * len(shape))


ANY = pl.BlockSpec(memory_space=pl.ANY)


def params(grid=True):
    return pltpu.CompilerParams(
        dimension_semantics=("arbitrary",) if grid else None, vmem_limit_bytes=60 * 1024 * 1024
    )


def shape_of(shape, dtype):
    return jax.ShapeDtypeStruct(shape, dtype)


def cost(flops, read):
    return pl.CostEstimate(flops=int(flops), bytes_accessed=int(read), transcendentals=0)


def small_call(kernel, outs, name, scalars=0, scratch=()):
    vmem = pl.BlockSpec(memory_space=pltpu.VMEM)
    smem = pl.BlockSpec(memory_space=pltpu.SMEM)

    def call(*args):
        return pl.pallas_call(
            kernel,
            in_specs=[smem] * scalars + [vmem] * (len(args) - scalars),
            out_specs=[vmem] * len(outs),
            out_shape=[shape_of(*out) for out in outs],
            scratch_shapes=scratch,
            compiler_params=params(False),
            name=name,
        )(*args)

    return call


def group_specs(width, start):
    heads = width // HEAD_DIM
    lanes = GROUP * SEQ
    deep = lambda i, info: (start + i, 0, 0)
    return (
        pl.BlockSpec((lanes, width), lambda i, info: (start + i, 0)),
        pl.BlockSpec((None, 3 * width, lanes), deep),
        pl.BlockSpec((None, GROUP * heads * SEQ, SEQ), deep),
        pl.BlockSpec((None, width, lanes), deep),
    )


def attend_call(info, x, vec, start, stop, weights, before=()):
    width = x.shape[1]
    heads = width // HEAD_DIM
    lanes = GROUP * SEQ
    groups = x.shape[0] // lanes
    tokens, qkv_spec, att_spec, deep_spec = group_specs(width, start)
    fresh = start == 0
    return pl.pallas_call(
        functools.partial(attend_kernel, start),
        grid_spec=pltpu.PrefetchScalarGridSpec(
            num_scalar_prefetch=1,
            grid=(stop - start,),
            in_specs=[tokens, fixed(vec.shape)] + [fixed(w.shape) for w in weights] + [ANY] * len(before),
            out_specs=[qkv_spec, att_spec, deep_spec] + [fixed((3 * width, width))] * fresh,
            scratch_shapes=[
                pltpu.VMEM((width, lanes), bf16),
                pltpu.VMEM((3 * width, lanes), bf16),
                pltpu.VMEM((GROUP * heads, SEQ, SEQ), f32),
                pltpu.VMEM((GROUP * heads, SEQ, SEQ), bf16),
            ] + [pltpu.VMEM((3 * width, width), f32)] * fresh,
        ),
        out_shape=[
            shape_of((groups, 3 * width, lanes), bf16),
            shape_of((groups, GROUP * heads * SEQ, SEQ), bf16),
            shape_of((groups, width, lanes), bf16),
        ] + [shape_of((3 * width, width), bf16)] * fresh,
        input_output_aliases={3 + len(weights) + i: i for i in range(len(before))},
        compiler_params=params(),
        cost_estimate=cost(4e9 * (stop - start), 3e6 * (stop - start)),
        name="attend",
    )(info, x, vec, *weights, *before)


def mlp_call(info, x, cot, attn, own, other, vec, ub):
    width = x.shape[1]
    ff = ub.shape[0]
    half = own.shape[0]
    lanes = GROUP * SEQ
    groups = x.shape[0] // lanes
    block = 256
    tokens, _, _, deep_spec = group_specs(width, 0)
    rows = 2 * (ff // (2 * half)) + 4 + ff // width
    return pl.pallas_call(
        mlp_kernel,
        grid_spec=pltpu.PrefetchScalarGridSpec(
            num_scalar_prefetch=1,
            grid=(groups,),
            in_specs=[
                tokens, tokens, deep_spec,
                fixed(own.shape), fixed(own.shape), fixed(vec.shape), fixed(ub.shape),
            ],
            out_specs=[
                tokens, deep_spec, fixed((width, width)), fixed((width, width)),
                fixed((half, rows, width)), fixed((half, rows, width)),
            ],
            scratch_shapes=[
                pltpu.VMEM((width, ff), bf16),
                pltpu.VMEM((width, ff), bf16),
                pltpu.VMEM((width, width), bf16),
                pltpu.VMEM((ff, width), bf16),
                pltpu.VMEM((ff, width), bf16),
                pltpu.VMEM((ff, width), f32),
                pltpu.VMEM((ff, width), f32),
                pltpu.VMEM((4, width, LANES), f32),
                pltpu.VMEM((ff, LANES), f32),
                pltpu.VMEM((width, lanes), f32),
                pltpu.VMEM((width, lanes), f32),
                pltpu.VMEM((width, lanes), bf16),
                pltpu.VMEM((width, lanes), bf16),
                pltpu.VMEM((ff, lanes), bf16),
                pltpu.VMEM((ff, lanes), bf16),
                pltpu.VMEM((width, lanes), bf16),
                pltpu.VMEM((1, lanes), f32),
                pltpu.VMEM((ff, width), f32),
                pltpu.VMEM((2, block, lanes), f32),
                pltpu.VMEM((2, block, lanes), f32),
            ],
        ),
        out_shape=[
            shape_of(x.shape, f32),
            shape_of((groups, width, lanes), f32),
            shape_of((width, width), f32),
            shape_of((width, width), bf16),
            shape_of((half, rows, width), f32),
            shape_of((half, rows, width), bf16),
        ],
        compiler_params=params(),
        cost_estimate=cost(10e9 * groups, 4e6 * groups),
        name="mlp",
    )(info, x, cot, attn, own, other, vec, ub)


def back_call(info, x, qkv, att, dh, wpn, wq, gp, vec, half, start, stop, before=()):
    width = x.shape[1]
    heads = width // HEAD_DIM
    lanes = GROUP * SEQ
    groups = x.shape[0] // lanes
    tokens, qkv_spec, att_spec, deep_spec = group_specs(width, start)
    blocks = width // LANES
    rows = -(-(blocks * (4 * width // (2 * half)) + 4 * blocks) // 16) * 16
    last = stop == groups
    sums = [(3 * width, width), (4, width, LANES)]
    shards = (half, rows, LANES)
    scratch = [
        pltpu.VMEM((width, 3 * width), bf16),
        pltpu.VMEM((width, lanes), f32),
        pltpu.VMEM((width, lanes), bf16),
        pltpu.VMEM((1, lanes), f32),
        pltpu.VMEM((width, lanes), bf16),
        pltpu.VMEM((3 * width, lanes), bf16),
        pltpu.VMEM((GROUP * heads, SEQ, SEQ), f32),
        pltpu.VMEM((GROUP * heads, SEQ, SEQ), bf16),
    ]
    if last:
        outs = [(shards, f32), (shards, bf16)]
        scratch = [pltpu.VMEM(shape, f32) for shape in sums + [(rows, LANES)]] + scratch
    else:
        outs = [(shape, f32) for shape in sums]
    return pl.pallas_call(
        functools.partial(back_kernel, start, last),
        grid_spec=pltpu.PrefetchScalarGridSpec(
            num_scalar_prefetch=1,
            grid=(stop - start,),
            in_specs=[
                tokens, qkv_spec, att_spec, deep_spec,
                fixed(wpn.shape), fixed(wq.shape), fixed(gp.shape), fixed(vec.shape),
            ] + ([ANY] + [fixed(shape) for shape in sums] if before else []),
            out_specs=[tokens] + [fixed(shape) for shape, _ in outs],
            scratch_shapes=scratch,
        ),
        out_shape=[shape_of(x.shape, f32)] + [shape_of(*out) for out in outs],
        input_output_aliases={9: 0} if before else {},
        compiler_params=params(),
        cost_estimate=cost(7e9 * (stop - start), 5e6 * (stop - start)),
        name="back",
    )(info, x, qkv, att, dh, wpn, wq, gp, vec, *before)


def order_ff(up_bias, par, half):
    parts = up_bias.reshape(half, 2, -1)
    return jnp.where(
        par == 0,
        jnp.concatenate([parts[:, 0], parts[:, 1]]),
        jnp.concatenate([parts[:, 1], parts[:, 0]]),
    ).reshape(-1)


def natural_ff(bias, half):
    return jnp.swapaxes(bias.reshape(2, half, -1), 0, 1).reshape(-1)


def spread_lanes(array):
    return jnp.broadcast_to(array[..., None], array.shape + (LANES,))


def body(
    block_in,
    out_grad,
    live_counts,
    qkv_weight,
    proj_weight,
    up_weight,
    down_weight,
    feature_vectors,
    up_bias,
    qkv_moment,
    proj_moment,
    up_moment,
    down_moment,
):
    devices = lax.axis_size("dp")
    half = devices // 2
    par = (lax.axis_index("dp") % 2).astype(jnp.int32)
    width = block_in.shape[1]
    groups = block_in.shape[0] // (GROUP * SEQ)
    ff = up_bias.shape[0]
    blocks = width // LANES
    turned = [w.T for w in (qkv_weight, proj_weight, up_weight, down_weight)]
    wq_s, wp_s, wu_s, wd_s = turned
    mq_s, mp_s, mu_s, md_s = [m.T for m in (qkv_moment, proj_moment, up_moment, down_moment)]
    cq, cp, cu, cd = (w.shape[0] for w in turned)
    pairs = [(i, i ^ 1) for i in range(devices)]
    planes = [[2 * i + c for i in range(half)] for c in range(2)]
    info = jnp.stack([live_counts[0], par])
    vec = spread_lanes(feature_vectors)
    ub = spread_lanes(order_ff(up_bias, par, half))

    def exchange(x):
        return lax.all_to_all(x, "dp", 0, 0, axis_index_groups=planes, tiled=True)

    def swap(x):
        return lax.ppermute(x, "dp", pairs)

    def after(x, *others):
        return lax.optimization_barrier((x,) + others)[0]

    first, second = small_call(
        prep_kernel,
        [((half, cq, width), bf16), ((half, -(-(cu + cd + cp) // 16) * 16, width), bf16)],
        "prep",
    )(wq_s, wp_s, wu_s, wd_s)
    wq_own = exchange(first)
    wq_other = swap(wq_own)
    rest_own = exchange(after(second, wq_own))

    early = groups - 2 if groups > 2 else groups
    qkv, att, attn, wq = attend_call(info, block_in, vec, 0, early, (wq_own, wq_other))
    rest_own = after(rest_own, attn)
    rest_other = swap(rest_own)
    if early < groups:
        qkv, att, attn = attend_call(info, block_in, vec, early, groups, (wq,), (qkv, att, attn))
    out, dh, gp, wpn, keep_b, send_b = mlp_call(
        info, block_in, out_grad, attn, rest_own, rest_other, vec, ub
    )

    def fold(keep, received):
        return exchange((keep + received.astype(f32)).astype(bf16))

    swapped = swap(send_b)
    one = 1 if groups > 2 else groups
    most = groups - 1 if groups > 2 else groups
    done = back_call(info, block_in, qkv, att, dh, wpn, wq, gp, vec, half, 0, one)
    got_b = fold(keep_b, after(swapped, done[1]))
    if one < groups:
        done = back_call(info, block_in, qkv, att, dh, wpn, wq, gp, vec, half, one, most, done)
    got_b = after(got_b, done[1])

    def sums(got, moment_a, moment_b, vectors, lanes, name):
        rows = moment_a.shape[0] + moment_b.shape[0]
        return small_call(
            state_kernel,
            [
                (moment_a.shape, f32), (moment_b.shape, f32), (moment_a.shape, f32), (moment_b.shape, f32),
                ((half, rows, width), bf16), ((rows, width), f32), ((vectors, lanes), f32),
            ],
            name + "_state",
        )(got, moment_a, moment_b)

    def polynomials(own, other, first, name):
        square = pltpu.VMEM((width, width), f32)
        parts = pltpu.VMEM((width, 3 * width), bf16)
        return small_call(
            newton_kernel,
            [((width + 8, width), f32)],
            name + "_newton",
            scalars=1,
            scratch=[square, square, square, parts, parts, parts, parts],
        )(jnp.stack([par, jnp.full((), first, jnp.int32)]), own, other)[0]

    def updates(mine, theirs, state, weight_a, weight_b, name):
        wide = (weight_a.shape[0] * devices, weight_b.shape[0] * devices)
        return small_call(
            functools.partial(update_kernel, wide),
            [(weight_a.shape, f32), (weight_b.shape, f32)],
            name + "_update",
            scalars=1,
        )(par.reshape(1), mine, theirs, state, weight_a, weight_b)

    gu, gd, su, sd, spread_b, state_b, vector_b = sums(
        got_b, mu_s, md_s, 4 + ff // width, width, "mlp"
    )
    own_b = exchange(spread_b)
    if most < groups:
        done = back_call(info, block_in, qkv, att, dh, wpn, wq, gp, vec, half, most, groups, done)
    dx, keep_a, send_a = done
    got_a = fold(keep_a, swap(send_a))
    other_b = swap(own_b)
    gq, gpr, sq, sp, spread_a, state_a, vector_a = sums(got_a, mq_s, mp_s, 4 * blocks, LANES, "att")
    own_a = exchange(spread_a)
    other_a = swap(own_a)
    mine_b = polynomials(own_b, other_b, cu, "mlp")
    uu, ud = updates(mine_b, swap(mine_b), state_b, wu_s, wd_s, "mlp")
    mine_a = polynomials(own_a, other_a, cq, "att")
    uq, up = updates(mine_a, swap(mine_a), state_a, wq_s, wp_s, "att")

    vector_grad = jnp.concatenate([vector_a.reshape(4, width), vector_b[:4]], axis=0)
    bias_grad = natural_ff(vector_b[4:].reshape(ff), half)

    def normalized_step(param, gradient):
        return param - vector_rate * gradient * lax.rsqrt(
            jnp.mean(gradient * gradient, axis=-1, keepdims=True) + norm_eps
        )

    return (
        out, dx, gq.T, gpr.T, gu.T, gd.T, vector_grad, bias_grad, uq.T, up.T, uu.T, ud.T,
        sq.T, sp.T, su.T, sd.T,
        normalized_step(feature_vectors, vector_grad),
        normalized_step(up_bias, bias_grad),
    )


def solution(mesh):
    rows, columns, whole = P("dp", None), P(None, "dp"), P()
    return jax.shard_map(
        body,
        mesh=mesh,
        in_specs=(rows, rows, P("dp")) + (columns,) * 4 + (whole,) * 2 + (columns,) * 4,
        out_specs=(rows, rows) + (columns,) * 4 + (whole,) * 2 + (columns,) * 8 + (whole,) * 2,
        check_vma=False,
    )
```

time: 450 us -> 332 us (0.74)
  Pallas kernels: 240 us -> 138 us
  starting transfers between devices: 26.4 us -> 78.9 us
  waiting for transfers between devices: 106 us -> 68.1 us
  local copies, waits for them, and re-layouts: 35.4 us -> 7.63 us
    pallas_call x8 -> x13, Pallas kernels: 240 us -> 138 us  [the longest x7 44.2 us: call(): pl.pallas_call(kernel, in_specs=[smem] * scalars + [vmem] * (len(args) -...]
    all_to_all x5, waiting for transfers between devices: 105 us -> 66.1 us  [exchange(): return lax.all_to_all(x, 'dp', 0, 0, axis_index_groups=planes, tiled=True)]
    ppermute x6 -> x8, starting transfers between devices: 0.72 us -> 37.5 us  [swap(): return lax.ppermute(x, 'dp', pairs)]
    unnamed x68 -> x40, local copies, waits for them, and re-layouts: 29 us -> 3.56 us
    all_to_all x5, starting transfers between devices: 25.7 us -> 41.4 us  [exchange(): return lax.all_to_all(x, 'dp', 0, 0, axis_index_groups=planes, tiled=True)]
  transfers between devices with their start and end apart: 11 -> 13, of which waited for: 6 -> 5; matrix products, arithmetic and copies ran while one was open for 7% -> 3% of each run, Pallas kernels for 17% -> 30%
where the time goes in v2:
time: 332 us; the launch traced here: 326 us
  Pallas kernels  138 us (42%)
  starting transfers between devices  78.9 us (24%)
  waiting for transfers between devices  68.1 us (21%)
  blocking collectives  23 us (7%)
  local copies, waits for them, and re-layouts  7.63 us (2%)
  other arithmetic  7.51 us (2%)
    all_to_all x5, waiting for transfers between devices, exchange(): return lax.all_to_all(x, 'dp', 0, 0, axis_index_groups=planes, tiled=True)  66.1 us
    pallas_call x7, Pallas kernels, call(): pl.pallas_call(kernel, in_specs=[smem] * scalars + [vmem] * (len(args) -...  44.2 us
    all_to_all x5, starting transfers between devices, exchange(): return lax.all_to_all(x, 'dp', 0, 0, axis_index_groups=planes, tiled=True)  41.4 us
    pallas_call x3, Pallas kernels, back_call(): pl.pallas_call(functools.partial(back_kernel, start, last), grid_spec=plt...  38.9 us
    ppermute x8, starting transfers between devices, swap(): return lax.ppermute(x, 'dp', pairs)  37.5 us
    pallas_call x1, Pallas kernels, mlp_call(): pl.pallas_call(mlp_kernel, grid_spec=pltpu.PrefetchScalarGridSpec(num_sca...  34 us
    all_to_all x1, blocking collectives, exchange(): return lax.all_to_all(x, 'dp', 0, 0, axis_index_groups=planes, tiled=True)  23 us
    pallas_call x2, Pallas kernels, attend_call(): pl.pallas_call(functools.partial(attend_kernel, start), grid_spec=pltpu.P...  21 us
  transfers between devices with their start and end apart: 13, of which 5 were waited for; matrix products, arithmetic and copies ran while one was open for 3% of the time, Pallas kernels for 30%

profile of v2, /device:TPU:0, one launch (start us, length us, event | category | flops | bytes accessed | tf_op | source)
XLA Modules:
  0.0 326.0 jit_solution(14510122417991162986)
XLA Ops:
  0.7 2.3 prep.1
  2.9 23.0 %all_to_all.30.refs_0_ = bf16[16,36,384]{2,1,0:T(8,128)(2,1)S(1)} all-to-all(bf16[16,36,384]{2,1,0:T(8,128)(2,1)} %get-tuple-element.64), channel_id=1, replica_groups={{0,2,4,6,8,10,12,14,16,18,20,22,24,26,28,30},{1,3,5,7,9,11,13,15,17,19,..., dimensions={0} | all-to-all | bytes 884736 | tf_op jit(solution)/shard_map/all_to_all | solution.py:754
  25.9 3.8 %all-to-all-start.1 = ((bf16[16,112,384]{2,1,0:T(8,128)(2,1)}), bf16[16,112,384]{2,1,0:T(8,128)(2,1)S(1)}, u32[]{:S(2)}, u32[]{:S(2)}) async-start(bf16[16,112,384]{2,1,0:T(8,128)(2,1)} %get-tuple-element.71), calls=%async_computation.1 | async-start | bytes 2752512 | tf_op jit(solution)/shard_map/all_to_all | solution.py:754
  31.0 1.6 broadcast_in_dim.4.vec_ref
  32.6 15.9 %attend.2 = (bf16[8,1152,512]{2,1,0:T(8,128)(2,1)}, bf16[8,3072,256]{2,1,0:T(8,128)(2,1)}, bf16[8,384,512]{2,1,0:T(8,128)(2,1)}, bf16[1152,384]{1,0:T(8,128)(2,1)}) custom-call(s32[2]{0:T(128)} %pad_add_fusion.info, bf16[4096,384]{1,0:T(8,128)(2,1)} %x_ref.11, f32[8,384,128]{2,1,0:T(8,128)} %broadcast_in_dim.4.vec_ref, bf16[16,36,384]{2,1,0:T(8,128)(2,1)} %copy-done.10, ...), custom_call_target="tpu_custom_call" | custom-call | flops 24000000000 | bytes 18000000 | tf_op jit(solution)/shard_map/attend/pallas_call | solution.py:573
  48.5 12.1 %all-to-all-done.1.own_ref = bf16[16,112,384]{2,1,0:T(8,128)(2,1)S(1)} async-done(((bf16[16,112,384]{2,1,0:T(8,128)(2,1)}), bf16[16,112,384]{2,1,0:T(8,128)(2,1)S(1)}, u32[]{:S(2)}, u32[]{:S(2)}) %all-to-all-start.1) | async-done | bytes 1376288 | tf_op jit(solution)/shard_map/all_to_all | solution.py:754
  60.9 5.2 %attend.3 = (bf16[8,1152,512]{2,1,0:T(8,128)(2,1)}, bf16[8,3072,256]{2,1,0:T(8,128)(2,1)}, bf16[8,384,512]{2,1,0:T(8,128)(2,1)}) custom-call(s32[2]{0:T(128)} %pad_add_fusion.info, bf16[4096,384]{1,0:T(8,128)(2,1)} %x_ref.11, f32[8,384,128]{2,1,0:T(8,128)} %broadcast_in_dim.4.vec_ref, ...), custom_call_target="tpu_custom_call", output_to_operand_aliasing={{0}: (4, {}), {1}: (5, {}), {2}: (6, {})} | custom-call | flops 8000000000 | bytes 6000000 | tf_op jit(solution)/shard_map/attend/pallas_call | solution.py:573
  66.1 1.4 broadcast_in_dim.5.ub_ref
  67.4 34.0 %mlp.1 = (f32[4096,384]{1,0:T(8,128)}, f32[8,384,512]{2,1,0:T(8,128)}, f32[384,384]{1,0:T(8,128)}, bf16[384,384]{1,0:T(8,128)(2,1)}, f32[16,104,384]{2,1,0:T(8,128)}, /*index=5*/bf16[16,104,384]{2,1,0:T(8,128)(2,1)}) custom-call(s32[2]{0:T(128)} %pad_add_fusion.info, bf16[4096,384]{1,0:T(8,128)(2,1)} %x_ref.11, bf16[4096,384]{1,0:T(8,128)(2,1)} %cot_ref.1, ...), custom_call_target="tpu_custom_call" | custom-call | flops 80000000000 | bytes 32000000 | tf_op jit(solution)/shard_map/mlp/pallas_call | solution.py:608
  101.5 25.7 %collective-permute-start.3 = (bf16[16,104,384]{2,1,0:T(8,128)(2,1)}, bf16[16,104,384]{2,1,0:T(8,128)(2,1)S(1)}, u32[]{:S(2)}, u32[]{:S(2)}) collective-permute-start(bf16[16,104,384]{2,1,0:T(8,128)(2,1)} %get-tuple-element.91), channel_id=1, source_target_pairs={{0,1},{1,0},{2,3},{3,2},{4,5},{5,4},{6,7},{7,6},{8,9},{9,8},{10,11... | collective-permute-start | bytes 3833864 | tf_op jit(solution)/shard_map/ppermute | solution.py:757
  127.2 10.4 %back.3 = (f32[4096,384]{1,0:T(8,128)}, f32[1152,384]{1,0:T(8,128)}, f32[4,384,128]{2,1,0:T(8,128)}) custom-call(s32[2]{0:T(128)} %pad_add_fusion.info, bf16[4096,384]{1,0:T(8,128)(2,1)} %x_ref.11, bf16[8,1152,512]{2,1,0:T(8,128)(2,1)} %get-tuple-element.74.qkv_ref, bf16[8,3072,256]{2,1,0:T(8,128)(2,1)} %get-tuple-element.75.att_ref, ...), custom_call_target="tpu_custom_call" | custom-call | flops 7000000000 | bytes 5000000 | tf_op jit(solution)/shard_map/back/pallas_call | solution.py:684
  137.6 1.3 add_convert_fusion
  138.9 15.5 %all-to-all-start.3 = ((bf16[16,104,384]{2,1,0:T(8,128)(2,1)}), bf16[16,104,384]{2,1,0:T(8,128)(2,1)S(1)}, u32[]{:S(2)}, u32[]{:S(2)}) async-start(bf16[16,104,384]{2,1,0:T(8,128)(2,1)} %add_convert_fusion), calls=%async_computation.3 | async-start | bytes 2555904 | tf_op jit(solution)/shard_map/all_to_all | solution.py:754
  154.5 21.1 %back.4 = (f32[4096,384]{1,0:T(8,128)}, f32[1152,384]{1,0:T(8,128)}, f32[4,384,128]{2,1,0:T(8,128)}) custom-call(s32[2]{0:T(128)} %pad_add_fusion.info, bf16[4096,384]{1,0:T(8,128)(2,1)} %x_ref.11, bf16[8,1152,512]{2,1,0:T(8,128)(2,1)} %get-tuple-element.74.qkv_ref, ...), custom_call_target="tpu_custom_call", output_to_operand_aliasing={{0}: (9, {})} | custom-call | flops 41999998976 | bytes 30000000 | tf_op jit(solution)/shard_map/back/pallas_call | solution.py:684
  175.5 7.5 %back.5 = (f32[4096,384]{1,0:T(8,128)}, f32[16,160,128]{2,1,0:T(8,128)}, bf16[16,160,128]{2,1,0:T(8,128)(2,1)}) custom-call(s32[2]{0:T(128)} %pad_add_fusion.info, bf16[4096,384]{1,0:T(8,128)(2,1)} %x_ref.11, bf16[8,1152,512]{2,1,0:T(8,128)(2,1)} %get-tuple-element.74.qkv_ref, ...), custom_call_target="tpu_custom_call", output_to_operand_aliasing={{0}: (9, {})} | custom-call | flops 7000000000 | bytes 5000000 | tf_op jit(solution)/shard_map/back/pallas_call | solution.py:684
  183.0 11.2 %collective-permute-start.2 = (bf16[16,160,128]{2,1,0:T(8,128)(2,1)}, bf16[16,160,128]{2,1,0:T(8,128)(2,1)S(1)}, u32[]{:S(2)}, u32[]{:S(2)}) collective-permute-start(bf16[16,160,128]{2,1,0:T(8,128)(2,1)} %get-tuple-element.87), channel_id=1, source_target_pairs={{0,1},{1,0},{2,3},{3,2},{4,5},{5,4},{6,7},{7,6},{8,9},{9,8},{10,11... | collective-permute-start | bytes 1966088 | tf_op jit(solution)/shard_map/ppermute | solution.py:757
  194.2 1.9 collective-permute-done.2
  196.1 2.3 add_convert_fusion.1
  198.4 11.2 %all-to-all-start.2 = ((bf16[16,160,128]{2,1,0:T(8,128)(2,1)}), bf16[16,160,128]{2,1,0:T(8,128)(2,1)S(1)}, u32[]{:S(2)}, u32[]{:S(2)}) async-start(bf16[16,160,128]{2,1,0:T(8,128)(2,1)} %add_convert_fusion.1), calls=%async_computation.2 | async-start | bytes 1310720 | tf_op jit(solution)/shard_map/all_to_all | solution.py:754
  209.6 2.7 mlp_state.1
  212.3 15.0 %all-to-all-done.2.got_ref = bf16[16,160,128]{2,1,0:T(8,128)(2,1)S(1)} async-done(((bf16[16,160,128]{2,1,0:T(8,128)(2,1)}), bf16[16,160,128]{2,1,0:T(8,128)(2,1)S(1)}, u32[]{:S(2)}, u32[]{:S(2)}) %all-to-all-start.2) | async-done | bytes 655392 | tf_op jit(solution)/shard_map/all_to_all | solution.py:754
  227.3 4.5 %all-to-all-start.5 = ((bf16[16,96,384]{2,1,0:T(8,128)(2,1)}), bf16[16,96,384]{2,1,0:T(8,128)(2,1)S(1)}, u32[]{:S(2)}, u32[]{:S(2)}) async-start(bf16[16,96,384]{2,1,0:T(8,128)(2,1)} %get-tuple-element.102), calls=%async_computation.5 | async-start | bytes 2359296 | tf_op jit(solution)/shard_map/all_to_all | solution.py:754
  231.8 2.1 att_state.1
  233.9 23.9 %all-to-all-done.5.own_ref = bf16[16,96,384]{2,1,0:T(8,128)(2,1)S(1)} async-done(((bf16[16,96,384]{2,1,0:T(8,128)(2,1)}), bf16[16,96,384]{2,1,0:T(8,128)(2,1)S(1)}, u32[]{:S(2)}, u32[]{:S(2)}) %all-to-all-start.5) | async-done | bytes 1179680 | tf_op jit(solution)/shard_map/all_to_all | solution.py:754
  257.8 6.4 %all-to-all-start.4 = ((bf16[16,48,384]{2,1,0:T(8,128)(2,1)}), bf16[16,48,384]{2,1,0:T(8,128)(2,1)S(1)}, u32[]{:S(2)}, u32[]{:S(2)}) async-start(bf16[16,48,384]{2,1,0:T(8,128)(2,1)} %get-tuple-element.98), calls=%async_computation.4 | async-start | bytes 1179648 | tf_op jit(solution)/shard_map/all_to_all | solution.py:754
  264.3 15.2 %all-to-all-done.4.own_ref = bf16[16,48,384]{2,1,0:T(8,128)(2,1)S(1)} async-done(((bf16[16,48,384]{2,1,0:T(8,128)(2,1)}), bf16[16,48,384]{2,1,0:T(8,128)(2,1)S(1)}, u32[]{:S(2)}, u32[]{:S(2)}) %all-to-all-start.4) | async-done | bytes 589856 | tf_op jit(solution)/shard_map/all_to_all | solution.py:754
  281.4 0.8 copy-done.9
  282.3 15.4 %att_newton.1.mine_ref = f32[392,384]{1,0:T(8,128)} custom-call(s32[2]{0:T(128)} %pad_add_fusion.1.info, bf16[16,48,384]{2,1,0:T(8,128)(2,1)} %copy-done.4, bf16[16,48,384]{2,1,0:T(8,128)(2,1)} %copy-done.9), custom_call_target="tpu_custom_call" | custom-call | tf_op jit(solution)/shard_map/att_newton/pallas_call | solution.py:541
  299.8 1.0 copy-done.6
  300.8 16.5 %mlp_newton.1.mine_ref = f32[392,384]{1,0:T(8,128)} custom-call(s32[2]{0:T(128)} %pad_add_fusion.2.info, bf16[16,96,384]{2,1,0:T(8,128)(2,1)} %copy-done.1, bf16[16,96,384]{2,1,0:T(8,128)(2,1)} %copy-done.6), custom_call_target="tpu_custom_call" | custom-call | tf_op jit(solution)/shard_map/mlp_newton/pallas_call | solution.py:541
  319.5 2.6 att_update.1
  322.9 2.7 mlp_update.1
  (69 shorter events, 7.3 us)
Async XLA Ops:
  2.9 28.1 %copy-start.11 = (f32[8,384]{1,0:T(8,128)S(1)}, f32[8,384]{1,0:T(8,128)}, u32[]{:S(2)}) copy-start(f32[8,384]{1,0:T(8,128)} %param.20) | copy-start | bytes 36868
  25.9 6.7 %copy-start.10 = (bf16[16,36,384]{2,1,0:T(8,128)(2,1)}, bf16[16,36,384]{2,1,0:T(8,128)(2,1)S(1)}, u32[]{:S(2)}) copy-start(bf16[16,36,384]{2,1,0:T(8,128)(2,1)S(1)} %all_to_all.30.refs_0_) | copy-start | bytes 1327108
  25.9 5.1 %collective-permute-start = (bf16[16,36,384]{2,1,0:T(8,128)(2,1)S(1)}, bf16[16,36,384]{2,1,0:T(8,128)(2,1)S(1)}, u32[]{:S(2)}, u32[]{:S(2)}) collective-permute-start(bf16[16,36,384]{2,1,0:T(8,128)(2,1)S(1)} %all_to_all.30.refs_0_), channel_id=1, source_target_pairs={{0,1},{1,0},{2,3},{3,2},{4,5},{5,4},{6,7},{7,6},{8,9},{9,8},{10,11... | collective-permute-start | bytes 1327112 | tf_op jit(solution)/shard_map/ppermute | solution.py:757
  25.9 34.8 %all-to-all-start.1 = ((bf16[16,112,384]{2,1,0:T(8,128)(2,1)}), bf16[16,112,384]{2,1,0:T(8,128)(2,1)S(1)}, u32[]{:S(2)}, u32[]{:S(2)}) async-start(bf16[16,112,384]{2,1,0:T(8,128)(2,1)} %get-tuple-element.71), calls=%async_computation.1 | async-start | bytes 2752512 | tf_op jit(solution)/shard_map/all_to_all | solution.py:754
  31.0 1.6 copy-start.19
  32.6 28.0 %copy-start.14 = (f32[1536]{0:T(1024)S(1)}, f32[1536]{0:T(1024)}, u32[]{:S(2)}) copy-start(f32[1536]{0:T(1024)} %param.21) | copy-start | bytes 18436
  60.7 5.4 %copy-start.5 = (bf16[16,112,384]{2,1,0:T(8,128)(2,1)}, bf16[16,112,384]{2,1,0:T(8,128)(2,1)S(1)}, u32[]{:S(2)}) copy-start(bf16[16,112,384]{2,1,0:T(8,128)(2,1)S(1)} %all-to-all-done.1.own_ref) | copy-start | bytes 4128772
  60.7 5.4 %collective-permute-start.1 = (bf16[16,112,384]{2,1,0:T(8,128)(2,1)S(1)}, bf16[16,112,384]{2,1,0:T(8,128)(2,1)S(1)}, u32[]{:S(2)}, u32[]{:S(2)}) collective-permute-start(bf16[16,112,384]{2,1,0:T(8,128)(2,1)S(1)} %all-to-all-done.1.own_ref), channel_id=1, source_target_pairs={{0,1},{1,0},{2,3},{3,2},{4,5},{5,4},{6,7},{7,6},{8,9},{9,8},{10,11... | collective-permute-start | bytes 4128776 | tf_op jit(solution)/shard_map/ppermute | solution.py:757
  66.0 1.4 copy-start.18
  101.5 36.2 %collective-permute-start.3 = (bf16[16,104,384]{2,1,0:T(8,128)(2,1)}, bf16[16,104,384]{2,1,0:T(8,128)(2,1)S(1)}, u32[]{:S(2)}, u32[]{:S(2)}) collective-permute-start(bf16[16,104,384]{2,1,0:T(8,128)(2,1)} %get-tuple-element.91), channel_id=1, source_target_pairs={{0,1},{1,0},{2,3},{3,2},{4,5},{5,4},{6,7},{7,6},{8,9},{9,8},{10,11... | collective-permute-start | bytes 3833864 | tf_op jit(solution)/shard_map/ppermute | solution.py:757
  127.2 10.4 %copy-start.3 = (f32[16,104,384]{2,1,0:T(8,128)S(1)}, f32[16,104,384]{2,1,0:T(8,128)}, u32[]{:S(2)}) copy-start(f32[16,104,384]{2,1,0:T(8,128)} %get-tuple-element.90) | copy-start | bytes 7667716
  138.9 59.5 %all-to-all-start.3 = ((bf16[16,104,384]{2,1,0:T(8,128)(2,1)}), bf16[16,104,384]{2,1,0:T(8,128)(2,1)S(1)}, u32[]{:S(2)}, u32[]{:S(2)}) async-start(bf16[16,104,384]{2,1,0:T(8,128)(2,1)} %add_convert_fusion), calls=%async_computation.3 | async-start | bytes 2555904 | tf_op jit(solution)/shard_map/all_to_all | solution.py:754
  183.0 13.1 %collective-permute-start.2 = (bf16[16,160,128]{2,1,0:T(8,128)(2,1)}, bf16[16,160,128]{2,1,0:T(8,128)(2,1)S(1)}, u32[]{:S(2)}, u32[]{:S(2)}) collective-permute-start(bf16[16,160,128]{2,1,0:T(8,128)(2,1)} %get-tuple-element.87), channel_id=1, source_target_pairs={{0,1},{1,0},{2,3},{3,2},{4,5},{5,4},{6,7},{7,6},{8,9},{9,8},{10,11... | collective-permute-start | bytes 1966088 | tf_op jit(solution)/shard_map/ppermute | solution.py:757
  198.4 11.2 %copy-start = (bf16[16,104,384]{2,1,0:T(8,128)(2,1)}, bf16[16,104,384]{2,1,0:T(8,128)(2,1)S(1)}, u32[]{:S(2)}) copy-start(bf16[16,104,384]{2,1,0:T(8,128)(2,1)S(1)} %all-to-all-done.3.got_ref) | copy-start | bytes 3833860
  198.4 28.8 %all-to-all-start.2 = ((bf16[16,160,128]{2,1,0:T(8,128)(2,1)}), bf16[16,160,128]{2,1,0:T(8,128)(2,1)S(1)}, u32[]{:S(2)}, u32[]{:S(2)}) async-start(bf16[16,160,128]{2,1,0:T(8,128)(2,1)} %add_convert_fusion.1), calls=%async_computation.2 | async-start | bytes 1310720 | tf_op jit(solution)/shard_map/all_to_all | solution.py:754
  227.3 4.5 %copy-start.2 = (bf16[16,160,128]{2,1,0:T(8,128)(2,1)}, bf16[16,160,128]{2,1,0:T(8,128)(2,1)S(1)}, u32[]{:S(2)}) copy-start(bf16[16,160,128]{2,1,0:T(8,128)(2,1)S(1)} %all-to-all-done.2.got_ref) | copy-start | bytes 1966084
  227.3 30.5 %all-to-all-start.5 = ((bf16[16,96,384]{2,1,0:T(8,128)(2,1)}), bf16[16,96,384]{2,1,0:T(8,128)(2,1)S(1)}, u32[]{:S(2)}, u32[]{:S(2)}) async-start(bf16[16,96,384]{2,1,0:T(8,128)(2,1)} %get-tuple-element.102), calls=%async_computation.5 | async-start | bytes 2359296 | tf_op jit(solution)/shard_map/all_to_all | solution.py:754
  257.8 42.0 %copy-start.1 = (bf16[16,96,384]{2,1,0:T(8,128)(2,1)}, bf16[16,96,384]{2,1,0:T(8,128)(2,1)S(1)}, u32[]{:S(2)}) copy-start(bf16[16,96,384]{2,1,0:T(8,128)(2,1)S(1)} %all-to-all-done.5.own_ref) | copy-start | bytes 3538948
  257.8 21.7 %all-to-all-start.4 = ((bf16[16,48,384]{2,1,0:T(8,128)(2,1)}), bf16[16,48,384]{2,1,0:T(8,128)(2,1)S(1)}, u32[]{:S(2)}, u32[]{:S(2)}) async-start(bf16[16,48,384]{2,1,0:T(8,128)(2,1)} %get-tuple-element.98), calls=%async_computation.4 | async-start | bytes 1179648 | tf_op jit(solution)/shard_map/all_to_all | solution.py:754
  264.2 35.6 %collective-permute-start.6 = (bf16[16,96,384]{2,1,0:T(8,128)(2,1)S(1)}, bf16[16,96,384]{2,1,0:T(8,128)(2,1)S(1)}, u32[]{:S(2)}, u32[]{:S(2)}) collective-permute-start(bf16[16,96,384]{2,1,0:T(8,128)(2,1)S(1)} %all-to-all-done.5.own_ref), channel_id=1, source_target_pairs={{0,1},{1,0},{2,3},{3,2},{4,5},{5,4},{6,7},{7,6},{8,9},{9,8},{10,11... | collective-permute-start | bytes 3538952 | tf_op jit(solution)/shard_map/ppermute | solution.py:757
  279.4 2.0 copy-start.4
  279.4 2.0 collective-permute-start.4
  281.4 16.7 %copy-start.17 = (f32[8,384]{1,0:T(8,128)S(1)}, f32[8,384]{1,0:T(8,128)}, u32[]{:S(2)}) copy-start(f32[8,384]{1,0:T(8,128)} %get-tuple-element.97) | copy-start | bytes 36868
  281.4 0.8 copy-start.9
  297.7 19.7 %copy-start.15 = (f32[1536]{0:T(1024)S(1)}, f32[1536]{0:T(1024)}, u32[]{:S(2)}) copy-start(f32[1536]{0:T(1024)} %param.21) | copy-start | bytes 18436
  297.7 20.3 %copy-start.12 = (f32[8,384]{1,0:T(8,128)S(1)}, f32[8,384]{1,0:T(8,128)}, u32[]{:S(2)}) copy-start(f32[8,384]{1,0:T(8,128)} %param.20) | copy-start | bytes 36868
  297.7 21.0 %collective-permute-start.5 = (f32[392,384]{1,0:T(8,128)}, f32[392,384]{1,0:T(8,128)S(1)}, u32[]{:S(2)}, u32[]{:S(2)}) collective-permute-start(f32[392,384]{1,0:T(8,128)} %att_newton.1.mine_ref), channel_id=1, source_target_pairs={{0,1},{1,0},{2,3},{3,2},{4,5},{5,4},{6,7},{7,6},{8,9},{9,8},{10,11... | collective-permute-start | bytes 1806344 | tf_op jit(solution)/shard_map/ppermute | solution.py:757
  298.3 23.8 %copy-start.16 = (f32[1536]{0:T(1024)}, f32[1536]{0:T(1024)S(1)}, u32[]{:S(2)}) copy-start(f32[1536]{0:T(1024)S(1)} %reshape.79) | copy-start | bytes 18436
  299.8 25.8 %copy-start.13 = (f32[8,384]{1,0:T(8,128)}, f32[8,384]{1,0:T(8,128)S(1)}, u32[]{:S(2)}) copy-start(f32[8,384]{1,0:T(8,128)S(1)} %get-tuple-element.111) | copy-start | bytes 36868
  299.8 1.0 copy-start.6
  317.3 4.8 %collective-permute-start.7 = (f32[392,384]{1,0:T(8,128)}, f32[392,384]{1,0:T(8,128)S(1)}, u32[]{:S(2)}, u32[]{:S(2)}) collective-permute-start(f32[392,384]{1,0:T(8,128)} %mlp_newton.1.mine_ref), channel_id=1, source_target_pairs={{0,1},{1,0},{2,3},{3,2},{4,5},{5,4},{6,7},{7,6},{8,9},{9,8},{10,11... | collective-permute-start | bytes 1806344 | tf_op jit(solution)/shard_map/ppermute | solution.py:757
  322.1 0.8 copy-start.8
  (1 other events, 0.8 us)

commit v3 on v2

--- a/solution.py
+++ b/solution.py
@@ -88,12 +88,20 @@
         second_ref[index, second.shape[0] :, :] = jnp.zeros_like(second_ref[index, second.shape[0] :, :])
 
 
-def attend_kernel(start, info, x_ref, vec_ref, *refs):
+def normal_kernel(info, x_ref, vec_ref, z_ref):
+    @pl.when(pl.program_id(0) * GROUP < info[0])
+    def _():
+        for c in range(z_ref.shape[1] // LANES):
+            normed, _ = norm_parts(x_ref[cols(c), :].astype(f32).T)
+            z_ref[:, cols(c)] = (normed * vec_ref[0] + vec_ref[1]).astype(bf16)
+
+
+def attend_kernel(start, info, z_ref, vec_ref, *refs):
     if start == 0:
-        own_ref, other_ref, qkv_ref, att_ref, out_ref, wq_ref, z_scr, qkv_scr, s_scr, p_scr, stage = refs
+        own_ref, other_ref, qkv_ref, att_ref, out_ref, wq_ref, qkv_scr, s_scr, p_scr, stage = refs
     else:
-        wq_ref, _, _, _, qkv_ref, att_ref, out_ref, z_scr, qkv_scr, s_scr, p_scr = refs
-    width, lanes = z_scr.shape
+        wq_ref, _, _, _, qkv_ref, att_ref, out_ref, qkv_scr, s_scr, p_scr = refs
+    width, lanes = z_ref.shape
     heads = width // HEAD_DIM
     group = start + pl.program_id(0)
 
@@ -109,13 +117,9 @@
 
     @pl.when(group * GROUP < info[0])
     def _():
-        for c in range(lanes // LANES):
-            chunk = x_ref[cols(c), :].astype(f32).T
-            normed, _ = norm_parts(chunk)
-            z_scr[:, cols(c)] = (normed * vec_ref[0] + vec_ref[1]).astype(bf16)
         for part in range(3):
             rows = slice(part * width, (part + 1) * width)
-            made = nn(wq_ref[rows, :], z_scr[...])
+            made = nn(wq_ref[rows, :], z_ref[...])
             for c in range(lanes // LANES):
                 piece = made[:, cols(c)]
                 if part == 0:
@@ -151,9 +155,9 @@
 
 def mlp_kernel(
     info, x_ref, cot_ref, att_ref, own_ref, other_ref, vec_ref, ub_ref,
-    out_ref, dh_ref, gp_ref, wpn_ref, keep_ref, send_ref,
-    wun_scr, wdn_scr, wp_scr, wu_scr, wd_scr, gu_scr, gd_scr, rows_scr, bias_scr,
-    h_scr, n_scr, z_scr, m_scr, act_scr, du_scr, dhb_scr, s_scr, stage, u_scr, d_scr,
+    h_ref, act_ref, dh_ref, gp_ref, wpn_ref, wdn_ref, keep_ref, send_ref,
+    wun_scr, wp_scr, wu_scr, wd_scr, gu_scr, gd_scr, rows_scr, bias_scr,
+    n_scr, z_scr, m_scr, act_scr, du_scr, dhb_scr, s_scr, stage, u_scr, d_scr,
 ):
     width, lanes = z_scr.shape
     ff = wu_scr.shape[0]
@@ -165,10 +169,16 @@
     @pl.when(step == 0)
     def _():
         gp_ref[...] = jnp.zeros_like(gp_ref)
-        gu_scr[...] = jnp.zeros_like(gu_scr)
-        gd_scr[...] = jnp.zeros_like(gd_scr)
         rows_scr[...] = jnp.zeros_like(rows_scr)
-        bias_scr[...] = jnp.zeros_like(bias_scr)
+
+        def clear(index, carry):
+            rows = pl.ds(pl.multiple_of(index * LANES, LANES), LANES)
+            gu_scr[rows, :] = jnp.zeros((LANES, width), f32)
+            gd_scr[rows, :] = jnp.zeros((LANES, width), f32)
+            bias_scr[rows, :] = jnp.zeros((LANES, LANES), f32)
+            return carry
+
+        lax.fori_loop(0, ff // LANES, clear, 0)
         count = width // (2 * half)
         for shard in range(2 * half):
             rows = shard_rows(info[1], shard, own_ref, other_ref, 2 * part, count)
@@ -187,14 +197,14 @@
                         at = (side * half + index) * part
                         stage[at : at + part, :] = ref[index, low : low + part, :].astype(f32)
                 wide_scr[...] = stage[...].astype(bf16)
-        for c in range(ff // block):
-            rows = slice(c * block, (c + 1) * block)
+
+        def turn(index, carry):
+            rows = pl.ds(pl.multiple_of(index * block, block), block)
             wun_scr[:, rows] = wu_scr[rows, :].T
-            wdn_scr[:, rows] = wd_scr[rows, :].T
-
-    @pl.when(step * GROUP >= info[0])
-    def _():
-        out_ref[...] = jnp.zeros_like(out_ref)
+            wdn_ref[:, rows] = wd_scr[rows, :].T
+            return carry
+
+        lax.fori_loop(0, ff // block, turn, 0)
 
     @pl.when(step * GROUP < info[0])
     def _():
@@ -202,7 +212,7 @@
         total7 = jnp.zeros((width, LANES), f32)
         for c in range(lanes // LANES):
             chunk = x_ref[cols(c), :].astype(f32).T + made[:, cols(c)] + vec_ref[4]
-            h_scr[:, cols(c)] = chunk
+            h_ref[:, cols(c)] = chunk
             normed, scale = norm_parts(chunk)
             n_scr[:, cols(c)] = normed
             s_scr[:, cols(c)] = scale
@@ -227,7 +237,9 @@
                     u = u_scr[c % 2, here, cols(k)] + ub_ref[rows, :]
                     v = u * (1.0 / math.sqrt(2.0))
                     cdf = 0.5 + 0.5 * lax.erf(v)
-                    act_scr[rows, cols(k)] = (u * cdf).astype(bf16)
+                    act = (u * cdf).astype(bf16)
+                    act_scr[rows, cols(k)] = act
+                    act_ref[rows, cols(k)] = act
                     slope = cdf + (v * (1.0 / math.sqrt(math.pi))) * jnp.exp(-(v * v))
                     du = d_scr[c % 2, here, cols(k)] * slope
                     du_scr[rows, cols(k)] = du.astype(bf16)
@@ -246,11 +258,6 @@
                 first(c + 1)
             second(c)
             third(c)
-        down = nn(wdn_scr[...], act_scr[...])
-        for c in range(lanes // LANES):
-            image = step * GROUP + c * LANES // SEQ
-            whole = down[:, cols(c)] + h_scr[:, cols(c)] + vec_ref[7]
-            out_ref[cols(c), :] = jnp.where(image < info[0], whole, 0.0).T
         dz = nn(wun_scr[...], du_scr[...])
         total4 = jnp.zeros((width, LANES), f32)
         total5 = jnp.zeros((width, LANES), f32)
@@ -297,18 +304,35 @@
                 send_ref[index] = stage[: send_ref.shape[1], :].astype(bf16)
 
 
-def back_kernel(start, last, info, x_ref, qkv_ref, att_ref, dh_ref, wpn_ref, wq_ref, gp_ref, vec_ref, *refs):
+def out_kernel(start, info, h_ref, act_ref, wdn_ref, vec_ref, *refs):
+    out_ref = refs[-1]
+    group = start + pl.program_id(0)
+
+    @pl.when(group * GROUP >= info[0])
+    def _():
+        out_ref[...] = jnp.zeros_like(out_ref)
+
+    @pl.when(group * GROUP < info[0])
+    def _():
+        down = nn(wdn_ref[...], act_ref[...])
+        for c in range(h_ref.shape[1] // LANES):
+            image = group * GROUP + c * LANES // SEQ
+            whole = down[:, cols(c)] + h_ref[:, cols(c)] + vec_ref[7]
+            out_ref[cols(c), :] = jnp.where(image < info[0], whole, 0.0).T
+
+
+def back_kernel(start, last, info, z_ref, qkv_ref, att_ref, dh_ref, wpn_ref, wq_ref, gp_ref, row_ref, *refs):
     if start:
-        _, gq_in, rows_in = refs[:3]
+        gq_in, rows_in, _ = refs[:3]
         refs = refs[3:]
     if last:
-        out_ref, keep_ref, send_ref, gq_ref, rows_ref, stage = refs[:6]
+        dqkv_ref, keep_ref, send_ref, gq_ref, rows_ref, stage = refs[:6]
         refs = refs[6:]
     else:
-        out_ref, gq_ref, rows_ref = refs[:3]
+        dqkv_ref, gq_ref, rows_ref = refs[:3]
         refs = refs[3:]
-    wqn_scr, n_scr, z_scr, s_scr, da_scr, dqkv_scr, up_scr, ds_scr = refs
-    width, lanes = z_scr.shape
+    da_scr, dqkv_scr, up_scr, ds_scr = refs
+    width, lanes = z_ref.shape
     heads = width // HEAD_DIM
     step = pl.program_id(0)
     group = start + step
@@ -321,13 +345,6 @@
         else:
             gq_ref[...] = gq_in[...]
             rows_ref[...] = rows_in[...]
-        for c in range(3):
-            rows = slice(c * width, (c + 1) * width)
-            wqn_scr[:, rows] = wq_ref[rows, :].T
-
-    @pl.when(group * GROUP >= info[0])
-    def _():
-        out_ref[...] = jnp.zeros_like(out_ref)
 
     @pl.when(group * GROUP < info[0])
     def _():
@@ -338,12 +355,6 @@
                 low = head * HEAD_DIM
                 values = qkv_ref[2 * width + low : 2 * width + low + HEAD_DIM, span]
                 up_scr[image * heads + head] = tn(values, da_scr[low : low + HEAD_DIM, span])
-        for c in range(lanes // LANES):
-            chunk = x_ref[cols(c), :].astype(f32).T
-            normed, scale = norm_parts(chunk)
-            n_scr[:, cols(c)] = normed
-            s_scr[:, cols(c)] = scale
-            z_scr[:, cols(c)] = (normed * vec_ref[0] + vec_ref[1]).astype(bf16)
         for image in range(lanes // SEQ):
             span = slice(image * SEQ, (image + 1) * SEQ)
             for head in range(heads):
@@ -362,26 +373,15 @@
                 dquery = nn(keys, dscore) * (1.0 / math.sqrt(HEAD_DIM))
                 dkey = nt(query, dscore)
                 dvalue = nt(da_scr[low:high, span], att_ref[base : base + SEQ, :])
-                dqkv_scr[low:high, span] = dquery.astype(bf16)
-                dqkv_scr[width + low : width + high, span] = dkey.astype(bf16)
-                dqkv_scr[2 * width + low : 2 * width + high, span] = dvalue.astype(bf16)
-                rows_ref[2, low:high, :] += dquery[:, :LANES] + dquery[:, LANES:]
-                rows_ref[3, low:high, :] += dvalue[:, :LANES] + dvalue[:, LANES:]
+                for part, value in enumerate((dquery, dkey, dvalue)):
+                    rows = slice(part * width + low, part * width + high)
+                    made = value.astype(bf16)
+                    dqkv_scr[rows, span] = made
+                    dqkv_ref[rows, span] = made
+                    rows_ref[part, low:high, :] += value[:, :LANES] + value[:, LANES:]
         for part in range(3):
             rows = slice(part * width, (part + 1) * width)
-            gq_ref[rows, :] += nt(dqkv_scr[rows, :], z_scr[...])
-        dz = nn(wqn_scr[...], dqkv_scr[...])
-        total0 = jnp.zeros((width, LANES), f32)
-        total1 = jnp.zeros((width, LANES), f32)
-        for c in range(lanes // LANES):
-            piece = dz[:, cols(c)]
-            normed = n_scr[:, cols(c)]
-            dx = norm_back(piece * vec_ref[0], normed, s_scr[:, cols(c)]) + dh_ref[:, cols(c)]
-            out_ref[cols(c), :] = dx.T
-            total0 += piece * normed
-            total1 += piece
-        rows_ref[0] += total0
-        rows_ref[1] += total1
+            gq_ref[rows, :] += nt(dqkv_scr[rows, :], z_ref[...])
 
     if not last:
         return
@@ -393,9 +393,16 @@
         sizes = (3 * width // count, width // count)
         rows = sum(sizes)
         stage[...] = jnp.zeros_like(stage)
-        vector = []
-        for index in range(4):
-            vector += lane_rows(rows_ref[index])
+        cross, plain = jnp.zeros((1, width), f32), jnp.zeros((1, width), f32)
+        for part in range(3):
+            rows_of = slice(part * width, (part + 1) * width)
+            weight = wq_ref[rows_of, :].astype(f32)
+            total = jnp.sum(rows_ref[part], axis=1, keepdims=True)
+            cross += jnp.sum(weight * gq_ref[rows_of, :], axis=0, keepdims=True)
+            plain += jnp.sum(weight * total, axis=0, keepdims=True)
+        cross = (cross - row_ref[1:2, :] * plain) / row_ref[0:1, :]
+        vector = [value[:, cols(c)] for value in (cross, plain) for c in range(blocks)]
+        vector += lane_rows(rows_ref[0]) + lane_rows(rows_ref[2])
         for index, row in enumerate(vector):
             stage[blocks * rows + index : blocks * rows + index + 1, :] = rounded(row)
         for shard in range(count):
@@ -414,13 +421,42 @@
                 send_ref[shard // 2] = stage[...].astype(bf16)
 
 
+def input_kernel(start, info, x_ref, dqkv_ref, dh_ref, wq_ref, vec_ref, *refs):
+    out_ref, wqn_scr, s_scr, n_scr = refs[-4:]
+    width, lanes = n_scr.shape
+    step = pl.program_id(0)
+    group = start + step
+
+    @pl.when(step == 0)
+    def _():
+        for c in range(3):
+            rows = slice(c * width, (c + 1) * width)
+            wqn_scr[:, rows] = wq_ref[rows, :].T
+
+    @pl.when(group * GROUP >= info[0])
+    def _():
+        out_ref[...] = jnp.zeros_like(out_ref)
+
+    @pl.when(group * GROUP < info[0])
+    def _():
+        dz = nn(wqn_scr[...], dqkv_ref[...])
+        for c in range(lanes // LANES):
+            normed, scale = norm_parts(x_ref[cols(c), :].astype(f32).T)
+            n_scr[:, cols(c)] = normed
+            s_scr[:, cols(c)] = scale
+        for c in range(lanes // LANES):
+            inner = dz[:, cols(c)] * vec_ref[0]
+            dx = norm_back(inner, n_scr[:, cols(c)], s_scr[:, cols(c)]) + dh_ref[:, cols(c)]
+            out_ref[cols(c), :] = dx.T
+
+
 def unpack_att(total, rows, width, vectors):
     blocks = width // LANES
     grad = jnp.concatenate([total[c * rows : (c + 1) * rows] for c in range(blocks)], axis=1)
     return grad, total[blocks * rows : blocks * rows + vectors]
 
 
-def state_kernel(got_ref, ma_ref, mb_ref, ga_ref, gb_ref, sa_ref, sb_ref, spread_ref, state_ref, vec_ref):
+def state_kernel(info, got_ref, ma_ref, mb_ref, ga_ref, gb_ref, sa_ref, sb_ref, spread_ref, state_ref, vec_ref):
     first, width = ma_ref.shape
     rows = first + mb_ref.shape[0]
     total = got_ref[0].astype(f32)
@@ -436,8 +472,14 @@
     sa_ref[...] = state[:first]
     sb_ref[...] = state[first:]
     state_ref[...] = state
-    for index in range(spread_ref.shape[0]):
-        spread_ref[index] = state.astype(bf16)
+    if got_ref.shape[2] == width:
+        ours = info[0] == 0
+        high, low = state[:first].astype(bf16), state[first:].astype(bf16)
+        spread_ref[0] = jnp.where(ours, high, low)
+        spread_ref[1] = jnp.where(ours, low, high)
+    else:
+        for index in range(spread_ref.shape[0]):
+            spread_ref[index] = state.astype(bf16)
 
 
 def store_parts(x, left_ref, right_ref):
@@ -452,19 +494,21 @@
 
 
 def newton_kernel(info, own_ref, other_ref, out_ref, whole_ref, gram_scr, poly_scr, pa, pb, sa, sb):
-    count, rows, width = own_ref.shape
-    first = info[1]
+    width = own_ref.shape[-1]
     eye = (
         lax.broadcasted_iota(jnp.int32, (width, width), 0)
         == lax.broadcasted_iota(jnp.int32, (width, width), 1)
     ).astype(f32)
     gram = jnp.zeros((width, width), f32)
-    place = lax.broadcasted_iota(jnp.int32, (rows, width), 0)
-    mine = (place < first) == (info[0] == 0)
     for ref in (own_ref, other_ref):
-        part = jnp.concatenate(
-            [jnp.where(mine, ref[index].astype(f32), 0.0) for index in range(count)], axis=0
-        ).astype(bf16)
+        if len(ref.shape) == 2:
+            part = ref[...]
+        else:
+            place = lax.broadcasted_iota(jnp.int32, ref.shape[1:], 0)
+            mine = (place < info[1]) == (info[0] == 0)
+            part = jnp.concatenate(
+                [jnp.where(mine, ref[index].astype(f32), 0.0) for index in range(ref.shape[0])], axis=0
+            ).astype(bf16)
         gram += tn(part, part)
     norm = lax.rsqrt(jnp.sum(gram * eye) + norm_eps)
     out_ref[width:, :] = jnp.full((8, width), norm, f32)
@@ -551,7 +595,7 @@
     return call
 
 
-def group_specs(width, start):
+def group_specs(width, ff, start):
     heads = width // HEAD_DIM
     lanes = GROUP * SEQ
     deep = lambda i, info: (start + i, 0, 0)
@@ -560,145 +604,26 @@
         pl.BlockSpec((None, 3 * width, lanes), deep),
         pl.BlockSpec((None, GROUP * heads * SEQ, SEQ), deep),
         pl.BlockSpec((None, width, lanes), deep),
+        pl.BlockSpec((None, ff, lanes), deep),
     )
 
 
-def attend_call(info, x, vec, start, stop, weights, before=()):
-    width = x.shape[1]
-    heads = width // HEAD_DIM
-    lanes = GROUP * SEQ
-    groups = x.shape[0] // lanes
-    tokens, qkv_spec, att_spec, deep_spec = group_specs(width, start)
-    fresh = start == 0
+def grid_call(kernel, info, start, stop, ins, outs, scratch, name, flops, before=()):
     return pl.pallas_call(
-        functools.partial(attend_kernel, start),
+        kernel,
         grid_spec=pltpu.PrefetchScalarGridSpec(
             num_scalar_prefetch=1,
             grid=(stop - start,),
-            in_specs=[tokens, fixed(vec.shape)] + [fixed(w.shape) for w in weights] + [ANY] * len(before),
-            out_specs=[qkv_spec, att_spec, deep_spec] + [fixed((3 * width, width))] * fresh,
-            scratch_shapes=[
-                pltpu.VMEM((width, lanes), bf16),
-                pltpu.VMEM((3 * width, lanes), bf16),
-                pltpu.VMEM((GROUP * heads, SEQ, SEQ), f32),
-                pltpu.VMEM((GROUP * heads, SEQ, SEQ), bf16),
-            ] + [pltpu.VMEM((3 * width, width), f32)] * fresh,
+            in_specs=[spec or fixed(array.shape) for spec, array in ins] + [ANY] * len(before),
+            out_specs=[spec or fixed(shape) for spec, shape, _ in outs],
+            scratch_shapes=[pltpu.VMEM(*one) for one in scratch],
         ),
-        out_shape=[
-            shape_of((groups, 3 * width, lanes), bf16),
-            shape_of((groups, GROUP * heads * SEQ, SEQ), bf16),
-            shape_of((groups, width, lanes), bf16),
-        ] + [shape_of((3 * width, width), bf16)] * fresh,
-        input_output_aliases={3 + len(weights) + i: i for i in range(len(before))},
+        out_shape=[shape_of(shape, dtype) for _, shape, dtype in outs],
+        input_output_aliases={1 + len(ins) + i: i for i in range(len(before))},
         compiler_params=params(),
-        cost_estimate=cost(4e9 * (stop - start), 3e6 * (stop - start)),
-        name="attend",
-    )(info, x, vec, *weights, *before)
-
-
-def mlp_call(info, x, cot, attn, own, other, vec, ub):
-    width = x.shape[1]
-    ff = ub.shape[0]
-    half = own.shape[0]
-    lanes = GROUP * SEQ
-    groups = x.shape[0] // lanes
-    block = 256
-    tokens, _, _, deep_spec = group_specs(width, 0)
-    rows = 2 * (ff // (2 * half)) + 4 + ff // width
-    return pl.pallas_call(
-        mlp_kernel,
-        grid_spec=pltpu.PrefetchScalarGridSpec(
-            num_scalar_prefetch=1,
-            grid=(groups,),
-            in_specs=[
-                tokens, tokens, deep_spec,
-                fixed(own.shape), fixed(own.shape), fixed(vec.shape), fixed(ub.shape),
-            ],
-            out_specs=[
-                tokens, deep_spec, fixed((width, width)), fixed((width, width)),
-                fixed((half, rows, width)), fixed((half, rows, width)),
-            ],
-            scratch_shapes=[
-                pltpu.VMEM((width, ff), bf16),
-                pltpu.VMEM((width, ff), bf16),
-                pltpu.VMEM((width, width), bf16),
-                pltpu.VMEM((ff, width), bf16),
-                pltpu.VMEM((ff, width), bf16),
-                pltpu.VMEM((ff, width), f32),
-                pltpu.VMEM((ff, width), f32),
-                pltpu.VMEM((4, width, LANES), f32),
-                pltpu.VMEM((ff, LANES), f32),
-                pltpu.VMEM((width, lanes), f32),
-                pltpu.VMEM((width, lanes), f32),
-                pltpu.VMEM((width, lanes), bf16),
-                pltpu.VMEM((width, lanes), bf16),
-                pltpu.VMEM((ff, lanes), bf16),
-                pltpu.VMEM((ff, lanes), bf16),
-                pltpu.VMEM((width, lanes), bf16),
-                pltpu.VMEM((1, lanes), f32),
-                pltpu.VMEM((ff, width), f32),
-                pltpu.VMEM((2, block, lanes), f32),
-                pltpu.VMEM((2, block, lanes), f32),
-            ],
-        ),
-        out_shape=[
-            shape_of(x.shape, f32),
-            shape_of((groups, width, lanes), f32),
-            shape_of((width, width), f32),
-            shape_of((width, width), bf16),
-            shape_of((half, rows, width), f32),
-            shape_of((half, rows, width), bf16),
-        ],
-        compiler_params=params(),
-        cost_estimate=cost(10e9 * groups, 4e6 * groups),
-        name="mlp",
-    )(info, x, cot, attn, own, other, vec, ub)
-
-
-def back_call(info, x, qkv, att, dh, wpn, wq, gp, vec, half, start, stop, before=()):
-    width = x.shape[1]
-    heads = width // HEAD_DIM
-    lanes = GROUP * SEQ
-    groups = x.shape[0] // lanes
-    tokens, qkv_spec, att_spec, deep_spec = group_specs(width, start)
-    blocks = width // LANES
-    rows = -(-(blocks * (4 * width // (2 * half)) + 4 * blocks) // 16) * 16
-    last = stop == groups
-    sums = [(3 * width, width), (4, width, LANES)]
-    shards = (half, rows, LANES)
-    scratch = [
-        pltpu.VMEM((width, 3 * width), bf16),
-        pltpu.VMEM((width, lanes), f32),
-        pltpu.VMEM((width, lanes), bf16),
-        pltpu.VMEM((1, lanes), f32),
-        pltpu.VMEM((width, lanes), bf16),
-        pltpu.VMEM((3 * width, lanes), bf16),
-        pltpu.VMEM((GROUP * heads, SEQ, SEQ), f32),
-        pltpu.VMEM((GROUP * heads, SEQ, SEQ), bf16),
-    ]
-    if last:
-        outs = [(shards, f32), (shards, bf16)]
-        scratch = [pltpu.VMEM(shape, f32) for shape in sums + [(rows, LANES)]] + scratch
-    else:
-        outs = [(shape, f32) for shape in sums]
-    return pl.pallas_call(
-        functools.partial(back_kernel, start, last),
-        grid_spec=pltpu.PrefetchScalarGridSpec(
-            num_scalar_prefetch=1,
-            grid=(stop - start,),
-            in_specs=[
-                tokens, qkv_spec, att_spec, deep_spec,
-                fixed(wpn.shape), fixed(wq.shape), fixed(gp.shape), fixed(vec.shape),
-            ] + ([ANY] + [fixed(shape) for shape in sums] if before else []),
-            out_specs=[tokens] + [fixed(shape) for shape, _ in outs],
-            scratch_shapes=scratch,
-        ),
-        out_shape=[shape_of(x.shape, f32)] + [shape_of(*out) for out in outs],
-        input_output_aliases={9: 0} if before else {},
-        compiler_params=params(),
-        cost_estimate=cost(7e9 * (stop - start), 5e6 * (stop - start)),
-        name="back",
-    )(info, x, qkv, att, dh, wpn, wq, gp, vec, *before)
+        cost_estimate=cost(flops * (stop - start), 4e6 * (stop - start)),
+        name=name,
+    )(info, *[array for _, array in ins], *before)
 
 
 def order_ff(up_bias, par, half):
@@ -764,42 +689,141 @@
         [((half, cq, width), bf16), ((half, -(-(cu + cd + cp) // 16) * 16, width), bf16)],
         "prep",
     )(wq_s, wp_s, wu_s, wd_s)
+    lanes = GROUP * SEQ
+    heads = width // HEAD_DIM
+    tokens, qkv_spec, att_spec, deep_spec, ff_spec = group_specs(width, ff, 0)
+    wide = (groups, width, lanes)
+    z1 = grid_call(
+        normal_kernel, info, 0, groups, [(tokens, block_in), (None, vec)], [(deep_spec, wide, bf16)], [],
+        "normal", 1e9,
+    )[0]
     wq_own = exchange(first)
     wq_other = swap(wq_own)
     rest_own = exchange(after(second, wq_own))
 
+    def attend(start, stop, weights, before=()):
+        _, qkv_at, att_at, deep_at, _ = group_specs(width, ff, start)
+        fresh = start == 0
+        return grid_call(
+            functools.partial(attend_kernel, start), info, start, stop,
+            [(deep_at, z1), (None, vec)] + [(None, w) for w in weights],
+            [
+                (qkv_at, (groups, 3 * width, lanes), bf16),
+                (att_at, (groups, GROUP * heads * SEQ, SEQ), bf16),
+                (deep_at, wide, bf16),
+            ] + [(None, (3 * width, width), bf16)] * fresh,
+            [
+                ((3 * width, lanes), bf16),
+                ((GROUP * heads, SEQ, SEQ), f32),
+                ((GROUP * heads, SEQ, SEQ), bf16),
+            ] + [((3 * width, width), f32)] * fresh,
+            "attend", 4e9, before,
+        )
+
     early = groups - 2 if groups > 2 else groups
-    qkv, att, attn, wq = attend_call(info, block_in, vec, 0, early, (wq_own, wq_other))
+    qkv, att, attn, wq = attend(0, early, (wq_own, wq_other))
     rest_own = after(rest_own, attn)
     rest_other = swap(rest_own)
     if early < groups:
-        qkv, att, attn = attend_call(info, block_in, vec, early, groups, (wq,), (qkv, att, attn))
-    out, dh, gp, wpn, keep_b, send_b = mlp_call(
-        info, block_in, out_grad, attn, rest_own, rest_other, vec, ub
+        qkv, att, attn = attend(early, groups, (wq,), (qkv, att, attn))
+
+    block = 256
+    rows_b = 2 * cu + 4 + ff // width
+    h1, act, dh, gp, wpn, wdn, keep_b, send_b = grid_call(
+        mlp_kernel, info, 0, groups,
+        [(tokens, block_in), (tokens, out_grad), (deep_spec, attn)]
+        + [(None, array) for array in (rest_own, rest_other, vec, ub)],
+        [
+            (deep_spec, wide, f32),
+            (ff_spec, (groups, ff, lanes), bf16),
+            (deep_spec, wide, f32),
+            (None, (width, width), f32),
+            (None, (width, width), bf16),
+            (None, (width, ff), bf16),
+            (None, (half, rows_b, width), f32),
+            (None, (half, rows_b, width), bf16),
+        ],
+        [
+            ((width, ff), bf16),
+            ((width, width), bf16),
+            ((ff, width), bf16),
+            ((ff, width), bf16),
+            ((ff, width), f32),
+            ((ff, width), f32),
+            ((4, width, LANES), f32),
+            ((ff, LANES), f32),
+            ((width, lanes), f32),
+            ((width, lanes), bf16),
+            ((width, lanes), bf16),
+            ((ff, lanes), bf16),
+            ((ff, lanes), bf16),
+            ((width, lanes), bf16),
+            ((1, lanes), f32),
+            ((ff, width), f32),
+            ((2, block, lanes), f32),
+            ((2, block, lanes), f32),
+        ],
+        "mlp", 10e9,
     )
 
+    def back(start, stop, before=()):
+        _, qkv_at, att_at, deep_at, _ = group_specs(width, ff, start)
+        last = stop == groups
+        rows = -(-(blocks * (cq + cp) + 4 * blocks) // 16) * 16
+        totals = [(3 * width, width), (3, width, LANES)]
+        scratch = [
+            ((width, lanes), bf16),
+            ((3 * width, lanes), bf16),
+            ((GROUP * heads, SEQ, SEQ), f32),
+            ((GROUP * heads, SEQ, SEQ), bf16),
+        ]
+        ins = [
+            (deep_at, z1), (qkv_at, qkv), (att_at, att), (deep_at, dh),
+            (None, wpn), (None, wq), (None, gp), (None, feature_vectors),
+        ]
+        outs = [(qkv_at, (groups, 3 * width, lanes), bf16)]
+        if last:
+            outs += [(None, (half, rows, LANES), f32), (None, (half, rows, LANES), bf16)]
+            scratch = [(shape, f32) for shape in totals + [(rows, LANES)]] + scratch
+        else:
+            outs += [(None, shape, f32) for shape in totals]
+        kernel = functools.partial(back_kernel, start, last)
+        if not before:
+            return grid_call(kernel, info, start, stop, ins, outs, scratch, "back", 6e9)
+        ins += [(None, array) for array in before[1:]]
+        return grid_call(kernel, info, start, stop, ins, outs, scratch, "back", 6e9, before[:1])
+
+    def out_part(start, stop, before=()):
+        tokens, _, _, deep_at, ff_at = group_specs(width, ff, start)
+        return grid_call(
+            functools.partial(out_kernel, start), info, start, stop,
+            [(deep_at, h1), (ff_at, act), (None, wdn), (None, vec)],
+            [(tokens, block_in.shape, f32)], [], "out", 1.5e9, before,
+        )
+
+    def input_part(start, stop, dqkv, before=()):
+        tokens, qkv_at, _, deep_at, _ = group_specs(width, ff, start)
+        return grid_call(
+            functools.partial(input_kernel, start), info, start, stop,
+            [(tokens, block_in), (qkv_at, dqkv), (deep_at, dh), (None, wq), (None, vec)],
+            [(tokens, block_in.shape, f32)],
+            [((width, 3 * width), bf16), ((1, lanes), f32), ((width, lanes), f32)], "input", 2e9, before,
+        )
+
     def fold(keep, received):
-        return exchange((keep + received.astype(f32)).astype(bf16))
-
-    swapped = swap(send_b)
-    one = 1 if groups > 2 else groups
-    most = groups - 1 if groups > 2 else groups
-    done = back_call(info, block_in, qkv, att, dh, wpn, wq, gp, vec, half, 0, one)
-    got_b = fold(keep_b, after(swapped, done[1]))
-    if one < groups:
-        done = back_call(info, block_in, qkv, att, dh, wpn, wq, gp, vec, half, one, most, done)
-    got_b = after(got_b, done[1])
-
-    def sums(got, moment_a, moment_b, vectors, lanes, name):
+        return (keep + received.astype(f32)).astype(bf16)
+
+    def sums(got, moment_a, moment_b, vectors, spread, name):
         rows = moment_a.shape[0] + moment_b.shape[0]
         return small_call(
             state_kernel,
             [
                 (moment_a.shape, f32), (moment_b.shape, f32), (moment_a.shape, f32), (moment_b.shape, f32),
-                ((half, rows, width), bf16), ((rows, width), f32), ((vectors, lanes), f32),
+                (spread, bf16), ((rows, width), f32), (vectors, f32),
             ],
             name + "_state",
-        )(got, moment_a, moment_b)
+            scalars=1,
+        )(par.reshape(1), got, moment_a, moment_b)
 
     def polynomials(own, other, first, name):
         square = pltpu.VMEM((width, width), f32)
@@ -821,22 +845,48 @@
             scalars=1,
         )(par.reshape(1), mine, theirs, state, weight_a, weight_b)
 
+    swapped = swap(send_b)
+    one = 1 if groups > 2 else groups
+    done = back(0, one)
+    swapped = after(swapped, done[1])
+    got_b = exchange(fold(keep_b, swapped))
+    if one < groups:
+        done = back(one, groups, done)
+    dqkv, keep_a, send_a = done
+    summed_a = fold(keep_a, swap(send_a))
+    got_b = after(got_b, summed_a)
     gu, gd, su, sd, spread_b, state_b, vector_b = sums(
-        got_b, mu_s, md_s, 4 + ff // width, width, "mlp"
+        got_b, mu_s, md_s, (4 + ff // width, width), (2, cu, width), "mlp"
     )
-    own_b = exchange(spread_b)
-    if most < groups:
-        done = back_call(info, block_in, qkv, att, dh, wpn, wq, gp, vec, half, most, groups, done)
-    dx, keep_a, send_a = done
-    got_a = fold(keep_a, swap(send_a))
-    other_b = swap(own_b)
-    gq, gpr, sq, sp, spread_a, state_a, vector_a = sums(got_a, mq_s, mp_s, 4 * blocks, LANES, "att")
+    got_a = exchange(summed_a)
+
+    bits = [1 << k for k in range(1, devices.bit_length() - 1)][::-1]
+    pool = jnp.concatenate([spread_b[0], swap(spread_b[1])], axis=0)
+    mid = groups // 2
+    for index, bit in enumerate(bits):
+        moved = lax.ppermute(pool, "dp", [(i, i ^ bit) for i in range(devices)])
+        if index == 0:
+            out = out_part(0, mid)
+            moved = after(moved, out[0])
+        elif index == 1:
+            out = out_part(mid, groups, out)
+            moved = after(moved, out[0])
+        elif index == 2:
+            dx = input_part(0, mid, dqkv)
+            moved = after(moved, dx[0])
+        if index + 1 < len(bits):
+            pool = jnp.concatenate([pool, moved], axis=0)
+    gq, gpr, sq, sp, spread_a, state_a, vector_a = sums(
+        got_a, mq_s, mp_s, (4 * blocks, LANES), (half, cq + cp, width), "att"
+    )
     own_a = exchange(spread_a)
+    dx = input_part(mid, groups, dqkv, dx)
+    mine_b = polynomials(pool, moved, cu, "mlp")
     other_a = swap(own_a)
-    mine_b = polynomials(own_b, other_b, cu, "mlp")
     uu, ud = updates(mine_b, swap(mine_b), state_b, wu_s, wd_s, "mlp")
     mine_a = polynomials(own_a, other_a, cq, "att")
     uq, up = updates(mine_a, swap(mine_a), state_a, wq_s, wp_s, "att")
+    out, dx = out[0], dx[0]
 
     vector_grad = jnp.concatenate([vector_a.reshape(4, width), vector_b[:4]], axis=0)
     bias_grad = natural_ff(vector_b[4:].reshape(ff), half)

time: 332 us -> 340 us (1.024)
  blocking collectives: 23 us -> 0 us
  Pallas kernels: 138 us -> 159 us
  waiting for transfers between devices: 68.1 us -> 73.8 us
  local copies, waits for them, and re-layouts: 7.63 us -> 11.9 us
    all_to_all x1 -> x0, blocking collectives: 23 us -> none  [exchange(): return lax.all_to_all(x, 'dp', 0, 0, axis_index_groups=planes, tiled=True)]
    pallas_call x6 -> x10, Pallas kernels: 94 us -> 116 us  [grid_call(): pl.pallas_call(kernel, grid_spec=pltpu.PrefetchScalarGridSpec(num_scalar_...]
    ppermute x0 -> x4, waiting for transfers between devices: none -> 21.4 us  [body(): moved = lax.ppermute(pool, 'dp', [(i, i ^ bit) for i in range(devices)])]
    all_to_all x5, waiting for transfers between devices: 66.1 us -> 50.4 us  [exchange(): return lax.all_to_all(x, 'dp', 0, 0, axis_index_groups=planes, tiled=True)]
    all_to_all x5, starting transfers between devices: 41.4 us -> 27.2 us  [exchange(): return lax.all_to_all(x, 'dp', 0, 0, axis_index_groups=planes, tiled=True)]
    ppermute x8, starting transfers between devices: 37.5 us -> 45.8 us  [swap(): return lax.ppermute(x, 'dp', pairs)]
    ppermute x0 -> x4, starting transfers between devices: none -> 6.98 us  [body(): moved = lax.ppermute(pool, 'dp', [(i, i ^ bit) for i in range(devices)])]
    unnamed x40 -> x44, local copies, waits for them, and re-layouts: 3.56 us -> 6.85 us
  transfers between devices with their start and end apart: 13 -> 17, of which waited for: 5 -> 8; matrix products, arithmetic and copies ran while one was open for 3% -> 3% of each run, Pallas kernels for 30% -> 24%
where the time goes in v3:
time: 340 us; the launch traced here: 336 us
  Pallas kernels  159 us (47%)
  starting transfers between devices  80 us (24%)
  waiting for transfers between devices  73.8 us (22%)
  local copies, waits for them, and re-layouts  11.9 us (4%)
  other arithmetic  8.99 us (3%)
    pallas_call x10, Pallas kernels, grid_call(): pl.pallas_call(kernel, grid_spec=pltpu.PrefetchScalarGridSpec(num_scalar_...  116 us
    all_to_all x5, waiting for transfers between devices, exchange(): return lax.all_to_all(x, 'dp', 0, 0, axis_index_groups=planes, tiled=True)  50.4 us
    ppermute x8, starting transfers between devices, swap(): return lax.ppermute(x, 'dp', pairs)  45.8 us
    pallas_call x7, Pallas kernels, call(): pl.pallas_call(kernel, in_specs=[smem] * scalars + [vmem] * (len(args) -...  42.8 us
    all_to_all x5, starting transfers between devices, exchange(): return lax.all_to_all(x, 'dp', 0, 0, axis_index_groups=planes, tiled=True)  27.2 us
    ppermute x4, waiting for transfers between devices, body(): moved = lax.ppermute(pool, 'dp', [(i, i ^ bit) for i in range(devices)])  21.4 us
    ppermute x4, starting transfers between devices, body(): moved = lax.ppermute(pool, 'dp', [(i, i ^ bit) for i in range(devices)])  6.98 us
    unnamed x44, local copies, waits for them, and re-layouts  6.85 us
  transfers between devices with their start and end apart: 17, of which 8 were waited for; matrix products, arithmetic and copies ran while one was open for 3% of the time, Pallas kernels for 24%

profile of v3, /device:TPU:0, one launch (start us, length us, event | category | flops | bytes accessed | tf_op | source)
XLA Modules:
  0.0 336.2 jit_solution(10032624269019117727)
XLA Ops:
  0.7 2.3 prep.1
  3.0 8.3 %all-to-all-start = ((bf16[16,36,384]{2,1,0:T(8,128)(2,1)}), bf16[16,36,384]{2,1,0:T(8,128)(2,1)S(1)}, u32[]{:S(2)}, u32[]{:S(2)}) async-start(bf16[16,36,384]{2,1,0:T(8,128)(2,1)} %get-tuple-element.66), calls=%async_computation | async-start | bytes 983040 | tf_op jit(solution)/shard_map/all_to_all | solution.py:679
  12.7 13.2 %all-to-all-done.refs_0_ = bf16[16,36,384]{2,1,0:T(8,128)(2,1)S(1)} async-done(((bf16[16,36,384]{2,1,0:T(8,128)(2,1)}), bf16[16,36,384]{2,1,0:T(8,128)(2,1)S(1)}, u32[]{:S(2)}, u32[]{:S(2)}) %all-to-all-start) | async-done | bytes 442400 | tf_op jit(solution)/shard_map/all_to_all | solution.py:679
  25.8 3.8 %all-to-all-start.1 = ((bf16[16,112,384]{2,1,0:T(8,128)(2,1)}), bf16[16,112,384]{2,1,0:T(8,128)(2,1)S(1)}, u32[]{:S(2)}, u32[]{:S(2)}) async-start(bf16[16,112,384]{2,1,0:T(8,128)(2,1)} %get-tuple-element.73), calls=%async_computation.1 | async-start | bytes 2752512 | tf_op jit(solution)/shard_map/all_to_all | solution.py:679
  31.4 7.6 %normal.1.z_ref = bf16[8,384,512]{2,1,0:T(8,128)(2,1)} custom-call(s32[2]{0:T(128)} %pad_add_fusion.info, bf16[4096,384]{1,0:T(8,128)(2,1)} %x_ref.7, f32[8,384,128]{2,1,0:T(8,128)} %broadcast_in_dim.4.vec_ref), custom_call_target="tpu_custom_call" | custom-call | flops 8000000000 | bytes 32000000 | tf_op jit(solution)/shard_map/normal/pallas_call | solution.py:612
  39.8 13.1 %attend.2 = (bf16[8,1152,512]{2,1,0:T(8,128)(2,1)}, bf16[8,3072,256]{2,1,0:T(8,128)(2,1)}, bf16[8,384,512]{2,1,0:T(8,128)(2,1)}, bf16[1152,384]{1,0:T(8,128)(2,1)}) custom-call(s32[2]{0:T(128)} %pad_add_fusion.info, bf16[8,384,512]{2,1,0:T(8,128)(2,1)} %normal.1.z_ref, f32[8,384,128]{2,1,0:T(8,128)} %broadcast_in_dim.4.vec_ref, ...), custom_call_target="tpu_custom_call" | custom-call | flops 24000000000 | bytes 24000000 | tf_op jit(solution)/shard_map/attend/pallas_call | solution.py:612
  53.0 6.8 %all-to-all-done.1.own_ref = bf16[16,112,384]{2,1,0:T(8,128)(2,1)S(1)} async-done(((bf16[16,112,384]{2,1,0:T(8,128)(2,1)}), bf16[16,112,384]{2,1,0:T(8,128)(2,1)S(1)}, u32[]{:S(2)}, u32[]{:S(2)}) %all-to-all-start.1) | async-done | bytes 1376288 | tf_op jit(solution)/shard_map/all_to_all | solution.py:679
  60.6 5.2 %attend.3 = (bf16[8,1152,512]{2,1,0:T(8,128)(2,1)}, bf16[8,3072,256]{2,1,0:T(8,128)(2,1)}, bf16[8,384,512]{2,1,0:T(8,128)(2,1)}) custom-call(s32[2]{0:T(128)} %pad_add_fusion.info, bf16[8,384,512]{2,1,0:T(8,128)(2,1)} %normal.1.z_ref, f32[8,384,128]{2,1,0:T(8,128)} %broadcast_in_dim.4.vec_ref, ...), custom_call_target="tpu_custom_call", output_to_operand_aliasing={{0}: (4, {}), {1}: (5, {}), {2}: (6, {})} | custom-call | flops 8000000000 | bytes 8000000 | tf_op jit(solution)/shard_map/attend/pallas_call | solution.py:612
  67.1 30.2 %mlp.1 = (f32[8,384,512]{2,1,0:T(8,128)}, bf16[8,1536,512]{2,1,0:T(8,128)(2,1)}, f32[8,384,512]{2,1,0:T(8,128)}, f32[384,384]{1,0:T(8,128)}, bf16[384,384]{1,0:T...) custom-call(s32[2]{0:T(128)} %pad_add_fusion.info, ...), custom_call_target="tpu_custom_call" | custom-call | flops 80000000000 | bytes 32000000 | tf_op jit(solution)/shard_map/mlp/pallas_call | solution.py:612
  97.3 8.2 %back.2 = (bf16[8,1152,512]{2,1,0:T(8,128)(2,1)}, f32[1152,384]{1,0:T(8,128)}, f32[3,384,128]{2,1,0:T(8,128)}) custom-call(s32[2]{0:T(128)} %pad_add_fusion.info, bf16[8,384,512]{2,1,0:T(8,128)(2,1)} %normal.1.z_ref, bf16[8,1152,512]{2,1,0:T(8,128)(2,1)} %get-tuple-element.78.qkv_ref, bf16[8,3072,256]{2,1,0:T(8,128)(2,1)} %get-tuple-element.79.att_ref, ...), custom_call_target="tpu_custom_call" | custom-call | flops 6000000000 | bytes 4000000 | tf_op jit(solution)/shard_map/back/pallas_call | solution.py:612
  105.5 19.7 %back.3 = (bf16[8,1152,512]{2,1,0:T(8,128)(2,1)}, f32[16,160,128]{2,1,0:T(8,128)}, bf16[16,160,128]{2,1,0:T(8,128)(2,1)}) custom-call(s32[2]{0:T(128)} %pad_add_fusion.info, bf16[8,384,512]{2,1,0:T(8,128)(2,1)} %normal.1.z_ref, bf16[8,1152,512]{2,1,0:T(8,128)(2,1)} %get-tuple-element.78.qkv_ref, ...), custom_call_target="tpu_custom_call", output_to_operand_aliasing={{0}: (11, {})} | custom-call | flops 41999998976 | bytes 28000000 | tf_op jit(solution)/shard_map/back/pallas_call | solution.py:612
  125.2 42.7 %collective-permute-start.2 = (bf16[16,160,128]{2,1,0:T(8,128)(2,1)}, bf16[16,160,128]{2,1,0:T(8,128)(2,1)S(1)}, u32[]{:S(2)}, u32[]{:S(2)}) collective-permute-start(bf16[16,160,128]{2,1,0:T(8,128)(2,1)} %get-tuple-element.88), channel_id=1, source_target_pairs={{0,1},{1,0},{2,3},{3,2},{4,5},{5,4},{6,7},{7,6},{8,9},{9,8},{10,11... | collective-permute-start | bytes 1966088 | tf_op jit(solution)/shard_map/ppermute | solution.py:682
  169.9 2.5 add_convert_fusion.1
  172.4 6.4 %all-to-all-start.2 = ((bf16[16,160,128]{2,1,0:T(8,128)(2,1)}), bf16[16,160,128]{2,1,0:T(8,128)(2,1)S(1)}, u32[]{:S(2)}, u32[]{:S(2)}) async-start(bf16[16,160,128]{2,1,0:T(8,128)(2,1)} %add_convert_fusion.1), calls=%async_computation.2 | async-start | bytes 1310720 | tf_op jit(solution)/shard_map/all_to_all | solution.py:679
  178.9 17.6 %all-to-all-done.2.got_ref = bf16[16,160,128]{2,1,0:T(8,128)(2,1)S(1)} async-done(((bf16[16,160,128]{2,1,0:T(8,128)(2,1)}), bf16[16,160,128]{2,1,0:T(8,128)(2,1)S(1)}, u32[]{:S(2)}, u32[]{:S(2)}) %all-to-all-start.2) | async-done | bytes 655392 | tf_op jit(solution)/shard_map/all_to_all | solution.py:679
  199.5 4.6 %all-to-all-start.4 = ((bf16[16,48,384]{2,1,0:T(8,128)(2,1)}), bf16[16,48,384]{2,1,0:T(8,128)(2,1)S(1)}, u32[]{:S(2)}, u32[]{:S(2)}) async-start(bf16[16,48,384]{2,1,0:T(8,128)(2,1)} %get-tuple-element.99), calls=%async_computation.4 | async-start | bytes 1179648 | tf_op jit(solution)/shard_map/all_to_all | solution.py:679
  204.1 2.6 add_convert_fusion
  206.7 12.8 %all-to-all-done.4.own_ref = bf16[16,48,384]{2,1,0:T(8,128)(2,1)S(1)} async-done(((bf16[16,48,384]{2,1,0:T(8,128)(2,1)}), bf16[16,48,384]{2,1,0:T(8,128)(2,1)S(1)}, u32[]{:S(2)}, u32[]{:S(2)}) %all-to-all-start.4) | async-done | bytes 589856 | tf_op jit(solution)/shard_map/all_to_all | solution.py:679
  219.5 4.1 %all-to-all-start.3 = ((bf16[16,104,384]{2,1,0:T(8,128)(2,1)}), bf16[16,104,384]{2,1,0:T(8,128)(2,1)S(1)}, u32[]{:S(2)}, u32[]{:S(2)}) async-start(bf16[16,104,384]{2,1,0:T(8,128)(2,1)} %add_convert_fusion), calls=%async_computation.3 | async-start | bytes 2555904 | tf_op jit(solution)/shard_map/all_to_all | solution.py:679
  224.8 9.3 %input.2.refs_0_ = f32[4096,384]{1,0:T(8,128)} custom-call(s32[2]{0:T(128)} %pad_add_fusion.info, bf16[4096,384]{1,0:T(8,128)(2,1)} %x_ref.7, bf16[8,1152,512]{2,1,0:T(8,128)(2,1)} %get-tuple-element.86.dqkv_ref, f32[8,384,512]{2,1,0:T(8,128)} %get-tuple-element.80.dh_ref, bf16[1152,384]{1,0:T(8,128)(2,1)} %get-tuple-element.67.refs_0_.wq_ref, ...), custom_call_target="tpu_custom_call" | custom-call | flops 8000000000 | bytes 16000000 | tf_op jit(solution)/shard_map/input/pallas_call | solution.py:612
  234.2 8.3 %out.2.refs_0_ = f32[4096,384]{1,0:T(8,128)} custom-call(s32[2]{0:T(128)} %pad_add_fusion.info, f32[8,384,512]{2,1,0:T(8,128)} %get-tuple-element.75.h_ref, bf16[8,1536,512]{2,1,0:T(8,128)(2,1)} %get-tuple-element.76.act_ref, bf16[384,1536]{1,0:T(8,128)(2,1)} %get-tuple-element.77.wdn_ref, f32[8,384,128]{2,1,0:T(8,128)} %broadcast_in_dim.4.vec_ref), custom_call_target="tpu_custom_call" | custom-call | flops 6000000000 | bytes 16000000 | tf_op jit(solution)/shard_map/out/pallas_call | solution.py:612
  243.3 15.5 %att_newton.1.mine_ref = f32[392,384]{1,0:T(8,128)} custom-call(s32[2]{0:T(128)} %pad_add_fusion.1.info, bf16[16,48,384]{2,1,0:T(8,128)(2,1)} %copy-done.3, bf16[16,48,384]{2,1,0:T(8,128)(2,1)} %copy-done.9), custom_call_target="tpu_custom_call" | custom-call | tf_op jit(solution)/shard_map/att_newton/pallas_call | solution.py:585
  262.0 2.3 mlp_state.1
  268.2 2.9 collective-permute-start.7
  271.2 4.4 %collective-permute-done.7 = bf16[96,384]{1,0:T(8,128)(2,1)S(1)} collective-permute-done((bf16[96,384]{1,0:T(8,128)(2,1)S(1)}, bf16[96,384]{1,0:T(8,128)(2,1)S(1)}, u32[]{:S(2)}, u32[]{:S(2)}) %collective-permute-start.7) | collective-permute-done | bytes 73760 | tf_op jit(solution)/shard_map/ppermute | solution.py:867
  276.4 7.2 %out.3 = f32[4096,384]{1,0:T(8,128)} custom-call(s32[2]{0:T(128)} %pad_add_fusion.info, f32[8,384,512]{2,1,0:T(8,128)} %get-tuple-element.75.h_ref, bf16[8,1536,512]{2,1,0:T(8,128)(2,1)} %get-tuple-element.76.act_ref, bf16[384,1536]{1,0:T(8,128)(2,1)} %get-tuple-element.77.wdn_ref, ...), custom_call_target="tpu_custom_call", output_to_operand_aliasing={{}: (5, {})} | custom-call | flops 6000000000 | bytes 16000000 | tf_op jit(solution)/shard_map/out/pallas_call | solution.py:612
  285.6 7.3 %collective-permute-done.9 = bf16[384,384]{1,0:T(8,128)(2,1)S(1)} collective-permute-done((bf16[384,384]{1,0:T(8,128)(2,1)S(1)}, bf16[384,384]{1,0:T(8,128)(2,1)S(1)}, u32[]{:S(2)}, u32[]{:S(2)}) %collective-permute-start.9) | collective-permute-done | bytes 294944 | tf_op jit(solution)/shard_map/ppermute | solution.py:867
  296.4 2.6 att_update.1
  299.0 9.7 %collective-permute-done.10.other_ref = bf16[768,384]{1,0:T(8,128)(2,1)S(1)} collective-permute-done((bf16[768,384]{1,0:T(8,128)(2,1)S(1)}, bf16[768,384]{1,0:T(8,128)(2,1)S(1)}, u32[]{:S(2)}, u32[]{:S(2)}) %collective-permute-start.10) | collective-permute-done | bytes 589856 | tf_op jit(solution)/shard_map/ppermute | solution.py:867
  309.6 15.4 %mlp_newton.1.mine_ref = f32[392,384]{1,0:T(8,128)} custom-call(s32[2]{0:T(128)} %pad_add_fusion.2.info, bf16[768,384]{1,0:T(8,128)(2,1)} %copy-done.5, bf16[768,384]{1,0:T(8,128)(2,1)} %copy-done.8), custom_call_target="tpu_custom_call" | custom-call | tf_op jit(solution)/shard_map/mlp_newton/pallas_call | solution.py:585
  325.0 7.7 %input.3 = f32[4096,384]{1,0:T(8,128)} custom-call(s32[2]{0:T(128)} %pad_add_fusion.info, bf16[4096,384]{1,0:T(8,128)(2,1)} %x_ref.7, bf16[8,1152,512]{2,1,0:T(8,128)(2,1)} %get-tuple-element.86.dqkv_ref, f32[8,384,512]{2,1,0:T(8,128)} %get-tuple-element.80.dh_ref, ...), custom_call_target="tpu_custom_call", output_to_operand_aliasing={{}: (6, {})} | custom-call | flops 8000000000 | bytes 16000000 | tf_op jit(solution)/shard_map/input/pallas_call | solution.py:612
  333.5 2.7 mlp_update.1
  (89 shorter events, 27.0 us)
Async XLA Ops:
  0.7 29.1 %copy-start.11 = (f32[8,384]{1,0:T(8,128)S(1)}, f32[8,384]{1,0:T(8,128)}, u32[]{:S(2)}) copy-start(f32[8,384]{1,0:T(8,128)} %row_ref.3) | copy-start | bytes 36868
  3.0 22.8 %all-to-all-start = ((bf16[16,36,384]{2,1,0:T(8,128)(2,1)}), bf16[16,36,384]{2,1,0:T(8,128)(2,1)S(1)}, u32[]{:S(2)}, u32[]{:S(2)}) async-start(bf16[16,36,384]{2,1,0:T(8,128)(2,1)} %get-tuple-element.66), calls=%async_computation | async-start | bytes 983040 | tf_op jit(solution)/shard_map/all_to_all | solution.py:679
  25.8 13.2 %copy-start.10 = (bf16[16,36,384]{2,1,0:T(8,128)(2,1)}, bf16[16,36,384]{2,1,0:T(8,128)(2,1)S(1)}, u32[]{:S(2)}) copy-start(bf16[16,36,384]{2,1,0:T(8,128)(2,1)S(1)} %all-to-all-done.refs_0_) | copy-start | bytes 1327108
  25.8 33.9 %all-to-all-start.1 = ((bf16[16,112,384]{2,1,0:T(8,128)(2,1)}), bf16[16,112,384]{2,1,0:T(8,128)(2,1)S(1)}, u32[]{:S(2)}, u32[]{:S(2)}) async-start(bf16[16,112,384]{2,1,0:T(8,128)(2,1)} %get-tuple-element.73), calls=%async_computation.1 | async-start | bytes 2752512 | tf_op jit(solution)/shard_map/all_to_all | solution.py:679
  29.7 9.3 %collective-permute-start = (bf16[16,36,384]{2,1,0:T(8,128)(2,1)S(1)}, bf16[16,36,384]{2,1,0:T(8,128)(2,1)S(1)}, u32[]{:S(2)}, u32[]{:S(2)}) collective-permute-start(bf16[16,36,384]{2,1,0:T(8,128)(2,1)S(1)} %all-to-all-done.refs_0_), channel_id=1, source_target_pairs={{0,1},{1,0},{2,3},{3,2},{4,5},{5,4},{6,7},{7,6},{8,9},{9,8},{10,11... | collective-permute-start | bytes 1327112 | tf_op jit(solution)/shard_map/ppermute | solution.py:682
  39.0 21.4 %copy-start.14 = (f32[1536]{0:T(1024)S(1)}, f32[1536]{0:T(1024)}, u32[]{:S(2)}) copy-start(f32[1536]{0:T(1024)} %param.21) | copy-start | bytes 18436
  59.8 6.0 %copy-start.4 = (bf16[16,112,384]{2,1,0:T(8,128)(2,1)}, bf16[16,112,384]{2,1,0:T(8,128)(2,1)S(1)}, u32[]{:S(2)}) copy-start(bf16[16,112,384]{2,1,0:T(8,128)(2,1)S(1)} %all-to-all-done.1.own_ref) | copy-start | bytes 4128772
  59.8 6.0 %collective-permute-start.1 = (bf16[16,112,384]{2,1,0:T(8,128)(2,1)S(1)}, bf16[16,112,384]{2,1,0:T(8,128)(2,1)S(1)}, u32[]{:S(2)}, u32[]{:S(2)}) collective-permute-start(bf16[16,112,384]{2,1,0:T(8,128)(2,1)S(1)} %all-to-all-done.1.own_ref), channel_id=1, source_target_pairs={{0,1},{1,0},{2,3},{3,2},{4,5},{5,4},{6,7},{7,6},{8,9},{9,8},{10,11... | collective-permute-start | bytes 4128776 | tf_op jit(solution)/shard_map/ppermute | solution.py:682
  65.7 1.4 copy-start.18
  125.2 44.7 %collective-permute-start.2 = (bf16[16,160,128]{2,1,0:T(8,128)(2,1)}, bf16[16,160,128]{2,1,0:T(8,128)(2,1)S(1)}, u32[]{:S(2)}, u32[]{:S(2)}) collective-permute-start(bf16[16,160,128]{2,1,0:T(8,128)(2,1)} %get-tuple-element.88), channel_id=1, source_target_pairs={{0,1},{1,0},{2,3},{3,2},{4,5},{5,4},{6,7},{7,6},{8,9},{9,8},{10,11... | collective-permute-start | bytes 1966088 | tf_op jit(solution)/shard_map/ppermute | solution.py:682
  169.9 34.2 %copy-start.2 = (f32[16,104,384]{2,1,0:T(8,128)S(1)}, f32[16,104,384]{2,1,0:T(8,128)}, u32[]{:S(2)}) copy-start(f32[16,104,384]{2,1,0:T(8,128)} %get-tuple-element.91) | copy-start | bytes 7667716
  172.4 24.2 %all-to-all-start.2 = ((bf16[16,160,128]{2,1,0:T(8,128)(2,1)}), bf16[16,160,128]{2,1,0:T(8,128)(2,1)S(1)}, u32[]{:S(2)}, u32[]{:S(2)}) async-start(bf16[16,160,128]{2,1,0:T(8,128)(2,1)} %add_convert_fusion.1), calls=%async_computation.2 | async-start | bytes 1310720 | tf_op jit(solution)/shard_map/all_to_all | solution.py:679
  178.8 25.3 %collective-permute-start.3 = (bf16[16,104,384]{2,1,0:T(8,128)(2,1)}, bf16[16,104,384]{2,1,0:T(8,128)(2,1)}, u32[]{:S(2)}, u32[]{:S(2)}) collective-permute-start(bf16[16,104,384]{2,1,0:T(8,128)(2,1)} %get-tuple-element.92), channel_id=1, source_target_pairs={{0,1},{1,0},{2,3},{3,2},{4,5},{5,4},{6,7},{7,6},{8,9},{9,8},{10,11... | collective-permute-start | bytes 3833864 | tf_op jit(solution)/shard_map/ppermute | solution.py:682
  199.5 20.1 %all-to-all-start.4 = ((bf16[16,48,384]{2,1,0:T(8,128)(2,1)}), bf16[16,48,384]{2,1,0:T(8,128)(2,1)S(1)}, u32[]{:S(2)}, u32[]{:S(2)}) async-start(bf16[16,48,384]{2,1,0:T(8,128)(2,1)} %get-tuple-element.99), calls=%async_computation.4 | async-start | bytes 1179648 | tf_op jit(solution)/shard_map/all_to_all | solution.py:679
  219.5 14.6 %copy-start.3 = (bf16[16,48,384]{2,1,0:T(8,128)(2,1)}, bf16[16,48,384]{2,1,0:T(8,128)(2,1)S(1)}, u32[]{:S(2)}) copy-start(bf16[16,48,384]{2,1,0:T(8,128)(2,1)S(1)} %all-to-all-done.4.own_ref) | copy-start | bytes 1769476
  219.5 41.4 %all-to-all-start.3 = ((bf16[16,104,384]{2,1,0:T(8,128)(2,1)}), bf16[16,104,384]{2,1,0:T(8,128)(2,1)S(1)}, u32[]{:S(2)}, u32[]{:S(2)}) async-start(bf16[16,104,384]{2,1,0:T(8,128)(2,1)} %add_convert_fusion), calls=%async_computation.3 | async-start | bytes 2555904 | tf_op jit(solution)/shard_map/all_to_all | solution.py:679
  224.8 17.6 %collective-permute-start.4 = (bf16[16,48,384]{2,1,0:T(8,128)(2,1)S(1)}, bf16[16,48,384]{2,1,0:T(8,128)(2,1)S(1)}, u32[]{:S(2)}, u32[]{:S(2)}) collective-permute-start(bf16[16,48,384]{2,1,0:T(8,128)(2,1)S(1)} %all-to-all-done.4.own_ref), channel_id=1, source_target_pairs={{0,1},{1,0},{2,3},{3,2},{4,5},{5,4},{6,7},{7,6},{8,9},{9,8},{10,11... | collective-permute-start | bytes 1769480 | tf_op jit(solution)/shard_map/ppermute | solution.py:682
  234.2 8.3 %copy-start.17 = (f32[12,128]{1,0:T(8,128)S(1)}, f32[12,128]{1,0:T(8,128)}, u32[]{:S(2)}) copy-start(f32[12,128]{1,0:T(8,128)} %get-tuple-element.97) | copy-start | bytes 18436
  258.8 36.8 %collective-permute-start.5 = (f32[392,384]{1,0:T(8,128)}, f32[392,384]{1,0:T(8,128)S(1)}, u32[]{:S(2)}, u32[]{:S(2)}) collective-permute-start(f32[392,384]{1,0:T(8,128)} %att_newton.1.mine_ref), channel_id=1, source_target_pairs={{0,1},{1,0},{2,3},{3,2},{4,5},{5,4},{6,7},{7,6},{8,9},{9,8},{10,11... | collective-permute-start | bytes 1806344 | tf_op jit(solution)/shard_map/ppermute | solution.py:682
  261.0 1.0 copy-start
  265.8 2.3 collective-permute-start.6
  267.4 26.9 %copy-start.16 = (f32[1536]{0:T(1024)}, f32[1536]{0:T(1024)S(1)}, u32[]{:S(2)}) copy-start(f32[1536]{0:T(1024)S(1)} %reshape.81) | copy-start | bytes 18436
  268.2 7.4 %collective-permute-start.7 = (bf16[96,384]{1,0:T(8,128)(2,1)S(1)}, bf16[96,384]{1,0:T(8,128)(2,1)S(1)}, u32[]{:S(2)}, u32[]{:S(2)}) collective-permute-start(bf16[96,384]{1,0:T(8,128)(2,1)S(1)} %pad_maximum_fusion.2), channel_id=1, source_target_pairs={{0,16},{1,17},{2,18},{3,19},{4,20},{5,21},{6,22},{7,23},{8,24},{9,... | collective-permute-start | bytes 221192 | tf_op jit(solution)/shard_map/ppermute | solution.py:867
  271.2 23.7 %copy-start.13 = (f32[8,384]{1,0:T(8,128)}, f32[8,384]{1,0:T(8,128)S(1)}, u32[]{:S(2)}) copy-start(f32[8,384]{1,0:T(8,128)S(1)} %get-tuple-element.115) | copy-start | bytes 36868
  275.6 18.7 %copy-start.15 = (f32[1536]{0:T(1024)S(1)}, f32[1536]{0:T(1024)}, u32[]{:S(2)}) copy-start(f32[1536]{0:T(1024)} %param.21) | copy-start | bytes 18436
  275.6 19.3 %copy-start.12 = (f32[8,384]{1,0:T(8,128)S(1)}, f32[8,384]{1,0:T(8,128)}, u32[]{:S(2)}) copy-start(f32[8,384]{1,0:T(8,128)} %row_ref.3) | copy-start | bytes 36868
  275.6 8.0 %collective-permute-start.8 = (bf16[192,384]{1,0:T(8,128)(2,1)S(1)}, bf16[192,384]{1,0:T(8,128)(2,1)S(1)}, u32[]{:S(2)}, u32[]{:S(2)}) collective-permute-start(bf16[192,384]{1,0:T(8,128)(2,1)S(1)} %pad_maximum_fusion.1), channel_id=1, source_target_pairs={{0,8},{1,9},{2,10},{3,11},{4,12},{5,13},{6,14},{7,15},{8,0},{9,1},... | collective-permute-start | bytes 442376 | tf_op jit(solution)/shard_map/ppermute | solution.py:867
  283.6 9.3 %collective-permute-start.9 = (bf16[384,384]{1,0:T(8,128)(2,1)S(1)}, bf16[384,384]{1,0:T(8,128)(2,1)S(1)}, u32[]{:S(2)}, u32[]{:S(2)}) collective-permute-start(bf16[384,384]{1,0:T(8,128)(2,1)S(1)} %pad_maximum_fusion), channel_id=1, source_target_pairs={{0,4},{1,5},{2,6},{3,7},{4,0},{5,1},{6,2},{7,3},{8,12},{9,13},{10,... | collective-permute-start | bytes 884744 | tf_op jit(solution)/shard_map/ppermute | solution.py:867
  292.9 15.8 %copy-start.5 = (bf16[768,384]{1,0:T(8,128)(2,1)}, bf16[768,384]{1,0:T(8,128)(2,1)S(1)}, u32[]{:S(2)}) copy-start(bf16[768,384]{1,0:T(8,128)(2,1)S(1)} %constant_dynamic-update-slice_fusion.own_ref) | copy-start | bytes 1769476
  292.9 15.8 %collective-permute-start.10 = (bf16[768,384]{1,0:T(8,128)(2,1)S(1)}, bf16[768,384]{1,0:T(8,128)(2,1)S(1)}, u32[]{:S(2)}, u32[]{:S(2)}) collective-permute-start(bf16[768,384]{1,0:T(8,128)(2,1)S(1)} %constant_dynamic-update-slice_fusion.own_ref), channel_id=1, source_target_pairs={{0,2},{1,3},{2,0},{3,1},{4,6},{5,7},{6,4},{7,5},{8,10},{9,11},{10,... | collective-permute-start | bytes 1769480 | tf_op jit(solution)/shard_map/ppermute | solution.py:867
  295.6 0.8 copy-start.6
  325.0 7.7 %collective-permute-start.11 = (f32[392,384]{1,0:T(8,128)}, f32[392,384]{1,0:T(8,128)S(1)}, u32[]{:S(2)}, u32[]{:S(2)}) collective-permute-start(f32[392,384]{1,0:T(8,128)} %mlp_newton.1.mine_ref), channel_id=1, source_target_pairs={{0,1},{1,0},{2,3},{3,2},{4,5},{5,4},{6,7},{7,6},{8,9},{9,8},{10,11... | collective-permute-start | bytes 1806344 | tf_op jit(solution)/shard_map/ppermute | solution.py:682
  (5 other events, 4.1 us)

commit v4 on v3

--- a/solution.py
+++ b/solution.py
@@ -766,7 +766,7 @@
         "mlp", 10e9,
     )
 
-    def back(start, stop, before=()):
+    def back(start, stop, before=(), info=info):
         _, qkv_at, att_at, deep_at, _ = group_specs(width, ff, start)
         last = stop == groups
         rows = -(-(blocks * (cq + cp) + 4 * blocks) // 16) * 16
@@ -793,7 +793,7 @@
         ins += [(None, array) for array in before[1:]]
         return grid_call(kernel, info, start, stop, ins, outs, scratch, "back", 6e9, before[:1])
 
-    def out_part(start, stop, before=()):
+    def out_part(start, stop, info, before=()):
         tokens, _, _, deep_at, ff_at = group_specs(width, ff, start)
         return grid_call(
             functools.partial(out_kernel, start), info, start, stop,
@@ -801,7 +801,7 @@
             [(tokens, block_in.shape, f32)], [], "out", 1.5e9, before,
         )
 
-    def input_part(start, stop, dqkv, before=()):
+    def input_part(start, stop, dqkv, info, before=()):
         tokens, qkv_at, _, deep_at, _ = group_specs(width, ff, start)
         return grid_call(
             functools.partial(input_kernel, start), info, start, stop,
@@ -848,44 +848,53 @@
     swapped = swap(send_b)
     one = 1 if groups > 2 else groups
     done = back(0, one)
-    swapped = after(swapped, done[1])
-    got_b = exchange(fold(keep_b, swapped))
+    summed_b = fold(keep_b, after(swapped, done[1]))
+    got_b = exchange(summed_b)
     if one < groups:
-        done = back(one, groups, done)
+        done = back(one, groups, done, after(info, summed_b))
     dqkv, keep_a, send_a = done
+    send_a, got_b = lax.optimization_barrier((send_a, got_b))
     summed_a = fold(keep_a, swap(send_a))
-    got_b = after(got_b, summed_a)
+    got_a = exchange(summed_a)
+    gate = after(info, summed_a)
     gu, gd, su, sd, spread_b, state_b, vector_b = sums(
-        got_b, mu_s, md_s, (4 + ff // width, width), (2, cu, width), "mlp"
+        after(got_b, summed_a), mu_s, md_s, (4 + ff // width, width), (2, cu, width), "mlp"
     )
-    got_a = exchange(summed_a)
 
     bits = [1 << k for k in range(1, devices.bit_length() - 1)][::-1]
-    pool = jnp.concatenate([spread_b[0], swap(spread_b[1])], axis=0)
+
+    def gather_step(pool, bit):
+        return lax.ppermute(pool, "dp", [(i, i ^ bit) for i in range(devices)])
+
+    def joined(pool, moved):
+        return jnp.concatenate([pool, moved], axis=0)
+
     mid = groups // 2
-    for index, bit in enumerate(bits):
-        moved = lax.ppermute(pool, "dp", [(i, i ^ bit) for i in range(devices)])
-        if index == 0:
-            out = out_part(0, mid)
-            moved = after(moved, out[0])
-        elif index == 1:
-            out = out_part(mid, groups, out)
-            moved = after(moved, out[0])
-        elif index == 2:
-            dx = input_part(0, mid, dqkv)
-            moved = after(moved, dx[0])
-        if index + 1 < len(bits):
-            pool = jnp.concatenate([pool, moved], axis=0)
+    pool = joined(spread_b[0], swap(spread_b[1]))
+    moved = gather_step(pool, bits[0])
+    out = out_part(0, mid, after(gate, pool))
+    for bit in bits[1:-2]:
+        pool = joined(pool, after(moved, out[0]))
+        moved = gather_step(pool, bit)
+    out = out_part(mid, groups, after(gate, pool), out)
+    got_a = after(got_a, out[0])
     gq, gpr, sq, sp, spread_a, state_a, vector_a = sums(
         got_a, mq_s, mp_s, (4 * blocks, LANES), (half, cq + cp, width), "att"
     )
     own_a = exchange(spread_a)
-    dx = input_part(mid, groups, dqkv, dx)
-    mine_b = polynomials(pool, moved, cu, "mlp")
+    pool = joined(pool, after(moved, spread_a))
+    moved = gather_step(pool, bits[-2])
+    dx = input_part(0, mid, dqkv, after(info, pool))
+    pool = joined(pool, after(moved, dx[0]))
+    moved = gather_step(pool, bits[-1])
+    dx = input_part(mid, groups, dqkv, after(info, pool), dx)
+    own_a = after(own_a, dx[0])
     other_a = swap(own_a)
+    mine_a = polynomials(own_a, other_a, cq, "att")
+    theirs_a = swap(mine_a)
+    mine_b = polynomials(pool, after(moved, mine_a), cu, "mlp")
+    uq, up = updates(mine_a, after(theirs_a, mine_b), state_a, wq_s, wp_s, "att")
     uu, ud = updates(mine_b, swap(mine_b), state_b, wu_s, wd_s, "mlp")
-    mine_a = polynomials(own_a, other_a, cq, "att")
-    uq, up = updates(mine_a, swap(mine_a), state_a, wq_s, wp_s, "att")
     out, dx = out[0], dx[0]
 
     vector_grad = jnp.concatenate([vector_a.reshape(4, width), vector_b[:4]], axis=0)

time: 340 us -> 294 us (0.86)
  waiting for transfers between devices: 73.8 us -> 34.3 us
  Pallas kernels: 159 us -> 167 us
  starting transfers between devices: 80 us -> 72.4 us
    all_to_all x5, waiting for transfers between devices: 50.4 us -> 26.3 us  [exchange(): return lax.all_to_all(x, 'dp', 0, 0, axis_index_groups=planes, tiled=True)]
    ppermute x8, starting transfers between devices: 45.8 us -> 24 us  [swap(): return lax.ppermute(x, 'dp', pairs)]
    ppermute x4, waiting for transfers between devices: 21.4 us -> 5.26 us  [gather_step(): return lax.ppermute(pool, 'dp', [(i, i ^ bit) for i in range(devices)])]
    all_to_all x5, starting transfers between devices: 27.2 us -> 38.6 us  [exchange(): return lax.all_to_all(x, 'dp', 0, 0, axis_index_groups=planes, tiled=True)]
    pallas_call x10, Pallas kernels: 116 us -> 124 us  [grid_call(): pl.pallas_call(kernel, grid_spec=pltpu.PrefetchScalarGridSpec(num_scalar_...]
    unnamed x44 -> x46, local copies, waits for them, and re-layouts: 6.85 us -> 5.76 us
  transfers between devices with their start and end apart: 17 -> 17, of which waited for: 8 -> 6; matrix products, arithmetic and copies ran while one was open for 3% -> 3% of each run, Pallas kernels for 24% -> 43%
where the time goes in v4:
time: 294 us
  Pallas kernels  167 us (57%)
  starting transfers between devices  72.4 us (25%)
  waiting for transfers between devices  34.3 us (12%)
  local copies, waits for them, and re-layouts  9.94 us (3%)
  other arithmetic  7.46 us (3%)
    pallas_call x10, Pallas kernels, grid_call(): pl.pallas_call(kernel, grid_spec=pltpu.PrefetchScalarGridSpec(num_scalar_...  124 us
    pallas_call x7, Pallas kernels, call(): pl.pallas_call(kernel, in_specs=[smem] * scalars + [vmem] * (len(args) -...  42.8 us
    all_to_all x5, starting transfers between devices, exchange(): return lax.all_to_all(x, 'dp', 0, 0, axis_index_groups=planes, tiled=True)  38.6 us
    all_to_all x5, waiting for transfers between devices, exchange(): return lax.all_to_all(x, 'dp', 0, 0, axis_index_groups=planes, tiled=True)  26.3 us
    ppermute x8, starting transfers between devices, swap(): return lax.ppermute(x, 'dp', pairs)  24 us
    ppermute x4, starting transfers between devices, gather_step(): return lax.ppermute(pool, 'dp', [(i, i ^ bit) for i in range(devices)])  9.85 us
  transfers between devices with their start and end apart: 17, of which 6 were waited for; matrix products, arithmetic and copies ran while one was open for 3% of the time, Pallas kernels for 43%

profile of v4, /device:TPU:0, one launch (start us, length us, event | category | flops | bytes accessed | tf_op | source)
XLA Modules:
  0.0 293.6 jit_solution(14673818563047365464)
XLA Ops:
  0.7 2.3 prep.1
  2.9 8.3 %all-to-all-start = ((bf16[16,36,384]{2,1,0:T(8,128)(2,1)}), bf16[16,36,384]{2,1,0:T(8,128)(2,1)S(1)}, u32[]{:S(2)}, u32[]{:S(2)}) async-start(bf16[16,36,384]{2,1,0:T(8,128)(2,1)} %get-tuple-element.78), calls=%async_computation | async-start | bytes 983040 | tf_op jit(solution)/shard_map/all_to_all | solution.py:679
  12.5 13.3 %all-to-all-done.refs_0_ = bf16[16,36,384]{2,1,0:T(8,128)(2,1)S(1)} async-done(((bf16[16,36,384]{2,1,0:T(8,128)(2,1)}), bf16[16,36,384]{2,1,0:T(8,128)(2,1)S(1)}, u32[]{:S(2)}, u32[]{:S(2)}) %all-to-all-start) | async-done | bytes 442400 | tf_op jit(solution)/shard_map/all_to_all | solution.py:679
  25.8 3.8 %all-to-all-start.1 = ((bf16[16,112,384]{2,1,0:T(8,128)(2,1)}), bf16[16,112,384]{2,1,0:T(8,128)(2,1)S(1)}, u32[]{:S(2)}, u32[]{:S(2)}) async-start(bf16[16,112,384]{2,1,0:T(8,128)(2,1)} %get-tuple-element.85), calls=%async_computation.1 | async-start | bytes 2752512 | tf_op jit(solution)/shard_map/all_to_all | solution.py:679
  31.3 8.2 %normal.1.z_ref = bf16[8,384,512]{2,1,0:T(8,128)(2,1)} custom-call(s32[2]{0:T(128)} %pad_add_fusion.info, bf16[4096,384]{1,0:T(8,128)(2,1)} %x_ref.7, f32[8,384,128]{2,1,0:T(8,128)} %broadcast_in_dim.4.vec_ref), custom_call_target="tpu_custom_call" | custom-call | flops 8000000000 | bytes 32000000 | tf_op jit(solution)/shard_map/normal/pallas_call | solution.py:612
  40.3 14.5 %attend.2 = (bf16[8,1152,512]{2,1,0:T(8,128)(2,1)}, bf16[8,3072,256]{2,1,0:T(8,128)(2,1)}, bf16[8,384,512]{2,1,0:T(8,128)(2,1)}, bf16[1152,384]{1,0:T(8,128)(2,1)}) custom-call(s32[2]{0:T(128)} %pad_add_fusion.info, bf16[8,384,512]{2,1,0:T(8,128)(2,1)} %normal.1.z_ref, f32[8,384,128]{2,1,0:T(8,128)} %broadcast_in_dim.4.vec_ref, ...), custom_call_target="tpu_custom_call" | custom-call | flops 24000000000 | bytes 24000000 | tf_op jit(solution)/shard_map/attend/pallas_call | solution.py:612
  54.8 4.9 %all-to-all-done.1.own_ref = bf16[16,112,384]{2,1,0:T(8,128)(2,1)S(1)} async-done(((bf16[16,112,384]{2,1,0:T(8,128)(2,1)}), bf16[16,112,384]{2,1,0:T(8,128)(2,1)S(1)}, u32[]{:S(2)}, u32[]{:S(2)}) %all-to-all-start.1) | async-done | bytes 1376288 | tf_op jit(solution)/shard_map/all_to_all | solution.py:679
  59.9 5.1 %attend.3 = (bf16[8,1152,512]{2,1,0:T(8,128)(2,1)}, bf16[8,3072,256]{2,1,0:T(8,128)(2,1)}, bf16[8,384,512]{2,1,0:T(8,128)(2,1)}) custom-call(s32[2]{0:T(128)} %pad_add_fusion.info, bf16[8,384,512]{2,1,0:T(8,128)(2,1)} %normal.1.z_ref, f32[8,384,128]{2,1,0:T(8,128)} %broadcast_in_dim.4.vec_ref, ...), custom_call_target="tpu_custom_call", output_to_operand_aliasing={{0}: (4, {}), {1}: (5, {}), {2}: (6, {})} | custom-call | flops 8000000000 | bytes 8000000 | tf_op jit(solution)/shard_map/attend/pallas_call | solution.py:612
  66.5 35.1 %mlp.1 = (f32[8,384,512]{2,1,0:T(8,128)}, bf16[8,1536,512]{2,1,0:T(8,128)(2,1)}, f32[8,384,512]{2,1,0:T(8,128)}, f32[384,384]{1,0:T(8,128)}, bf16[384,384]{1,0:T...) custom-call(s32[2]{0:T(128)} %pad_add_fusion.info, ...), custom_call_target="tpu_custom_call" | custom-call | flops 80000000000 | bytes 32000000 | tf_op jit(solution)/shard_map/mlp/pallas_call | solution.py:612
  101.6 22.0 %collective-permute-start.2 = (bf16[16,104,384]{2,1,0:T(8,128)(2,1)}, bf16[16,104,384]{2,1,0:T(8,128)(2,1)S(1)}, u32[]{:S(2)}, u32[]{:S(2)}) collective-permute-start(bf16[16,104,384]{2,1,0:T(8,128)(2,1)} %get-tuple-element.88), channel_id=1, source_target_pairs={{0,1},{1,0},{2,3},{3,2},{4,5},{5,4},{6,7},{7,6},{8,9},{9,8},{10,11... | collective-permute-start | bytes 3833864 | tf_op jit(solution)/shard_map/ppermute | solution.py:682
  123.6 8.4 %back.2 = (bf16[8,1152,512]{2,1,0:T(8,128)(2,1)}, f32[1152,384]{1,0:T(8,128)}, f32[3,384,128]{2,1,0:T(8,128)}) custom-call(s32[2]{0:T(128)} %pad_add_fusion.info, bf16[8,384,512]{2,1,0:T(8,128)(2,1)} %normal.1.z_ref, bf16[8,1152,512]{2,1,0:T(8,128)(2,1)} %get-tuple-element.89.qkv_ref, bf16[8,3072,256]{2,1,0:T(8,128)(2,1)} %get-tuple-element.90.att_ref, ...), custom_call_target="tpu_custom_call" | custom-call | flops 6000000000 | bytes 4000000 | tf_op jit(solution)/shard_map/back/pallas_call | solution.py:612
  133.3 14.3 %all-to-all-start.2 = ((bf16[16,104,384]{2,1,0:T(8,128)(2,1)}), bf16[16,104,384]{2,1,0:T(8,128)(2,1)S(1)}, u32[]{:S(2)}, u32[]{:S(2)}) async-start(bf16[16,104,384]{2,1,0:T(8,128)(2,1)} %add_convert_fusion), calls=%async_computation.2 | async-start | bytes 2555904 | tf_op jit(solution)/shard_map/all_to_all | solution.py:679
  147.6 20.7 %back.3 = (bf16[8,1152,512]{2,1,0:T(8,128)(2,1)}, f32[16,160,128]{2,1,0:T(8,128)}, bf16[16,160,128]{2,1,0:T(8,128)(2,1)}) custom-call(s32[2]{0:T(128)} %pad_add_fusion.info, bf16[8,384,512]{2,1,0:T(8,128)(2,1)} %normal.1.z_ref, bf16[8,1152,512]{2,1,0:T(8,128)(2,1)} %get-tuple-element.89.qkv_ref, ...), custom_call_target="tpu_custom_call", output_to_operand_aliasing={{0}: (11, {})} | custom-call | flops 41999998976 | bytes 28000000 | tf_op jit(solution)/shard_map/back/pallas_call | solution.py:612
  168.3 8.1 %all-to-all-done.2.got_ref = bf16[16,104,384]{2,1,0:T(8,128)(2,1)S(1)} async-done(((bf16[16,104,384]{2,1,0:T(8,128)(2,1)}), bf16[16,104,384]{2,1,0:T(8,128)(2,1)S(1)}, u32[]{:S(2)}, u32[]{:S(2)}) %all-to-all-start.2) | async-done | bytes 1277984 | tf_op jit(solution)/shard_map/all_to_all | solution.py:679
  176.5 2.3 collective-permute-done.3
  178.8 2.3 add_convert_fusion.1
  181.1 7.0 %all-to-all-start.3 = ((bf16[16,160,128]{2,1,0:T(8,128)(2,1)}), bf16[16,160,128]{2,1,0:T(8,128)(2,1)S(1)}, u32[]{:S(2)}, u32[]{:S(2)}) async-start(bf16[16,160,128]{2,1,0:T(8,128)(2,1)} %add_convert_fusion.1), calls=%async_computation.3 | async-start | bytes 1310720 | tf_op jit(solution)/shard_map/all_to_all | solution.py:679
  188.1 2.3 mlp_state.1
  192.4 2.9 collective-permute-start.5
  195.3 8.2 %out.2.refs_0_ = f32[4096,384]{1,0:T(8,128)} custom-call(s32[2]{0:T(128)} %pad_add_fusion.info, f32[8,384,512]{2,1,0:T(8,128)} %get-tuple-element.107.h_ref, bf16[8,1536,512]{2,1,0:T(8,128)(2,1)} %get-tuple-element.108.act_ref, bf16[384,1536]{1,0:T(8,128)(2,1)} %get-tuple-element.109.wdn_ref, f32[8,384,128]{2,1,0:T(8,128)} %broadcast_in_dim.4.vec_ref), custom_call_target="tpu_custom_call" | custom-call | flops 6000000000 | bytes 16000000 | tf_op jit(solution)/shard_map/out/pallas_call | solution.py:612
  203.5 5.2 %collective-permute-done.5 = bf16[96,384]{1,0:T(8,128)(2,1)S(1)} collective-permute-done((bf16[96,384]{1,0:T(8,128)(2,1)S(1)}, bf16[96,384]{1,0:T(8,128)(2,1)S(1)}, u32[]{:S(2)}, u32[]{:S(2)}) %collective-permute-start.5) | collective-permute-done | bytes 73760 | tf_op jit(solution)/shard_map/ppermute | solution.py:867
  208.8 7.2 %out.3 = f32[4096,384]{1,0:T(8,128)} custom-call(s32[2]{0:T(128)} %pad_add_fusion.info, f32[8,384,512]{2,1,0:T(8,128)} %get-tuple-element.107.h_ref, bf16[8,1536,512]{2,1,0:T(8,128)(2,1)} %get-tuple-element.108.act_ref, bf16[384,1536]{1,0:T(8,128)(2,1)} %get-tuple-element.109.wdn_ref, ...), custom_call_target="tpu_custom_call", output_to_operand_aliasing={{}: (5, {})} | custom-call | flops 6000000000 | bytes 16000000 | tf_op jit(solution)/shard_map/out/pallas_call | solution.py:612
  216.8 2.1 att_state.1
  219.0 2.5 collective-permute-start.7
  221.5 5.2 %all-to-all-start.4 = ((bf16[16,48,384]{2,1,0:T(8,128)(2,1)}), bf16[16,48,384]{2,1,0:T(8,128)(2,1)S(1)}, u32[]{:S(2)}, u32[]{:S(2)}) async-start(bf16[16,48,384]{2,1,0:T(8,128)(2,1)} %get-tuple-element.113), calls=%async_computation.4 | async-start | bytes 1179648 | tf_op jit(solution)/shard_map/all_to_all | solution.py:679
  226.7 9.1 %input.2.refs_0_ = f32[4096,384]{1,0:T(8,128)} custom-call(s32[2]{0:T(128)} %pad_add_fusion.info, bf16[4096,384]{1,0:T(8,128)(2,1)} %x_ref.7, bf16[8,1152,512]{2,1,0:T(8,128)(2,1)} %get-tuple-element.116.dqkv_ref, f32[8,384,512]{2,1,0:T(8,128)} %get-tuple-element.91.dh_ref, bf16[1152,384]{1,0:T(8,128)(2,1)} %get-tuple-element.79.refs_0_.wq_ref, ...), custom_call_target="tpu_custom_call" | custom-call | flops 8000000000 | bytes 16000000 | tf_op jit(solution)/shard_map/input/pallas_call | solution.py:612
  235.9 7.8 %input.3 = f32[4096,384]{1,0:T(8,128)} custom-call(s32[2]{0:T(128)} %pad_add_fusion.info, bf16[4096,384]{1,0:T(8,128)(2,1)} %x_ref.7, bf16[8,1152,512]{2,1,0:T(8,128)(2,1)} %get-tuple-element.116.dqkv_ref, f32[8,384,512]{2,1,0:T(8,128)} %get-tuple-element.91.dh_ref, ...), custom_call_target="tpu_custom_call", output_to_operand_aliasing={{}: (6, {})} | custom-call | flops 8000000000 | bytes 16000000 | tf_op jit(solution)/shard_map/input/pallas_call | solution.py:612
  245.1 4.4 %collective-permute-start.10 = (bf16[768,384]{1,0:T(8,128)(2,1)S(1)}, bf16[768,384]{1,0:T(8,128)(2,1)S(1)}, u32[]{:S(2)}, u32[]{:S(2)}) collective-permute-start(bf16[768,384]{1,0:T(8,128)(2,1)S(1)} %constant_dynamic-update-slice_fusion.own_ref), channel_id=1, source_target_pairs={{0,2},{1,3},{2,0},{3,1},{4,6},{5,7},{6,4},{7,5},{8,10},{9,11},{10,... | collective-permute-start | bytes 1769480 | tf_op jit(solution)/shard_map/ppermute | solution.py:867
  252.9 15.5 %att_newton.1.mine_ref = f32[392,384]{1,0:T(8,128)} custom-call(s32[2]{0:T(128)} %pad_add_fusion.1.info, bf16[16,48,384]{2,1,0:T(8,128)(2,1)} %copy-done.3, bf16[16,48,384]{2,1,0:T(8,128)(2,1)} %copy-done.9), custom_call_target="tpu_custom_call" | custom-call | tf_op jit(solution)/shard_map/att_newton/pallas_call | solution.py:585
  269.3 15.4 %mlp_newton.1.mine_ref = f32[392,384]{1,0:T(8,128)} custom-call(s32[2]{0:T(128)} %pad_add_fusion.2.info, bf16[768,384]{1,0:T(8,128)(2,1)} %copy-done.5, bf16[768,384]{1,0:T(8,128)(2,1)} %copy-done.8), custom_call_target="tpu_custom_call" | custom-call | tf_op jit(solution)/shard_map/mlp_newton/pallas_call | solution.py:585
  287.4 2.6 att_update.1
  290.8 2.7 mlp_update.1
  (91 shorter events, 17.6 us)
Async XLA Ops:
  0.7 29.0 %copy-start.11 = (f32[8,384]{1,0:T(8,128)S(1)}, f32[8,384]{1,0:T(8,128)}, u32[]{:S(2)}) copy-start(f32[8,384]{1,0:T(8,128)} %row_ref.3) | copy-start | bytes 36868
  2.9 22.8 %all-to-all-start = ((bf16[16,36,384]{2,1,0:T(8,128)(2,1)}), bf16[16,36,384]{2,1,0:T(8,128)(2,1)S(1)}, u32[]{:S(2)}, u32[]{:S(2)}) async-start(bf16[16,36,384]{2,1,0:T(8,128)(2,1)} %get-tuple-element.78), calls=%async_computation | async-start | bytes 983040 | tf_op jit(solution)/shard_map/all_to_all | solution.py:679
  25.8 13.7 %copy-start.10 = (bf16[16,36,384]{2,1,0:T(8,128)(2,1)}, bf16[16,36,384]{2,1,0:T(8,128)(2,1)S(1)}, u32[]{:S(2)}) copy-start(bf16[16,36,384]{2,1,0:T(8,128)(2,1)S(1)} %all-to-all-done.refs_0_) | copy-start | bytes 1327108
  25.8 33.9 %all-to-all-start.1 = ((bf16[16,112,384]{2,1,0:T(8,128)(2,1)}), bf16[16,112,384]{2,1,0:T(8,128)(2,1)S(1)}, u32[]{:S(2)}, u32[]{:S(2)}) async-start(bf16[16,112,384]{2,1,0:T(8,128)(2,1)} %get-tuple-element.85), calls=%async_computation.1 | async-start | bytes 2752512 | tf_op jit(solution)/shard_map/all_to_all | solution.py:679
  29.6 9.9 %collective-permute-start = (bf16[16,36,384]{2,1,0:T(8,128)(2,1)S(1)}, bf16[16,36,384]{2,1,0:T(8,128)(2,1)S(1)}, u32[]{:S(2)}, u32[]{:S(2)}) collective-permute-start(bf16[16,36,384]{2,1,0:T(8,128)(2,1)S(1)} %all-to-all-done.refs_0_), channel_id=1, source_target_pairs={{0,1},{1,0},{2,3},{3,2},{4,5},{5,4},{6,7},{7,6},{8,9},{9,8},{10,11... | collective-permute-start | bytes 1327112 | tf_op jit(solution)/shard_map/ppermute | solution.py:682
  39.5 20.2 %copy-start.14 = (f32[1536]{0:T(1024)S(1)}, f32[1536]{0:T(1024)}, u32[]{:S(2)}) copy-start(f32[1536]{0:T(1024)} %param.21) | copy-start | bytes 18436
  59.7 5.4 %copy-start.4 = (bf16[16,112,384]{2,1,0:T(8,128)(2,1)}, bf16[16,112,384]{2,1,0:T(8,128)(2,1)S(1)}, u32[]{:S(2)}) copy-start(bf16[16,112,384]{2,1,0:T(8,128)(2,1)S(1)} %all-to-all-done.1.own_ref) | copy-start | bytes 4128772
  59.7 5.4 %collective-permute-start.1 = (bf16[16,112,384]{2,1,0:T(8,128)(2,1)S(1)}, bf16[16,112,384]{2,1,0:T(8,128)(2,1)S(1)}, u32[]{:S(2)}, u32[]{:S(2)}) collective-permute-start(bf16[16,112,384]{2,1,0:T(8,128)(2,1)S(1)} %all-to-all-done.1.own_ref), channel_id=1, source_target_pairs={{0,1},{1,0},{2,3},{3,2},{4,5},{5,4},{6,7},{7,6},{8,9},{9,8},{10,11... | collective-permute-start | bytes 4128776 | tf_op jit(solution)/shard_map/ppermute | solution.py:682
  65.1 1.4 copy-start.19
  101.6 30.4 %collective-permute-start.2 = (bf16[16,104,384]{2,1,0:T(8,128)(2,1)}, bf16[16,104,384]{2,1,0:T(8,128)(2,1)S(1)}, u32[]{:S(2)}, u32[]{:S(2)}) collective-permute-start(bf16[16,104,384]{2,1,0:T(8,128)(2,1)} %get-tuple-element.88), channel_id=1, source_target_pairs={{0,1},{1,0},{2,3},{3,2},{4,5},{5,4},{6,7},{7,6},{8,9},{9,8},{10,11... | collective-permute-start | bytes 3833864 | tf_op jit(solution)/shard_map/ppermute | solution.py:682
  123.6 8.4 %copy-start.2 = (f32[16,104,384]{2,1,0:T(8,128)S(1)}, f32[16,104,384]{2,1,0:T(8,128)}, u32[]{:S(2)}) copy-start(f32[16,104,384]{2,1,0:T(8,128)} %get-tuple-element.87) | copy-start | bytes 7667716
  133.3 43.2 %all-to-all-start.2 = ((bf16[16,104,384]{2,1,0:T(8,128)(2,1)}), bf16[16,104,384]{2,1,0:T(8,128)(2,1)S(1)}, u32[]{:S(2)}, u32[]{:S(2)}) async-start(bf16[16,104,384]{2,1,0:T(8,128)(2,1)} %add_convert_fusion), calls=%async_computation.2 | async-start | bytes 2555904 | tf_op jit(solution)/shard_map/all_to_all | solution.py:679
  176.5 11.6 %copy-start = (bf16[16,104,384]{2,1,0:T(8,128)(2,1)}, bf16[16,104,384]{2,1,0:T(8,128)(2,1)S(1)}, u32[]{:S(2)}) copy-start(bf16[16,104,384]{2,1,0:T(8,128)(2,1)S(1)} %all-to-all-done.2.got_ref) | copy-start | bytes 3833860
  176.5 2.3 collective-permute-start.3
  181.1 34.9 %all-to-all-start.3 = ((bf16[16,160,128]{2,1,0:T(8,128)(2,1)}), bf16[16,160,128]{2,1,0:T(8,128)(2,1)S(1)}, u32[]{:S(2)}, u32[]{:S(2)}) async-start(bf16[16,160,128]{2,1,0:T(8,128)(2,1)} %add_convert_fusion.1), calls=%async_computation.3 | async-start | bytes 1310720 | tf_op jit(solution)/shard_map/all_to_all | solution.py:679
  191.1 1.3 collective-permute-start.4
  192.4 16.3 %collective-permute-start.5 = (bf16[96,384]{1,0:T(8,128)(2,1)S(1)}, bf16[96,384]{1,0:T(8,128)(2,1)S(1)}, u32[]{:S(2)}, u32[]{:S(2)}) collective-permute-start(bf16[96,384]{1,0:T(8,128)(2,1)S(1)} %pad_maximum_fusion.2), channel_id=1, source_target_pairs={{0,16},{1,17},{2,18},{3,19},{4,20},{5,21},{6,22},{7,23},{8,24},{9,... | collective-permute-start | bytes 221192 | tf_op jit(solution)/shard_map/ppermute | solution.py:867
  208.7 10.2 %collective-permute-start.6 = (bf16[192,384]{1,0:T(8,128)(2,1)S(1)}, bf16[192,384]{1,0:T(8,128)(2,1)S(1)}, u32[]{:S(2)}, u32[]{:S(2)}) collective-permute-start(bf16[192,384]{1,0:T(8,128)(2,1)S(1)} %pad_maximum_fusion.1), channel_id=1, source_target_pairs={{0,8},{1,9},{2,10},{3,11},{4,12},{5,13},{6,14},{7,15},{8,0},{9,1},... | collective-permute-start | bytes 442376 | tf_op jit(solution)/shard_map/ppermute | solution.py:867
  219.0 16.8 %collective-permute-start.7 = (bf16[384,384]{1,0:T(8,128)(2,1)S(1)}, bf16[384,384]{1,0:T(8,128)(2,1)S(1)}, u32[]{:S(2)}, u32[]{:S(2)}) collective-permute-start(bf16[384,384]{1,0:T(8,128)(2,1)S(1)} %pad_maximum_fusion), channel_id=1, source_target_pairs={{0,4},{1,5},{2,6},{3,7},{4,0},{5,1},{6,2},{7,3},{8,12},{9,13},{10,... | collective-permute-start | bytes 884744 | tf_op jit(solution)/shard_map/ppermute | solution.py:867
  221.5 22.2 %all-to-all-start.4 = ((bf16[16,48,384]{2,1,0:T(8,128)(2,1)}), bf16[16,48,384]{2,1,0:T(8,128)(2,1)S(1)}, u32[]{:S(2)}, u32[]{:S(2)}) async-start(bf16[16,48,384]{2,1,0:T(8,128)(2,1)} %get-tuple-element.113), calls=%async_computation.4 | async-start | bytes 1179648 | tf_op jit(solution)/shard_map/all_to_all | solution.py:679
  235.9 9.2 %copy-start.5 = (bf16[768,384]{1,0:T(8,128)(2,1)}, bf16[768,384]{1,0:T(8,128)(2,1)S(1)}, u32[]{:S(2)}) copy-start(bf16[768,384]{1,0:T(8,128)(2,1)S(1)} %constant_dynamic-update-slice_fusion.own_ref) | copy-start | bytes 1769476
  235.9 14.7 %copy-start.17 = (f32[8,384]{1,0:T(8,128)S(1)}, f32[8,384]{1,0:T(8,128)}, u32[]{:S(2)}) copy-start(f32[8,384]{1,0:T(8,128)} %get-tuple-element.124) | copy-start | bytes 36868
  243.7 41.4 %copy-start.15 = (f32[1536]{0:T(1024)S(1)}, f32[1536]{0:T(1024)}, u32[]{:S(2)}) copy-start(f32[1536]{0:T(1024)} %param.21) | copy-start | bytes 18436
  243.7 42.0 %copy-start.18 = (f32[12,128]{1,0:T(8,128)S(1)}, f32[12,128]{1,0:T(8,128)}, u32[]{:S(2)}) copy-start(f32[12,128]{1,0:T(8,128)} %get-tuple-element.123) | copy-start | bytes 18436
  243.7 42.2 %copy-start.12 = (f32[8,384]{1,0:T(8,128)S(1)}, f32[8,384]{1,0:T(8,128)}, u32[]{:S(2)}) copy-start(f32[8,384]{1,0:T(8,128)} %row_ref.3) | copy-start | bytes 36868
  243.7 8.4 %copy-start.3 = (bf16[16,48,384]{2,1,0:T(8,128)(2,1)}, bf16[16,48,384]{2,1,0:T(8,128)(2,1)S(1)}, u32[]{:S(2)}) copy-start(bf16[16,48,384]{2,1,0:T(8,128)(2,1)S(1)} %all-to-all-done.4.own_ref) | copy-start | bytes 1769476
  243.7 8.3 %collective-permute-start.8 = (bf16[16,48,384]{2,1,0:T(8,128)(2,1)S(1)}, bf16[16,48,384]{2,1,0:T(8,128)(2,1)S(1)}, u32[]{:S(2)}, u32[]{:S(2)}) collective-permute-start(bf16[16,48,384]{2,1,0:T(8,128)(2,1)S(1)} %all-to-all-done.4.own_ref), channel_id=1, source_target_pairs={{0,1},{1,0},{2,3},{3,2},{4,5},{5,4},{6,7},{7,6},{8,9},{9,8},{10,11... | collective-permute-start | bytes 1769480 | tf_op jit(solution)/shard_map/ppermute | solution.py:682
  245.1 23.5 %collective-permute-start.10 = (bf16[768,384]{1,0:T(8,128)(2,1)S(1)}, bf16[768,384]{1,0:T(8,128)(2,1)S(1)}, u32[]{:S(2)}, u32[]{:S(2)}) collective-permute-start(bf16[768,384]{1,0:T(8,128)(2,1)S(1)} %constant_dynamic-update-slice_fusion.own_ref), channel_id=1, source_target_pairs={{0,2},{1,3},{2,0},{3,1},{4,6},{5,7},{6,4},{7,5},{8,10},{9,11},{10,... | collective-permute-start | bytes 1769480 | tf_op jit(solution)/shard_map/ppermute | solution.py:867
  250.8 42.7 %copy-start.16 = (f32[1536]{0:T(1024)}, f32[1536]{0:T(1024)S(1)}, u32[]{:S(2)}) copy-start(f32[1536]{0:T(1024)S(1)} %reshape.81) | copy-start | bytes 18436
  268.4 18.2 %collective-permute-start.9 = (f32[392,384]{1,0:T(8,128)}, f32[392,384]{1,0:T(8,128)S(1)}, u32[]{:S(2)}, u32[]{:S(2)}) collective-permute-start(f32[392,384]{1,0:T(8,128)} %att_newton.1.mine_ref), channel_id=1, source_target_pairs={{0,1},{1,0},{2,3},{3,2},{4,5},{5,4},{6,7},{7,6},{8,9},{9,8},{10,11... | collective-permute-start | bytes 1806344 | tf_op jit(solution)/shard_map/ppermute | solution.py:682
  284.8 5.2 %collective-permute-start.11 = (f32[392,384]{1,0:T(8,128)}, f32[392,384]{1,0:T(8,128)S(1)}, u32[]{:S(2)}, u32[]{:S(2)}) collective-permute-start(f32[392,384]{1,0:T(8,128)} %mlp_newton.1.mine_ref), channel_id=1, source_target_pairs={{0,1},{1,0},{2,3},{3,2},{4,5},{5,4},{6,7},{7,6},{8,9},{9,8},{10,11... | collective-permute-start | bytes 1806344 | tf_op jit(solution)/shard_map/ppermute | solution.py:682
  285.9 7.6 %copy-start.13 = (f32[8,384]{1,0:T(8,128)}, f32[8,384]{1,0:T(8,128)S(1)}, u32[]{:S(2)}) copy-start(f32[8,384]{1,0:T(8,128)S(1)} %get-tuple-element.139) | copy-start | bytes 36868
  (6 other events, 4.9 us)

commit v5 on v4

--- a/solution.py
+++ b/solution.py
@@ -493,67 +493,87 @@
     right_ref[:, 2 * width :] = high
 
 
-def newton_kernel(info, own_ref, other_ref, out_ref, whole_ref, gram_scr, poly_scr, pa, pb, sa, sb):
+def symmetric(left_ref, right_ref, out_ref):
+    width = out_ref.shape[0]
+    cut = (width // 256) * 256
+    if cut in (0, width):
+        out_ref[...] = nt(left_ref[...], right_ref[...])
+        return
+    made = nt(left_ref[...], right_ref[:cut, :])
+    out_ref[:, :cut] = made
+    out_ref[:cut, cut:] = made[cut:, :].T
+    out_ref[cut:, cut:] = nt(left_ref[cut:, :], right_ref[cut:, :])
+
+
+def newton_kernel(info, own_ref, other_ref, pool_ref, moved_ref, out_ref, whole, gram, poly, pa, pb, sa, sb):
     width = own_ref.shape[-1]
     eye = (
         lax.broadcasted_iota(jnp.int32, (width, width), 0)
         == lax.broadcasted_iota(jnp.int32, (width, width), 1)
     ).astype(f32)
-    gram = jnp.zeros((width, width), f32)
+    first = jnp.zeros((width, width), f32)
     for ref in (own_ref, other_ref):
-        if len(ref.shape) == 2:
-            part = ref[...]
-        else:
-            place = lax.broadcasted_iota(jnp.int32, ref.shape[1:], 0)
-            mine = (place < info[1]) == (info[0] == 0)
-            part = jnp.concatenate(
-                [jnp.where(mine, ref[index].astype(f32), 0.0) for index in range(ref.shape[0])], axis=0
-            ).astype(bf16)
-        gram += tn(part, part)
-    norm = lax.rsqrt(jnp.sum(gram * eye) + norm_eps)
-    out_ref[width:, :] = jnp.full((8, width), norm, f32)
-    gram_scr[...] = gram * (norm * norm)
-    whole_ref[...] = eye
-
-    def turn(index, carry):
-        store_parts(gram_scr[...], sa, sb)
-        gram = gram_scr[...]
-        poly = newton_a * eye + newton_b * gram + newton_c * nt(sa[...], sb[...])
-        store_parts(poly, pa, pb)
-        poly_scr[...] = nt(pa[...], sb[...])
-        store_parts(whole_ref[...], sa, sb)
-        whole_ref[...] = nt(pa[...], sb[...])
-
-        @pl.when(index < 4)
+        place = lax.broadcasted_iota(jnp.int32, ref.shape[1:], 0)
+        mine = (place < info[1]) == (info[0] == 0)
+        part = jnp.concatenate(
+            [jnp.where(mine, ref[index].astype(f32), 0.0) for index in range(ref.shape[0])], axis=0
+        ).astype(bf16)
+        first += tn(part, part)
+    second = tn(pool_ref[...], pool_ref[...]) + tn(moved_ref[...], moved_ref[...])
+    for index, made in enumerate((first, second)):
+        norm = lax.rsqrt(jnp.sum(made * eye) + norm_eps)
+        out_ref[index, width:, :] = jnp.full((8, width), norm, f32)
+        gram[index] = made * (norm * norm)
+        whole[index] = eye
+
+    def turn(step, carry):
+        for k in range(2):
+            store_parts(gram[k], sa.at[k], sb.at[k])
+        for k in range(2):
+            symmetric(sa.at[k], sb.at[k], poly.at[k])
+        for k in range(2):
+            made = newton_a * eye + newton_b * gram[k] + newton_c * poly[k]
+            store_parts(made, pa.at[k], pb.at[k])
+        for k in range(2):
+            symmetric(pa.at[k], sb.at[k], poly.at[k])
+        for k in range(2):
+            store_parts(whole[k], sa.at[k], sb.at[k])
+        for k in range(2):
+            symmetric(pa.at[k], sb.at[k], whole.at[k])
+
+        @pl.when(step < 4)
         def _():
-            store_parts(poly_scr[...], sa, sb)
-            gram_scr[...] = nt(sa[...], pb[...])
+            for k in range(2):
+                store_parts(poly[k], sa.at[k], sb.at[k])
+            for k in range(2):
+                symmetric(sa.at[k], pb.at[k], gram.at[k])
 
         return carry
 
     lax.fori_loop(0, 5, turn, 0)
-    out_ref[:width, :] = whole_ref[...]
-
-
-def update_kernel(
-    wide, info, mine_ref, theirs_ref, state_ref, wa_ref, wb_ref, ua_ref, ub_ref
-):
-    first = wa_ref.shape[0]
-    rows = state_ref.shape[0]
+    for index in range(2):
+        out_ref[index, :width, :] = whole[index]
+
+
+def update_kernel(wide, info, mine_ref, theirs_ref, sa_ref, sb_ref, *refs):
     ours = info[0] == 0
-    for low, high, w_ref, u_ref, columns, is_first in (
-        (0, first, wa_ref, ua_ref, wide[0], True),
-        (first, rows, wb_ref, ub_ref, wide[1], False),
-    ):
-        pick = ours if is_first else jnp.logical_not(ours)
-        width = mine_ref.shape[1]
-        whole = jnp.where(pick, mine_ref[:width, :], theirs_ref[:width, :])
-        norm = jnp.where(pick, mine_ref[width : width + 1, :], theirs_ref[width : width + 1, :])
-        state = state_ref[low:high, :] * norm
-        sh, sl = split_parts(state)
-        ph, pl_ = split_parts(whole)
-        ortho = nt(sh, ph) + (nt(sl, ph) + nt(sh, pl_))
-        u_ref[...] = w_ref[...] - (matrix_rate * 0.2 * math.sqrt(columns)) * ortho
+    width = mine_ref.shape[2]
+    for pair, state_ref in enumerate((sa_ref, sb_ref)):
+        low = 0
+        for side in range(2):
+            w_ref, u_ref = refs[2 * pair + side], refs[4 + 2 * pair + side]
+            high = low + w_ref.shape[0]
+            pick = ours if side == 0 else jnp.logical_not(ours)
+            whole = jnp.where(pick, mine_ref[pair, :width, :], theirs_ref[pair, :width, :])
+            norm = jnp.where(
+                pick, mine_ref[pair, width : width + 1, :], theirs_ref[pair, width : width + 1, :]
+            )
+            sh, sl = split_parts(state_ref[low:high, :] * norm)
+            ph, pl_ = split_parts(whole)
+            ortho = nt(sh, ph) + (nt(sl, ph) + nt(sh, pl_))
+            rate = matrix_rate * 0.2 * math.sqrt(wide[2 * pair + side])
+            u_ref[...] = w_ref[...] - rate * ortho
+            low = high
 
 
 def fixed(shape):
@@ -697,7 +717,7 @@
         normal_kernel, info, 0, groups, [(tokens, block_in), (None, vec)], [(deep_spec, wide, bf16)], [],
         "normal", 1e9,
     )[0]
-    wq_own = exchange(first)
+    wq_own = after(exchange(first), z1)
     wq_other = swap(wq_own)
     rest_own = exchange(after(second, wq_own))
 
@@ -825,26 +845,6 @@
             scalars=1,
         )(par.reshape(1), got, moment_a, moment_b)
 
-    def polynomials(own, other, first, name):
-        square = pltpu.VMEM((width, width), f32)
-        parts = pltpu.VMEM((width, 3 * width), bf16)
-        return small_call(
-            newton_kernel,
-            [((width + 8, width), f32)],
-            name + "_newton",
-            scalars=1,
-            scratch=[square, square, square, parts, parts, parts, parts],
-        )(jnp.stack([par, jnp.full((), first, jnp.int32)]), own, other)[0]
-
-    def updates(mine, theirs, state, weight_a, weight_b, name):
-        wide = (weight_a.shape[0] * devices, weight_b.shape[0] * devices)
-        return small_call(
-            functools.partial(update_kernel, wide),
-            [(weight_a.shape, f32), (weight_b.shape, f32)],
-            name + "_update",
-            scalars=1,
-        )(par.reshape(1), mine, theirs, state, weight_a, weight_b)
-
     swapped = swap(send_b)
     one = 1 if groups > 2 else groups
     done = back(0, one)
@@ -890,11 +890,21 @@
     dx = input_part(mid, groups, dqkv, after(info, pool), dx)
     own_a = after(own_a, dx[0])
     other_a = swap(own_a)
-    mine_a = polynomials(own_a, other_a, cq, "att")
-    theirs_a = swap(mine_a)
-    mine_b = polynomials(pool, after(moved, mine_a), cu, "mlp")
-    uq, up = updates(mine_a, after(theirs_a, mine_b), state_a, wq_s, wp_s, "att")
-    uu, ud = updates(mine_b, swap(mine_b), state_b, wu_s, wd_s, "mlp")
+    square = pltpu.VMEM((2, width, width), f32)
+    parts = pltpu.VMEM((2, width, 3 * width), bf16)
+    mine = small_call(
+        newton_kernel,
+        [((2, width + 8, width), f32)],
+        "newton",
+        scalars=1,
+        scratch=[square, square, square, parts, parts, parts, parts],
+    )(jnp.stack([par, jnp.full((), cq, jnp.int32)]), own_a, other_a, pool, moved)[0]
+    uq, up, uu, ud = small_call(
+        functools.partial(update_kernel, tuple(w.shape[0] * devices for w in turned)),
+        [(w.shape, f32) for w in turned],
+        "update",
+        scalars=1,
+    )(par.reshape(1), mine, swap(mine), state_a, state_b, *turned)
     out, dx = out[0], dx[0]
 
     vector_grad = jnp.concatenate([vector_a.reshape(4, width), vector_b[:4]], axis=0)

time: 294 us -> 286 us (0.973)
  Pallas kernels: 167 us -> 157 us
  waiting for transfers between devices: 34.3 us -> 39.5 us
    pallas_call x7 -> x5, Pallas kernels: 42.8 us -> 32.6 us  [call(): pl.pallas_call(kernel, in_specs=[smem] * scalars + [vmem] * (len(args) -...]
    all_to_all x5, starting transfers between devices: 38.6 us -> 47.3 us  [exchange(): return lax.all_to_all(x, 'dp', 0, 0, axis_index_groups=planes, tiled=True)]
    ppermute x8 -> x7, starting transfers between devices: 24 us -> 15.5 us  [swap(): return lax.ppermute(x, 'dp', pairs)]
    ppermute x4, waiting for transfers between devices: 5.26 us -> 10.1 us  [gather_step(): return lax.ppermute(pool, 'dp', [(i, i ^ bit) for i in range(devices)])]
  transfers between devices with their start and end apart: 17 -> 16, of which waited for: 6 -> 8; matrix products, arithmetic and copies ran while one was open for 3% -> 3% of each run, Pallas kernels for 43% -> 33%
where the time goes in v5:
time: 286 us
  Pallas kernels  157 us (55%)
  starting transfers between devices  70.4 us (25%)
  waiting for transfers between devices  39.5 us (14%)
  local copies, waits for them, and re-layouts  10.1 us (4%)
  other arithmetic  6.95 us (2%)
    pallas_call x10, Pallas kernels, grid_call(): pl.pallas_call(kernel, grid_spec=pltpu.PrefetchScalarGridSpec(num_scalar_...  124 us
    all_to_all x5, starting transfers between devices, exchange(): return lax.all_to_all(x, 'dp', 0, 0, axis_index_groups=planes, tiled=True)  47.3 us
    pallas_call x5, Pallas kernels, call(): pl.pallas_call(kernel, in_specs=[smem] * scalars + [vmem] * (len(args) -...  32.6 us
    all_to_all x5, waiting for transfers between devices, exchange(): return lax.all_to_all(x, 'dp', 0, 0, axis_index_groups=planes, tiled=True)  26.6 us
    ppermute x7, starting transfers between devices, swap(): return lax.ppermute(x, 'dp', pairs)  15.5 us
    ppermute x4, waiting for transfers between devices, gather_step(): return lax.ppermute(pool, 'dp', [(i, i ^ bit) for i in range(devices)])  10.1 us
    ppermute x4, starting transfers between devices, gather_step(): return lax.ppermute(pool, 'dp', [(i, i ^ bit) for i in range(devices)])  7.56 us
  transfers between devices with their start and end apart: 16, of which 8 were waited for; matrix products, arithmetic and copies ran while one was open for 3% of the time, Pallas kernels for 33%

profile of v5, /device:TPU:0, one launch (start us, length us, event | category | flops | bytes accessed | tf_op | source)
XLA Modules:
  0.0 286.2 jit_solution(14038160136481565515)
XLA Ops:
  0.7 2.3 prep.1
  2.9 8.3 %all-to-all-start = ((bf16[16,36,384]{2,1,0:T(8,128)(2,1)}), bf16[16,36,384]{2,1,0:T(8,128)(2,1)S(1)}, u32[]{:S(2)}, u32[]{:S(2)}) async-start(bf16[16,36,384]{2,1,0:T(8,128)(2,1)} %get-tuple-element.77), calls=%async_computation | async-start | bytes 983040 | tf_op jit(solution)/shard_map/all_to_all | solution.py:699
  12.5 2.3 broadcast_in_dim.4.vec_ref
  14.8 8.2 %normal.1.z_ref = bf16[8,384,512]{2,1,0:T(8,128)(2,1)} custom-call(s32[2]{0:T(128)} %pad_add_fusion.info, bf16[4096,384]{1,0:T(8,128)(2,1)} %x_ref.7, f32[8,384,128]{2,1,0:T(8,128)} %broadcast_in_dim.4.vec_ref), custom_call_target="tpu_custom_call" | custom-call | flops 8000000000 | bytes 32000000 | tf_op jit(solution)/shard_map/normal/pallas_call | solution.py:632
  23.0 2.7 all-to-all-done.refs_0_
  25.8 4.3 %all-to-all-start.1 = ((bf16[16,112,384]{2,1,0:T(8,128)(2,1)}), bf16[16,112,384]{2,1,0:T(8,128)(2,1)S(1)}, u32[]{:S(2)}, u32[]{:S(2)}) async-start(bf16[16,112,384]{2,1,0:T(8,128)(2,1)} %get-tuple-element.85), calls=%async_computation.1 | async-start | bytes 2752512 | tf_op jit(solution)/shard_map/all_to_all | solution.py:699
  30.9 14.4 %attend.2 = (bf16[8,1152,512]{2,1,0:T(8,128)(2,1)}, bf16[8,3072,256]{2,1,0:T(8,128)(2,1)}, bf16[8,384,512]{2,1,0:T(8,128)(2,1)}, bf16[1152,384]{1,0:T(8,128)(2,1)}) custom-call(s32[2]{0:T(128)} %pad_add_fusion.info, bf16[8,384,512]{2,1,0:T(8,128)(2,1)} %normal.1.z_ref, f32[8,384,128]{2,1,0:T(8,128)} %broadcast_in_dim.4.vec_ref, ...), custom_call_target="tpu_custom_call" | custom-call | flops 24000000000 | bytes 24000000 | tf_op jit(solution)/shard_map/attend/pallas_call | solution.py:632
  45.4 15.6 %all-to-all-done.1.own_ref = bf16[16,112,384]{2,1,0:T(8,128)(2,1)S(1)} async-done(((bf16[16,112,384]{2,1,0:T(8,128)(2,1)}), bf16[16,112,384]{2,1,0:T(8,128)(2,1)S(1)}, u32[]{:S(2)}, u32[]{:S(2)}) %all-to-all-start.1) | async-done | bytes 1376288 | tf_op jit(solution)/shard_map/all_to_all | solution.py:699
  61.2 5.2 %attend.3 = (bf16[8,1152,512]{2,1,0:T(8,128)(2,1)}, bf16[8,3072,256]{2,1,0:T(8,128)(2,1)}, bf16[8,384,512]{2,1,0:T(8,128)(2,1)}) custom-call(s32[2]{0:T(128)} %pad_add_fusion.info, bf16[8,384,512]{2,1,0:T(8,128)(2,1)} %normal.1.z_ref, f32[8,384,128]{2,1,0:T(8,128)} %broadcast_in_dim.4.vec_ref, ...), custom_call_target="tpu_custom_call", output_to_operand_aliasing={{0}: (4, {}), {1}: (5, {}), {2}: (6, {})} | custom-call | flops 8000000000 | bytes 8000000 | tf_op jit(solution)/shard_map/attend/pallas_call | solution.py:632
  67.8 35.0 %mlp.1 = (f32[8,384,512]{2,1,0:T(8,128)}, bf16[8,1536,512]{2,1,0:T(8,128)(2,1)}, f32[8,384,512]{2,1,0:T(8,128)}, f32[384,384]{1,0:T(8,128)}, bf16[384,384]{1,0:T...) custom-call(s32[2]{0:T(128)} %pad_add_fusion.info, ...), custom_call_target="tpu_custom_call" | custom-call | flops 80000000000 | bytes 32000000 | tf_op jit(solution)/shard_map/mlp/pallas_call | solution.py:632
  102.8 15.4 %collective-permute-start.2 = (bf16[16,104,384]{2,1,0:T(8,128)(2,1)}, bf16[16,104,384]{2,1,0:T(8,128)(2,1)S(1)}, u32[]{:S(2)}, u32[]{:S(2)}) collective-permute-start(bf16[16,104,384]{2,1,0:T(8,128)(2,1)} %get-tuple-element.88), channel_id=1, source_target_pairs={{0,1},{1,0},{2,3},{3,2},{4,5},{5,4},{6,7},{7,6},{8,9},{9,8},{10,11... | collective-permute-start | bytes 3833864 | tf_op jit(solution)/shard_map/ppermute | solution.py:702
  118.1 8.6 %back.2 = (bf16[8,1152,512]{2,1,0:T(8,128)(2,1)}, f32[1152,384]{1,0:T(8,128)}, f32[3,384,128]{2,1,0:T(8,128)}) custom-call(s32[2]{0:T(128)} %pad_add_fusion.info, bf16[8,384,512]{2,1,0:T(8,128)(2,1)} %normal.1.z_ref, bf16[8,1152,512]{2,1,0:T(8,128)(2,1)} %get-tuple-element.89.qkv_ref, bf16[8,3072,256]{2,1,0:T(8,128)(2,1)} %get-tuple-element.90.att_ref, ...), custom_call_target="tpu_custom_call" | custom-call | flops 6000000000 | bytes 4000000 | tf_op jit(solution)/shard_map/back/pallas_call | solution.py:632
  128.0 21.5 %all-to-all-start.2 = ((bf16[16,104,384]{2,1,0:T(8,128)(2,1)}), bf16[16,104,384]{2,1,0:T(8,128)(2,1)S(1)}, u32[]{:S(2)}, u32[]{:S(2)}) async-start(bf16[16,104,384]{2,1,0:T(8,128)(2,1)} %add_convert_fusion), calls=%async_computation.2 | async-start | bytes 2555904 | tf_op jit(solution)/shard_map/all_to_all | solution.py:699
  149.6 20.6 %back.3 = (bf16[8,1152,512]{2,1,0:T(8,128)(2,1)}, f32[16,160,128]{2,1,0:T(8,128)}, bf16[16,160,128]{2,1,0:T(8,128)(2,1)}) custom-call(s32[2]{0:T(128)} %pad_add_fusion.info, bf16[8,384,512]{2,1,0:T(8,128)(2,1)} %normal.1.z_ref, bf16[8,1152,512]{2,1,0:T(8,128)(2,1)} %get-tuple-element.89.qkv_ref, ...), custom_call_target="tpu_custom_call", output_to_operand_aliasing={{0}: (11, {})} | custom-call | flops 41999998976 | bytes 28000000 | tf_op jit(solution)/shard_map/back/pallas_call | solution.py:632
  170.2 8.2 %all-to-all-done.2.got_ref = bf16[16,104,384]{2,1,0:T(8,128)(2,1)S(1)} async-done(((bf16[16,104,384]{2,1,0:T(8,128)(2,1)}), bf16[16,104,384]{2,1,0:T(8,128)(2,1)S(1)}, u32[]{:S(2)}, u32[]{:S(2)}) %all-to-all-start.2) | async-done | bytes 1277984 | tf_op jit(solution)/shard_map/all_to_all | solution.py:699
  178.4 2.3 collective-permute-done.3
  180.8 2.3 add_convert_fusion.1
  183.1 7.0 %all-to-all-start.3 = ((bf16[16,160,128]{2,1,0:T(8,128)(2,1)}), bf16[16,160,128]{2,1,0:T(8,128)(2,1)S(1)}, u32[]{:S(2)}, u32[]{:S(2)}) async-start(bf16[16,160,128]{2,1,0:T(8,128)(2,1)} %add_convert_fusion.1), calls=%async_computation.3 | async-start | bytes 1310720 | tf_op jit(solution)/shard_map/all_to_all | solution.py:699
  190.1 2.3 mlp_state.1
  194.4 2.9 %collective-permute-start.5 = (bf16[96,384]{1,0:T(8,128)(2,1)S(1)}, bf16[96,384]{1,0:T(8,128)(2,1)S(1)}, u32[]{:S(2)}, u32[]{:S(2)}) collective-permute-start(bf16[96,384]{1,0:T(8,128)(2,1)S(1)} %pad_maximum_fusion.2), channel_id=1, source_target_pairs={{0,16},{1,17},{2,18},{3,19},{4,20},{5,21},{6,22},{7,23},{8,24},{9,... | collective-permute-start | bytes 221192 | tf_op jit(solution)/shard_map/ppermute | solution.py:867
  197.3 8.2 %out.2.refs_0_ = f32[4096,384]{1,0:T(8,128)} custom-call(s32[2]{0:T(128)} %pad_add_fusion.info, f32[8,384,512]{2,1,0:T(8,128)} %get-tuple-element.107.h_ref, bf16[8,1536,512]{2,1,0:T(8,128)(2,1)} %get-tuple-element.108.act_ref, bf16[384,1536]{1,0:T(8,128)(2,1)} %get-tuple-element.109.wdn_ref, f32[8,384,128]{2,1,0:T(8,128)} %broadcast_in_dim.4.vec_ref), custom_call_target="tpu_custom_call" | custom-call | flops 6000000000 | bytes 16000000 | tf_op jit(solution)/shard_map/out/pallas_call | solution.py:632
  205.5 5.2 %collective-permute-done.5 = bf16[96,384]{1,0:T(8,128)(2,1)S(1)} collective-permute-done((bf16[96,384]{1,0:T(8,128)(2,1)S(1)}, bf16[96,384]{1,0:T(8,128)(2,1)S(1)}, u32[]{:S(2)}, u32[]{:S(2)}) %collective-permute-start.5) | collective-permute-done | bytes 73760 | tf_op jit(solution)/shard_map/ppermute | solution.py:867
  210.8 7.2 %out.3 = f32[4096,384]{1,0:T(8,128)} custom-call(s32[2]{0:T(128)} %pad_add_fusion.info, f32[8,384,512]{2,1,0:T(8,128)} %get-tuple-element.107.h_ref, bf16[8,1536,512]{2,1,0:T(8,128)(2,1)} %get-tuple-element.108.act_ref, bf16[384,1536]{1,0:T(8,128)(2,1)} %get-tuple-element.109.wdn_ref, ...), custom_call_target="tpu_custom_call", output_to_operand_aliasing={{}: (5, {})} | custom-call | flops 6000000000 | bytes 16000000 | tf_op jit(solution)/shard_map/out/pallas_call | solution.py:632
  218.8 2.1 att_state.1
  221.0 1.5 collective-permute-start.7
  222.5 6.2 %all-to-all-start.4 = ((bf16[16,48,384]{2,1,0:T(8,128)(2,1)}), bf16[16,48,384]{2,1,0:T(8,128)(2,1)S(1)}, u32[]{:S(2)}, u32[]{:S(2)}) async-start(bf16[16,48,384]{2,1,0:T(8,128)(2,1)} %get-tuple-element.113), calls=%async_computation.4 | async-start | bytes 1179648 | tf_op jit(solution)/shard_map/all_to_all | solution.py:699
  228.7 9.1 %input.2.refs_0_ = f32[4096,384]{1,0:T(8,128)} custom-call(s32[2]{0:T(128)} %pad_add_fusion.info, bf16[4096,384]{1,0:T(8,128)(2,1)} %x_ref.7, bf16[8,1152,512]{2,1,0:T(8,128)(2,1)} %get-tuple-element.116.dqkv_ref, f32[8,384,512]{2,1,0:T(8,128)} %get-tuple-element.91.dh_ref, bf16[1152,384]{1,0:T(8,128)(2,1)} %get-tuple-element.79.refs_0_.wq_ref, ...), custom_call_target="tpu_custom_call" | custom-call | flops 8000000000 | bytes 16000000 | tf_op jit(solution)/shard_map/input/pallas_call | solution.py:632
  237.9 3.1 %collective-permute-start.9 = (bf16[768,384]{1,0:T(8,128)(2,1)S(1)}, bf16[768,384]{1,0:T(8,128)(2,1)S(1)}, u32[]{:S(2)}, u32[]{:S(2)}) collective-permute-start(bf16[768,384]{1,0:T(8,128)(2,1)S(1)} %constant_dynamic-update-slice_fusion.pool_ref), channel_id=1, source_target_pairs={{0,2},{1,3},{2,0},{3,1},{4,6},{5,7},{6,4},{7,5},{8,10},{9,11},{10,... | collective-permute-start | bytes 1769480 | tf_op jit(solution)/shard_map/ppermute | solution.py:867
  240.9 7.7 %input.3 = f32[4096,384]{1,0:T(8,128)} custom-call(s32[2]{0:T(128)} %pad_add_fusion.info, bf16[4096,384]{1,0:T(8,128)(2,1)} %x_ref.7, bf16[8,1152,512]{2,1,0:T(8,128)(2,1)} %get-tuple-element.116.dqkv_ref, f32[8,384,512]{2,1,0:T(8,128)} %get-tuple-element.91.dh_ref, ...), custom_call_target="tpu_custom_call", output_to_operand_aliasing={{}: (6, {})} | custom-call | flops 8000000000 | bytes 16000000 | tf_op jit(solution)/shard_map/input/pallas_call | solution.py:632
  249.4 4.8 %collective-permute-done.9.moved_ref = bf16[768,384]{1,0:T(8,128)(2,1)S(1)} collective-permute-done((bf16[768,384]{1,0:T(8,128)(2,1)S(1)}, bf16[768,384]{1,0:T(8,128)(2,1)S(1)}, u32[]{:S(2)}, u32[]{:S(2)}) %collective-permute-start.9) | collective-permute-done | bytes 589856 | tf_op jit(solution)/shard_map/ppermute | solution.py:867
  255.9 22.3 %newton.1.mine_ref = f32[2,392,384]{2,1,0:T(8,128)} custom-call(s32[2]{0:T(128)} %pad_add_fusion.1.info, bf16[16,48,384]{2,1,0:T(8,128)(2,1)} %copy-done.3, bf16[16,48,384]{2,1,0:T(8,128)(2,1)} %copy-done.8, bf16[768,384]{1,0:T(8,128)(2,1)} %copy-done.6, bf16[768,384]{1,0:T(8,128)(2,1)} %copy-done.7), custom_call_target="tpu_custom_call" | custom-call | tf_op jit(solution)/shard_map/newton/pallas_call | solution.py:605
  282.3 3.7 %update.1 = (f32[36,384]{1,0:T(8,128)}, f32[12,384]{1,0:T(8,128)}, f32[48,384]{1,0:T(8,128)}, f32[48,384]{1,0:T(8,128)}) custom-call(s32[1]{0:T(128)} %bitcast.info, f32[2,392,384]{2,1,0:T(8,128)} %newton.1.mine_ref, f32[2,392,384]{2,1,0:T(8,128)} %copy-done.5, f32[48,384]{1,0:T(8,128)} %get-tuple-element.126.sa_ref, f32[96,384]{1,0:T(8,128)} %get-tuple-element.127.sb_ref, ...), custom_call_target="tpu_custom_call" | custom-call | tf_op jit(solution)/shard_map/update/pallas_call | solution.py:605
  (82 shorter events, 13.2 us)
Async XLA Ops:
  2.9 22.8 %all-to-all-start = ((bf16[16,36,384]{2,1,0:T(8,128)(2,1)}), bf16[16,36,384]{2,1,0:T(8,128)(2,1)S(1)}, u32[]{:S(2)}, u32[]{:S(2)}) async-start(bf16[16,36,384]{2,1,0:T(8,128)(2,1)} %get-tuple-element.77), calls=%async_computation | async-start | bytes 983040 | tf_op jit(solution)/shard_map/all_to_all | solution.py:699
  25.8 4.4 %copy-start.9 = (bf16[16,36,384]{2,1,0:T(8,128)(2,1)}, bf16[16,36,384]{2,1,0:T(8,128)(2,1)S(1)}, u32[]{:S(2)}) copy-start(bf16[16,36,384]{2,1,0:T(8,128)(2,1)S(1)} %all-to-all-done.refs_0_) | copy-start | bytes 1327108
  25.8 4.4 %collective-permute-start = (bf16[16,36,384]{2,1,0:T(8,128)(2,1)S(1)}, bf16[16,36,384]{2,1,0:T(8,128)(2,1)S(1)}, u32[]{:S(2)}, u32[]{:S(2)}) collective-permute-start(bf16[16,36,384]{2,1,0:T(8,128)(2,1)S(1)} %all-to-all-done.refs_0_), channel_id=1, source_target_pairs={{0,1},{1,0},{2,3},{3,2},{4,5},{5,4},{6,7},{7,6},{8,9},{9,8},{10,11... | collective-permute-start | bytes 1327112 | tf_op jit(solution)/shard_map/ppermute | solution.py:702
  25.8 35.2 %all-to-all-start.1 = ((bf16[16,112,384]{2,1,0:T(8,128)(2,1)}), bf16[16,112,384]{2,1,0:T(8,128)(2,1)S(1)}, u32[]{:S(2)}, u32[]{:S(2)}) async-start(bf16[16,112,384]{2,1,0:T(8,128)(2,1)} %get-tuple-element.85), calls=%async_computation.1 | async-start | bytes 2752512 | tf_op jit(solution)/shard_map/all_to_all | solution.py:699
  30.1 30.9 %copy-start.12 = (f32[1536]{0:T(1024)S(1)}, f32[1536]{0:T(1024)}, u32[]{:S(2)}) copy-start(f32[1536]{0:T(1024)} %param.21) | copy-start | bytes 18436
  61.0 5.4 %copy-start.4 = (bf16[16,112,384]{2,1,0:T(8,128)(2,1)}, bf16[16,112,384]{2,1,0:T(8,128)(2,1)S(1)}, u32[]{:S(2)}) copy-start(bf16[16,112,384]{2,1,0:T(8,128)(2,1)S(1)} %all-to-all-done.1.own_ref) | copy-start | bytes 4128772
  61.0 5.4 %collective-permute-start.1 = (bf16[16,112,384]{2,1,0:T(8,128)(2,1)S(1)}, bf16[16,112,384]{2,1,0:T(8,128)(2,1)S(1)}, u32[]{:S(2)}, u32[]{:S(2)}) collective-permute-start(bf16[16,112,384]{2,1,0:T(8,128)(2,1)S(1)} %all-to-all-done.1.own_ref), channel_id=1, source_target_pairs={{0,1},{1,0},{2,3},{3,2},{4,5},{5,4},{6,7},{7,6},{8,9},{9,8},{10,11... | collective-permute-start | bytes 4128776 | tf_op jit(solution)/shard_map/ppermute | solution.py:702
  66.4 1.4 copy-start.17
  102.8 24.0 %collective-permute-start.2 = (bf16[16,104,384]{2,1,0:T(8,128)(2,1)}, bf16[16,104,384]{2,1,0:T(8,128)(2,1)S(1)}, u32[]{:S(2)}, u32[]{:S(2)}) collective-permute-start(bf16[16,104,384]{2,1,0:T(8,128)(2,1)} %get-tuple-element.88), channel_id=1, source_target_pairs={{0,1},{1,0},{2,3},{3,2},{4,5},{5,4},{6,7},{7,6},{8,9},{9,8},{10,11... | collective-permute-start | bytes 3833864 | tf_op jit(solution)/shard_map/ppermute | solution.py:702
  118.1 8.6 %copy-start.2 = (f32[16,104,384]{2,1,0:T(8,128)S(1)}, f32[16,104,384]{2,1,0:T(8,128)}, u32[]{:S(2)}) copy-start(f32[16,104,384]{2,1,0:T(8,128)} %get-tuple-element.87) | copy-start | bytes 7667716
  128.0 50.4 %all-to-all-start.2 = ((bf16[16,104,384]{2,1,0:T(8,128)(2,1)}), bf16[16,104,384]{2,1,0:T(8,128)(2,1)S(1)}, u32[]{:S(2)}, u32[]{:S(2)}) async-start(bf16[16,104,384]{2,1,0:T(8,128)(2,1)} %add_convert_fusion), calls=%async_computation.2 | async-start | bytes 2555904 | tf_op jit(solution)/shard_map/all_to_all | solution.py:699
  178.4 11.6 %copy-start = (bf16[16,104,384]{2,1,0:T(8,128)(2,1)}, bf16[16,104,384]{2,1,0:T(8,128)(2,1)S(1)}, u32[]{:S(2)}) copy-start(bf16[16,104,384]{2,1,0:T(8,128)(2,1)S(1)} %all-to-all-done.2.got_ref) | copy-start | bytes 3833860
  178.4 2.3 collective-permute-start.3
  183.1 34.9 %all-to-all-start.3 = ((bf16[16,160,128]{2,1,0:T(8,128)(2,1)}), bf16[16,160,128]{2,1,0:T(8,128)(2,1)S(1)}, u32[]{:S(2)}, u32[]{:S(2)}) async-start(bf16[16,160,128]{2,1,0:T(8,128)(2,1)} %add_convert_fusion.1), calls=%async_computation.3 | async-start | bytes 1310720 | tf_op jit(solution)/shard_map/all_to_all | solution.py:699
  193.1 1.3 collective-permute-start.4
  194.4 16.3 %collective-permute-start.5 = (bf16[96,384]{1,0:T(8,128)(2,1)S(1)}, bf16[96,384]{1,0:T(8,128)(2,1)S(1)}, u32[]{:S(2)}, u32[]{:S(2)}) collective-permute-start(bf16[96,384]{1,0:T(8,128)(2,1)S(1)} %pad_maximum_fusion.2), channel_id=1, source_target_pairs={{0,16},{1,17},{2,18},{3,19},{4,20},{5,21},{6,22},{7,23},{8,24},{9,... | collective-permute-start | bytes 221192 | tf_op jit(solution)/shard_map/ppermute | solution.py:867
  210.7 10.2 %collective-permute-start.6 = (bf16[192,384]{1,0:T(8,128)(2,1)S(1)}, bf16[192,384]{1,0:T(8,128)(2,1)S(1)}, u32[]{:S(2)}, u32[]{:S(2)}) collective-permute-start(bf16[192,384]{1,0:T(8,128)(2,1)S(1)} %pad_maximum_fusion.1), channel_id=1, source_target_pairs={{0,8},{1,9},{2,10},{3,11},{4,12},{5,13},{6,14},{7,15},{8,0},{9,1},... | collective-permute-start | bytes 442376 | tf_op jit(solution)/shard_map/ppermute | solution.py:867
  218.0 0.8 copy-start.1
  221.0 16.8 %collective-permute-start.7 = (bf16[384,384]{1,0:T(8,128)(2,1)S(1)}, bf16[384,384]{1,0:T(8,128)(2,1)S(1)}, u32[]{:S(2)}, u32[]{:S(2)}) collective-permute-start(bf16[384,384]{1,0:T(8,128)(2,1)S(1)} %pad_maximum_fusion), channel_id=1, source_target_pairs={{0,4},{1,5},{2,6},{3,7},{4,0},{5,1},{6,2},{7,3},{8,12},{9,13},{10,... | collective-permute-start | bytes 884744 | tf_op jit(solution)/shard_map/ppermute | solution.py:867
  222.5 26.2 %all-to-all-start.4 = ((bf16[16,48,384]{2,1,0:T(8,128)(2,1)}), bf16[16,48,384]{2,1,0:T(8,128)(2,1)S(1)}, u32[]{:S(2)}, u32[]{:S(2)}) async-start(bf16[16,48,384]{2,1,0:T(8,128)(2,1)} %get-tuple-element.113), calls=%async_computation.4 | async-start | bytes 1179648 | tf_op jit(solution)/shard_map/all_to_all | solution.py:699
  237.8 10.8 %copy-start.6 = (bf16[768,384]{1,0:T(8,128)(2,1)}, bf16[768,384]{1,0:T(8,128)(2,1)S(1)}, u32[]{:S(2)}) copy-start(bf16[768,384]{1,0:T(8,128)(2,1)S(1)} %constant_dynamic-update-slice_fusion.pool_ref) | copy-start | bytes 1769476
  237.9 16.4 %collective-permute-start.9 = (bf16[768,384]{1,0:T(8,128)(2,1)S(1)}, bf16[768,384]{1,0:T(8,128)(2,1)S(1)}, u32[]{:S(2)}, u32[]{:S(2)}) collective-permute-start(bf16[768,384]{1,0:T(8,128)(2,1)S(1)} %constant_dynamic-update-slice_fusion.pool_ref), channel_id=1, source_target_pairs={{0,2},{1,3},{2,0},{3,1},{4,6},{5,7},{6,4},{7,5},{8,10},{9,11},{10,... | collective-permute-start | bytes 1769480 | tf_op jit(solution)/shard_map/ppermute | solution.py:867
  248.6 29.6 %copy-start.15 = (f32[8,384]{1,0:T(8,128)S(1)}, f32[8,384]{1,0:T(8,128)}, u32[]{:S(2)}) copy-start(f32[8,384]{1,0:T(8,128)} %get-tuple-element.124) | copy-start | bytes 36868
  248.6 31.1 %copy-start.13 = (f32[1536]{0:T(1024)S(1)}, f32[1536]{0:T(1024)}, u32[]{:S(2)}) copy-start(f32[1536]{0:T(1024)} %param.21) | copy-start | bytes 18436
  248.6 31.7 %copy-start.16 = (f32[12,128]{1,0:T(8,128)S(1)}, f32[12,128]{1,0:T(8,128)}, u32[]{:S(2)}) copy-start(f32[12,128]{1,0:T(8,128)} %get-tuple-element.123) | copy-start | bytes 18436
  248.6 31.8 %copy-start.10 = (f32[8,384]{1,0:T(8,128)S(1)}, f32[8,384]{1,0:T(8,128)}, u32[]{:S(2)}) copy-start(f32[8,384]{1,0:T(8,128)} %row_ref.3) | copy-start | bytes 36868
  248.7 5.5 %copy-start.3 = (bf16[16,48,384]{2,1,0:T(8,128)(2,1)}, bf16[16,48,384]{2,1,0:T(8,128)(2,1)S(1)}, u32[]{:S(2)}) copy-start(bf16[16,48,384]{2,1,0:T(8,128)(2,1)S(1)} %all-to-all-done.4.own_ref) | copy-start | bytes 1769476
  248.7 5.5 %collective-permute-start.8 = (bf16[16,48,384]{2,1,0:T(8,128)(2,1)S(1)}, bf16[16,48,384]{2,1,0:T(8,128)(2,1)S(1)}, u32[]{:S(2)}, u32[]{:S(2)}) collective-permute-start(bf16[16,48,384]{2,1,0:T(8,128)(2,1)S(1)} %all-to-all-done.4.own_ref), channel_id=1, source_target_pairs={{0,1},{1,0},{2,3},{3,2},{4,5},{5,4},{6,7},{7,6},{8,9},{9,8},{10,11... | collective-permute-start | bytes 1769480 | tf_op jit(solution)/shard_map/ppermute | solution.py:702
  278.2 3.1 %collective-permute-start.10 = (f32[2,392,384]{2,1,0:T(8,128)}, f32[2,392,384]{2,1,0:T(8,128)S(1)}, u32[]{:S(2)}, u32[]{:S(2)}) collective-permute-start(f32[2,392,384]{2,1,0:T(8,128)} %newton.1.mine_ref), channel_id=1, source_target_pairs={{0,1},{1,0},{2,3},{3,2},{4,5},{5,4},{6,7},{7,6},{8,9},{9,8},{10,11... | collective-permute-start | bytes 3612680 | tf_op jit(solution)/shard_map/ppermute | solution.py:702
  278.4 7.6 %copy-start.14 = (f32[1536]{0:T(1024)}, f32[1536]{0:T(1024)S(1)}, u32[]{:S(2)}) copy-start(f32[1536]{0:T(1024)S(1)} %reshape.80) | copy-start | bytes 18436
  280.4 5.5 %copy-start.11 = (f32[8,384]{1,0:T(8,128)}, f32[8,384]{1,0:T(8,128)S(1)}, u32[]{:S(2)}) copy-start(f32[8,384]{1,0:T(8,128)S(1)} %get-tuple-element.137) | copy-start | bytes 36868
  281.3 1.1 copy-start.5
  (3 other events, 2.4 us)

commit v6 on v5

--- a/solution.py
+++ b/solution.py
@@ -740,7 +740,7 @@
             "attend", 4e9, before,
         )
 
-    early = groups - 2 if groups > 2 else groups
+    early = groups
     qkv, att, attn, wq = attend(0, early, (wq_own, wq_other))
     rest_own = after(rest_own, attn)
     rest_other = swap(rest_own)

time: 286 us -> 281 us (0.983)
  Pallas kernels: 157 us -> 200 us
  starting transfers between devices: 70.4 us -> 38.3 us
  waiting for transfers between devices: 39.5 us -> 21.5 us
    pallas_call x10 -> x9, Pallas kernels: 124 us -> 168 us  [grid_call(): pl.pallas_call(kernel, grid_spec=pltpu.PrefetchScalarGridSpec(num_scalar_...]
    all_to_all x5, waiting for transfers between devices: 26.6 us -> 9.7 us  [exchange(): return lax.all_to_all(x, 'dp', 0, 0, axis_index_groups=planes, tiled=True)]
    ppermute x7, starting transfers between devices: 15.5 us -> 0.22 us  [swap(): return lax.ppermute(x, 'dp', pairs)]
    all_to_all x5, starting transfers between devices: 47.3 us -> 32.5 us  [exchange(): return lax.all_to_all(x, 'dp', 0, 0, axis_index_groups=planes, tiled=True)]
    ppermute x4, waiting for transfers between devices: 10.1 us -> 5.99 us  [gather_step(): return lax.ppermute(pool, 'dp', [(i, i ^ bit) for i in range(devices)])]
    ppermute x7, waiting for transfers between devices: 2.87 us -> 5.79 us  [swap(): return lax.ppermute(x, 'dp', pairs)]
  transfers between devices with their start and end apart: 16 -> 16, of which waited for: 8 -> 9; matrix products, arithmetic and copies ran while one was open for 3% -> 3% of each run, Pallas kernels for 33% -> 40%
where the time goes in v6:
time: 281 us; the launch traced here: 280 us
  Pallas kernels  200 us (71%)
  starting transfers between devices  38.3 us (14%)
  waiting for transfers between devices  21.5 us (8%)
  local copies, waits for them, and re-layouts  10 us (4%)
  other arithmetic  6.93 us (2%)
    pallas_call x9, Pallas kernels, grid_call(): pl.pallas_call(kernel, grid_spec=pltpu.PrefetchScalarGridSpec(num_scalar_...  168 us
    pallas_call x5, Pallas kernels, call(): pl.pallas_call(kernel, in_specs=[smem] * scalars + [vmem] * (len(args) -...  32.6 us
    all_to_all x5, starting transfers between devices, exchange(): return lax.all_to_all(x, 'dp', 0, 0, axis_index_groups=planes, tiled=True)  32.5 us
    all_to_all x5, waiting for transfers between devices, exchange(): return lax.all_to_all(x, 'dp', 0, 0, axis_index_groups=planes, tiled=True)  9.7 us
    ppermute x4, waiting for transfers between devices, gather_step(): return lax.ppermute(pool, 'dp', [(i, i ^ bit) for i in range(devices)])  5.99 us
    ppermute x7, waiting for transfers between devices, swap(): return lax.ppermute(x, 'dp', pairs)  5.79 us
  transfers between devices with their start and end apart: 16, of which 9 were waited for; matrix products, arithmetic and copies ran while one was open for 3% of the time, Pallas kernels for 40%

profile of v6, /device:TPU:0, one launch (start us, length us, event | category | flops | bytes accessed | tf_op | source)
XLA Modules:
  0.0 279.6 jit_solution(4823719681078911517)
XLA Ops:
  0.7 2.3 prep.1
  2.9 8.3 %all-to-all-start = ((bf16[16,36,384]{2,1,0:T(8,128)(2,1)}), bf16[16,36,384]{2,1,0:T(8,128)(2,1)S(1)}, u32[]{:S(2)}, u32[]{:S(2)}) async-start(bf16[16,36,384]{2,1,0:T(8,128)(2,1)} %get-tuple-element.74), calls=%async_computation | async-start | bytes 983040 | tf_op jit(solution)/shard_map/all_to_all | solution.py:699
  12.5 2.3 broadcast_in_dim.4.vec_ref
  14.8 9.1 %normal.1.z_ref = bf16[8,384,512]{2,1,0:T(8,128)(2,1)} custom-call(s32[2]{0:T(128)} %pad_add_fusion.info, bf16[4096,384]{1,0:T(8,128)(2,1)} %x_ref.7, f32[8,384,128]{2,1,0:T(8,128)} %broadcast_in_dim.4.vec_ref), custom_call_target="tpu_custom_call" | custom-call | flops 8000000000 | bytes 32000000 | tf_op jit(solution)/shard_map/normal/pallas_call | solution.py:632
  23.9 1.8 all-to-all-done.refs_0_
  25.8 4.2 %all-to-all-start.1 = ((bf16[16,112,384]{2,1,0:T(8,128)(2,1)}), bf16[16,112,384]{2,1,0:T(8,128)(2,1)S(1)}, u32[]{:S(2)}, u32[]{:S(2)}) async-start(bf16[16,112,384]{2,1,0:T(8,128)(2,1)} %get-tuple-element.78), calls=%async_computation.1 | async-start | bytes 2752512 | tf_op jit(solution)/shard_map/all_to_all | solution.py:699
  30.8 23.0 %attend.1 = (bf16[8,1152,512]{2,1,0:T(8,128)(2,1)}, bf16[8,3072,256]{2,1,0:T(8,128)(2,1)}, bf16[8,384,512]{2,1,0:T(8,128)(2,1)}, bf16[1152,384]{1,0:T(8,128)(2,1)}) custom-call(s32[2]{0:T(128)} %pad_add_fusion.info, bf16[8,384,512]{2,1,0:T(8,128)(2,1)} %normal.1.z_ref, f32[8,384,128]{2,1,0:T(8,128)} %broadcast_in_dim.4.vec_ref, ...), custom_call_target="tpu_custom_call" | custom-call | flops 32000000000 | bytes 32000000 | tf_op jit(solution)/shard_map/attend/pallas_call | solution.py:632
  53.8 7.1 %all-to-all-done.1.own_ref = bf16[16,112,384]{2,1,0:T(8,128)(2,1)S(1)} async-done(((bf16[16,112,384]{2,1,0:T(8,128)(2,1)}), bf16[16,112,384]{2,1,0:T(8,128)(2,1)S(1)}, u32[]{:S(2)}, u32[]{:S(2)}) %all-to-all-start.1) | async-done | bytes 1376288 | tf_op jit(solution)/shard_map/all_to_all | solution.py:699
  61.1 2.9 %collective-permute-done.1.other_ref = bf16[16,112,384]{2,1,0:T(8,128)(2,1)S(1)} collective-permute-done((bf16[16,112,384]{2,1,0:T(8,128)(2,1)S(1)}, bf16[16,112,384]{2,1,0:T(8,128)(2,1)S(1)}, u32[]{:S(2)}, u32[]{:S(2)}) %collective-permute-start.1) | collective-permute-done | bytes 1376288 | tf_op jit(solution)/shard_map/ppermute | solution.py:702
  64.0 1.3 broadcast_in_dim.5.ub_ref
  65.4 60.3 %mlp.1 = (f32[8,384,512]{2,1,0:T(8,128)}, bf16[8,1536,512]{2,1,0:T(8,128)(2,1)}, f32[8,384,512]{2,1,0:T(8,128)}, f32[384,384]{1,0:T(8,128)}, bf16[384,384]{1,0:T...) custom-call(s32[2]{0:T(128)} %pad_add_fusion.info, ...), custom_call_target="tpu_custom_call" | custom-call | flops 80000000000 | bytes 32000000 | tf_op jit(solution)/shard_map/mlp/pallas_call | solution.py:632
  125.7 8.6 %back.2 = (bf16[8,1152,512]{2,1,0:T(8,128)(2,1)}, f32[1152,384]{1,0:T(8,128)}, f32[3,384,128]{2,1,0:T(8,128)}) custom-call(s32[2]{0:T(128)} %pad_add_fusion.info, bf16[8,384,512]{2,1,0:T(8,128)(2,1)} %normal.1.z_ref, bf16[8,1152,512]{2,1,0:T(8,128)(2,1)} %get-tuple-element.82.qkv_ref, bf16[8,3072,256]{2,1,0:T(8,128)(2,1)} %get-tuple-element.83.att_ref, ...), custom_call_target="tpu_custom_call" | custom-call | flops 6000000000 | bytes 4000000 | tf_op jit(solution)/shard_map/back/pallas_call | solution.py:632
  134.3 1.3 add_convert_fusion
  135.6 7.6 %all-to-all-start.2 = ((bf16[16,104,384]{2,1,0:T(8,128)(2,1)}), bf16[16,104,384]{2,1,0:T(8,128)(2,1)S(1)}, u32[]{:S(2)}, u32[]{:S(2)}) async-start(bf16[16,104,384]{2,1,0:T(8,128)(2,1)} %add_convert_fusion), calls=%async_computation.2 | async-start | bytes 2555904 | tf_op jit(solution)/shard_map/all_to_all | solution.py:699
  143.2 28.3 %back.3 = (bf16[8,1152,512]{2,1,0:T(8,128)(2,1)}, f32[16,160,128]{2,1,0:T(8,128)}, bf16[16,160,128]{2,1,0:T(8,128)(2,1)}) custom-call(s32[2]{0:T(128)} %pad_add_fusion.info, bf16[8,384,512]{2,1,0:T(8,128)(2,1)} %normal.1.z_ref, bf16[8,1152,512]{2,1,0:T(8,128)(2,1)} %get-tuple-element.82.qkv_ref, ...), custom_call_target="tpu_custom_call", output_to_operand_aliasing={{0}: (11, {})} | custom-call | flops 41999998976 | bytes 28000000 | tf_op jit(solution)/shard_map/back/pallas_call | solution.py:632
  172.4 2.3 collective-permute-done.3
  174.7 2.3 add_convert_fusion.1
  177.0 7.2 %all-to-all-start.3 = ((bf16[16,160,128]{2,1,0:T(8,128)(2,1)}), bf16[16,160,128]{2,1,0:T(8,128)(2,1)S(1)}, u32[]{:S(2)}, u32[]{:S(2)}) async-start(bf16[16,160,128]{2,1,0:T(8,128)(2,1)} %add_convert_fusion.1), calls=%async_computation.3 | async-start | bytes 1310720 | tf_op jit(solution)/shard_map/all_to_all | solution.py:699
  184.2 2.3 mlp_state.1
  188.6 2.9 %collective-permute-start.5 = (bf16[96,384]{1,0:T(8,128)(2,1)S(1)}, bf16[96,384]{1,0:T(8,128)(2,1)S(1)}, u32[]{:S(2)}, u32[]{:S(2)}) collective-permute-start(bf16[96,384]{1,0:T(8,128)(2,1)S(1)} %pad_maximum_fusion.2), channel_id=1, source_target_pairs={{0,16},{1,17},{2,18},{3,19},{4,20},{5,21},{6,22},{7,23},{8,24},{9,... | collective-permute-start | bytes 221192 | tf_op jit(solution)/shard_map/ppermute | solution.py:867
  191.4 9.0 %out.2.refs_0_ = f32[4096,384]{1,0:T(8,128)} custom-call(s32[2]{0:T(128)} %pad_add_fusion.info, f32[8,384,512]{2,1,0:T(8,128)} %get-tuple-element.101.h_ref, bf16[8,1536,512]{2,1,0:T(8,128)(2,1)} %get-tuple-element.102.act_ref, bf16[384,1536]{1,0:T(8,128)(2,1)} %get-tuple-element.103.wdn_ref, f32[8,384,128]{2,1,0:T(8,128)} %broadcast_in_dim.4.vec_ref), custom_call_target="tpu_custom_call" | custom-call | flops 6000000000 | bytes 16000000 | tf_op jit(solution)/shard_map/out/pallas_call | solution.py:632
  200.5 4.4 %collective-permute-done.5 = bf16[96,384]{1,0:T(8,128)(2,1)S(1)} collective-permute-done((bf16[96,384]{1,0:T(8,128)(2,1)S(1)}, bf16[96,384]{1,0:T(8,128)(2,1)S(1)}, u32[]{:S(2)}, u32[]{:S(2)}) %collective-permute-start.5) | collective-permute-done | bytes 73760 | tf_op jit(solution)/shard_map/ppermute | solution.py:867
  205.0 9.0 %out.3 = f32[4096,384]{1,0:T(8,128)} custom-call(s32[2]{0:T(128)} %pad_add_fusion.info, f32[8,384,512]{2,1,0:T(8,128)} %get-tuple-element.101.h_ref, bf16[8,1536,512]{2,1,0:T(8,128)(2,1)} %get-tuple-element.102.act_ref, bf16[384,1536]{1,0:T(8,128)(2,1)} %get-tuple-element.103.wdn_ref, ...), custom_call_target="tpu_custom_call", output_to_operand_aliasing={{}: (5, {})} | custom-call | flops 6000000000 | bytes 16000000 | tf_op jit(solution)/shard_map/out/pallas_call | solution.py:632
  214.9 2.1 att_state.1
  217.7 5.2 %all-to-all-start.4 = ((bf16[16,48,384]{2,1,0:T(8,128)(2,1)}), bf16[16,48,384]{2,1,0:T(8,128)(2,1)S(1)}, u32[]{:S(2)}, u32[]{:S(2)}) async-start(bf16[16,48,384]{2,1,0:T(8,128)(2,1)} %get-tuple-element.107), calls=%async_computation.4 | async-start | bytes 1179648 | tf_op jit(solution)/shard_map/all_to_all | solution.py:699
  222.8 10.2 %input.2.refs_0_ = f32[4096,384]{1,0:T(8,128)} custom-call(s32[2]{0:T(128)} %pad_add_fusion.info, bf16[4096,384]{1,0:T(8,128)(2,1)} %x_ref.7, bf16[8,1152,512]{2,1,0:T(8,128)(2,1)} %get-tuple-element.110.dqkv_ref, f32[8,384,512]{2,1,0:T(8,128)} %get-tuple-element.84.dh_ref, bf16[1152,384]{1,0:T(8,128)(2,1)} %get-tuple-element.86.wq_ref, ...), custom_call_target="tpu_custom_call" | custom-call | flops 8000000000 | bytes 16000000 | tf_op jit(solution)/shard_map/input/pallas_call | solution.py:632
  233.1 2.0 collective-permute-start.9
  235.1 10.2 %input.3 = f32[4096,384]{1,0:T(8,128)} custom-call(s32[2]{0:T(128)} %pad_add_fusion.info, bf16[4096,384]{1,0:T(8,128)(2,1)} %x_ref.7, bf16[8,1152,512]{2,1,0:T(8,128)(2,1)} %get-tuple-element.110.dqkv_ref, f32[8,384,512]{2,1,0:T(8,128)} %get-tuple-element.84.dh_ref, bf16[1152,384]{1,0:T(8,128)(2,1)} %get-tuple-element.86.wq_ref, ...), custom_call_target="tpu_custom_call", output_to_operand_aliasing={{}: (6, {})} | custom-call | flops 8000000000 | bytes 16000000 | tf_op jit(solution)/shard_map/input/pallas_call | solution.py:632
  246.1 1.6 collective-permute-done.9.moved_ref
  249.3 22.3 %newton.1.mine_ref = f32[2,392,384]{2,1,0:T(8,128)} custom-call(s32[2]{0:T(128)} %pad_add_fusion.1.info, bf16[16,48,384]{2,1,0:T(8,128)(2,1)} %copy-done.3, bf16[16,48,384]{2,1,0:T(8,128)(2,1)} %copy-done.8, bf16[768,384]{1,0:T(8,128)(2,1)} %copy-done.6, bf16[768,384]{1,0:T(8,128)(2,1)} %copy-done.7), custom_call_target="tpu_custom_call" | custom-call | tf_op jit(solution)/shard_map/newton/pallas_call | solution.py:605
  274.7 1.1 copy-done.5
  275.8 3.7 %update.1 = (f32[36,384]{1,0:T(8,128)}, f32[12,384]{1,0:T(8,128)}, f32[48,384]{1,0:T(8,128)}, f32[48,384]{1,0:T(8,128)}) custom-call(s32[1]{0:T(128)} %bitcast.info, f32[2,392,384]{2,1,0:T(8,128)} %newton.1.mine_ref, f32[2,392,384]{2,1,0:T(8,128)} %copy-done.5, f32[48,384]{1,0:T(8,128)} %get-tuple-element.120.sa_ref, f32[96,384]{1,0:T(8,128)} %get-tuple-element.121.sb_ref, ...), custom_call_target="tpu_custom_call" | custom-call | tf_op jit(solution)/shard_map/update/pallas_call | solution.py:605
  (81 shorter events, 10.9 us)
Async XLA Ops:
  2.9 22.8 %all-to-all-start = ((bf16[16,36,384]{2,1,0:T(8,128)(2,1)}), bf16[16,36,384]{2,1,0:T(8,128)(2,1)S(1)}, u32[]{:S(2)}, u32[]{:S(2)}) async-start(bf16[16,36,384]{2,1,0:T(8,128)(2,1)} %get-tuple-element.74), calls=%async_computation | async-start | bytes 983040 | tf_op jit(solution)/shard_map/all_to_all | solution.py:699
  25.8 4.2 %copy-start.9 = (bf16[16,36,384]{2,1,0:T(8,128)(2,1)}, bf16[16,36,384]{2,1,0:T(8,128)(2,1)S(1)}, u32[]{:S(2)}) copy-start(bf16[16,36,384]{2,1,0:T(8,128)(2,1)S(1)} %all-to-all-done.refs_0_) | copy-start | bytes 1327108
  25.8 4.2 %collective-permute-start = (bf16[16,36,384]{2,1,0:T(8,128)(2,1)S(1)}, bf16[16,36,384]{2,1,0:T(8,128)(2,1)S(1)}, u32[]{:S(2)}, u32[]{:S(2)}) collective-permute-start(bf16[16,36,384]{2,1,0:T(8,128)(2,1)S(1)} %all-to-all-done.refs_0_), channel_id=1, source_target_pairs={{0,1},{1,0},{2,3},{3,2},{4,5},{5,4},{6,7},{7,6},{8,9},{9,8},{10,11... | collective-permute-start | bytes 1327112 | tf_op jit(solution)/shard_map/ppermute | solution.py:702
  25.8 35.1 %all-to-all-start.1 = ((bf16[16,112,384]{2,1,0:T(8,128)(2,1)}), bf16[16,112,384]{2,1,0:T(8,128)(2,1)S(1)}, u32[]{:S(2)}, u32[]{:S(2)}) async-start(bf16[16,112,384]{2,1,0:T(8,128)(2,1)} %get-tuple-element.78), calls=%async_computation.1 | async-start | bytes 2752512 | tf_op jit(solution)/shard_map/all_to_all | solution.py:699
  30.0 30.9 %copy-start.12 = (f32[1536]{0:T(1024)S(1)}, f32[1536]{0:T(1024)}, u32[]{:S(2)}) copy-start(f32[1536]{0:T(1024)} %param.21) | copy-start | bytes 18436
  60.9 4.5 %copy-start.4 = (bf16[16,112,384]{2,1,0:T(8,128)(2,1)}, bf16[16,112,384]{2,1,0:T(8,128)(2,1)S(1)}, u32[]{:S(2)}) copy-start(bf16[16,112,384]{2,1,0:T(8,128)(2,1)S(1)} %all-to-all-done.1.own_ref) | copy-start | bytes 4128772
  60.9 3.1 %collective-permute-start.1 = (bf16[16,112,384]{2,1,0:T(8,128)(2,1)S(1)}, bf16[16,112,384]{2,1,0:T(8,128)(2,1)S(1)}, u32[]{:S(2)}, u32[]{:S(2)}) collective-permute-start(bf16[16,112,384]{2,1,0:T(8,128)(2,1)S(1)} %all-to-all-done.1.own_ref), channel_id=1, source_target_pairs={{0,1},{1,0},{2,3},{3,2},{4,5},{5,4},{6,7},{7,6},{8,9},{9,8},{10,11... | collective-permute-start | bytes 4128776 | tf_op jit(solution)/shard_map/ppermute | solution.py:702
  64.0 1.3 copy-start.17
  125.6 8.7 %collective-permute-start.2 = (bf16[16,104,384]{2,1,0:T(8,128)(2,1)}, bf16[16,104,384]{2,1,0:T(8,128)(2,1)S(1)}, u32[]{:S(2)}, u32[]{:S(2)}) collective-permute-start(bf16[16,104,384]{2,1,0:T(8,128)(2,1)} %get-tuple-element.81), channel_id=1, source_target_pairs={{0,1},{1,0},{2,3},{3,2},{4,5},{5,4},{6,7},{7,6},{8,9},{9,8},{10,11... | collective-permute-start | bytes 3833864 | tf_op jit(solution)/shard_map/ppermute | solution.py:702
  125.7 8.6 %copy-start.2 = (f32[16,104,384]{2,1,0:T(8,128)S(1)}, f32[16,104,384]{2,1,0:T(8,128)}, u32[]{:S(2)}) copy-start(f32[16,104,384]{2,1,0:T(8,128)} %get-tuple-element.80) | copy-start | bytes 7667716
  135.6 36.7 %all-to-all-start.2 = ((bf16[16,104,384]{2,1,0:T(8,128)(2,1)}), bf16[16,104,384]{2,1,0:T(8,128)(2,1)S(1)}, u32[]{:S(2)}, u32[]{:S(2)}) async-start(bf16[16,104,384]{2,1,0:T(8,128)(2,1)} %add_convert_fusion), calls=%async_computation.2 | async-start | bytes 2555904 | tf_op jit(solution)/shard_map/all_to_all | solution.py:699
  172.3 11.9 %copy-start = (bf16[16,104,384]{2,1,0:T(8,128)(2,1)}, bf16[16,104,384]{2,1,0:T(8,128)(2,1)S(1)}, u32[]{:S(2)}) copy-start(bf16[16,104,384]{2,1,0:T(8,128)(2,1)S(1)} %all-to-all-done.2.got_ref) | copy-start | bytes 3833860
  172.4 2.3 collective-permute-start.3
  177.0 37.0 %all-to-all-start.3 = ((bf16[16,160,128]{2,1,0:T(8,128)(2,1)}), bf16[16,160,128]{2,1,0:T(8,128)(2,1)S(1)}, u32[]{:S(2)}, u32[]{:S(2)}) async-start(bf16[16,160,128]{2,1,0:T(8,128)(2,1)} %add_convert_fusion.1), calls=%async_computation.3 | async-start | bytes 1310720 | tf_op jit(solution)/shard_map/all_to_all | solution.py:699
  187.3 1.3 collective-permute-start.4
  188.6 16.3 %collective-permute-start.5 = (bf16[96,384]{1,0:T(8,128)(2,1)S(1)}, bf16[96,384]{1,0:T(8,128)(2,1)S(1)}, u32[]{:S(2)}, u32[]{:S(2)}) collective-permute-start(bf16[96,384]{1,0:T(8,128)(2,1)S(1)} %pad_maximum_fusion.2), channel_id=1, source_target_pairs={{0,16},{1,17},{2,18},{3,19},{4,20},{5,21},{6,22},{7,23},{8,24},{9,... | collective-permute-start | bytes 221192 | tf_op jit(solution)/shard_map/ppermute | solution.py:867
  204.9 12.1 %collective-permute-start.6 = (bf16[192,384]{1,0:T(8,128)(2,1)S(1)}, bf16[192,384]{1,0:T(8,128)(2,1)S(1)}, u32[]{:S(2)}, u32[]{:S(2)}) collective-permute-start(bf16[192,384]{1,0:T(8,128)(2,1)S(1)} %pad_maximum_fusion.1), channel_id=1, source_target_pairs={{0,8},{1,9},{2,10},{3,11},{4,12},{5,13},{6,14},{7,15},{8,0},{9,1},... | collective-permute-start | bytes 442376 | tf_op jit(solution)/shard_map/ppermute | solution.py:867
  214.0 0.8 copy-start.1
  217.0 16.0 %collective-permute-start.7 = (bf16[384,384]{1,0:T(8,128)(2,1)S(1)}, bf16[384,384]{1,0:T(8,128)(2,1)S(1)}, u32[]{:S(2)}, u32[]{:S(2)}) collective-permute-start(bf16[384,384]{1,0:T(8,128)(2,1)S(1)} %pad_maximum_fusion), channel_id=1, source_target_pairs={{0,4},{1,5},{2,6},{3,7},{4,0},{5,1},{6,2},{7,3},{8,12},{9,13},{10,... | collective-permute-start | bytes 884744 | tf_op jit(solution)/shard_map/ppermute | solution.py:867
  217.7 27.7 %all-to-all-start.4 = ((bf16[16,48,384]{2,1,0:T(8,128)(2,1)}), bf16[16,48,384]{2,1,0:T(8,128)(2,1)S(1)}, u32[]{:S(2)}, u32[]{:S(2)}) async-start(bf16[16,48,384]{2,1,0:T(8,128)(2,1)} %get-tuple-element.107), calls=%async_computation.4 | async-start | bytes 1179648 | tf_op jit(solution)/shard_map/all_to_all | solution.py:699
  233.1 12.2 %copy-start.6 = (bf16[768,384]{1,0:T(8,128)(2,1)}, bf16[768,384]{1,0:T(8,128)(2,1)S(1)}, u32[]{:S(2)}) copy-start(bf16[768,384]{1,0:T(8,128)(2,1)S(1)} %constant_dynamic-update-slice_fusion.pool_ref) | copy-start | bytes 1769476
  233.1 14.6 %collective-permute-start.9 = (bf16[768,384]{1,0:T(8,128)(2,1)S(1)}, bf16[768,384]{1,0:T(8,128)(2,1)S(1)}, u32[]{:S(2)}, u32[]{:S(2)}) collective-permute-start(bf16[768,384]{1,0:T(8,128)(2,1)S(1)} %constant_dynamic-update-slice_fusion.pool_ref), channel_id=1, source_target_pairs={{0,2},{1,3},{2,0},{3,1},{4,6},{5,7},{6,4},{7,5},{8,10},{9,11},{10,... | collective-permute-start | bytes 1769480 | tf_op jit(solution)/shard_map/ppermute | solution.py:867
  245.3 26.4 %copy-start.15 = (f32[8,384]{1,0:T(8,128)S(1)}, f32[8,384]{1,0:T(8,128)}, u32[]{:S(2)}) copy-start(f32[8,384]{1,0:T(8,128)} %get-tuple-element.118) | copy-start | bytes 36868
  245.3 27.9 %copy-start.13 = (f32[1536]{0:T(1024)S(1)}, f32[1536]{0:T(1024)}, u32[]{:S(2)}) copy-start(f32[1536]{0:T(1024)} %param.21) | copy-start | bytes 18436
  245.3 28.5 %copy-start.16 = (f32[12,128]{1,0:T(8,128)S(1)}, f32[12,128]{1,0:T(8,128)}, u32[]{:S(2)}) copy-start(f32[12,128]{1,0:T(8,128)} %get-tuple-element.117) | copy-start | bytes 18436
  245.3 28.6 %copy-start.10 = (f32[8,384]{1,0:T(8,128)S(1)}, f32[8,384]{1,0:T(8,128)}, u32[]{:S(2)}) copy-start(f32[8,384]{1,0:T(8,128)} %row_ref.3) | copy-start | bytes 36868
  245.3 2.3 copy-start.3
  245.3 2.3 collective-permute-start.8
  271.6 3.1 %collective-permute-start.10 = (f32[2,392,384]{2,1,0:T(8,128)}, f32[2,392,384]{2,1,0:T(8,128)S(1)}, u32[]{:S(2)}, u32[]{:S(2)}) collective-permute-start(f32[2,392,384]{2,1,0:T(8,128)} %newton.1.mine_ref), channel_id=1, source_target_pairs={{0,1},{1,0},{2,3},{3,2},{4,5},{5,4},{6,7},{7,6},{8,9},{9,8},{10,11... | collective-permute-start | bytes 3612680 | tf_op jit(solution)/shard_map/ppermute | solution.py:702
  271.8 7.6 %copy-start.14 = (f32[1536]{0:T(1024)}, f32[1536]{0:T(1024)S(1)}, u32[]{:S(2)}) copy-start(f32[1536]{0:T(1024)S(1)} %reshape.80) | copy-start | bytes 18436
  273.9 5.6 %copy-start.11 = (f32[8,384]{1,0:T(8,128)}, f32[8,384]{1,0:T(8,128)S(1)}, u32[]{:S(2)}) copy-start(f32[8,384]{1,0:T(8,128)S(1)} %get-tuple-element.131) | copy-start | bytes 36868
  274.7 1.1 copy-start.5
  (3 other events, 2.4 us)

commit v7 on v6

--- a/solution.py
+++ b/solution.py
@@ -505,7 +505,10 @@
     out_ref[cut:, cut:] = nt(left_ref[cut:, :], right_ref[cut:, :])
 
 
-def newton_kernel(info, own_ref, other_ref, pool_ref, moved_ref, out_ref, whole, gram, poly, pa, pb, sa, sb):
+def newton_kernel(
+    info, own_ref, other_ref, pool_ref, moved_ref, mine_a, theirs_a, mine_b, theirs_b,
+    mine_ref, send_ref, whole, gram, poly, pa, pb, sa, sb,
+):
     width = own_ref.shape[-1]
     eye = (
         lax.broadcasted_iota(jnp.int32, (width, width), 0)
@@ -520,9 +523,10 @@
         ).astype(bf16)
         first += tn(part, part)
     second = tn(pool_ref[...], pool_ref[...]) + tn(moved_ref[...], moved_ref[...])
+    norms = []
     for index, made in enumerate((first, second)):
         norm = lax.rsqrt(jnp.sum(made * eye) + norm_eps)
-        out_ref[index, width:, :] = jnp.full((8, width), norm, f32)
+        norms.append(norm)
         gram[index] = made * (norm * norm)
         whole[index] = eye
 
@@ -551,29 +555,23 @@
         return carry
 
     lax.fori_loop(0, 5, turn, 0)
-    for index in range(2):
-        out_ref[index, :width, :] = whole[index]
-
-
-def update_kernel(wide, info, mine_ref, theirs_ref, sa_ref, sb_ref, *refs):
-    ours = info[0] == 0
-    width = mine_ref.shape[2]
-    for pair, state_ref in enumerate((sa_ref, sb_ref)):
-        low = 0
-        for side in range(2):
-            w_ref, u_ref = refs[2 * pair + side], refs[4 + 2 * pair + side]
-            high = low + w_ref.shape[0]
-            pick = ours if side == 0 else jnp.logical_not(ours)
-            whole = jnp.where(pick, mine_ref[pair, :width, :], theirs_ref[pair, :width, :])
-            norm = jnp.where(
-                pick, mine_ref[pair, width : width + 1, :], theirs_ref[pair, width : width + 1, :]
-            )
-            sh, sl = split_parts(state_ref[low:high, :] * norm)
-            ph, pl_ = split_parts(whole)
-            ortho = nt(sh, ph) + (nt(sl, ph) + nt(sh, pl_))
-            rate = matrix_rate * 0.2 * math.sqrt(wide[2 * pair + side])
-            u_ref[...] = w_ref[...] - rate * ortho
-            low = high
+    low = 0
+    for k, pair in enumerate(((mine_a, theirs_a), (mine_b, theirs_b))):
+        ph, pl_ = split_parts(whole[k])
+        high = low + pair[0].shape[0]
+        for state_ref, to_ref in zip(pair, (mine_ref, send_ref)):
+            sh, sl = split_parts(state_ref[...] * norms[k])
+            to_ref[low:high, :] = nt(sh, ph) + (nt(sl, ph) + nt(sh, pl_))
+        low = high
+
+
+def update_kernel(wide, info, mine_ref, got_ref, *refs):
+    low = 0
+    for index, (w_ref, u_ref) in enumerate(zip(refs[:4], refs[4:])):
+        high = low + w_ref.shape[0]
+        ortho = jnp.where(info[0] == index % 2, mine_ref[low:high, :], got_ref[low:high, :])
+        u_ref[...] = w_ref[...] - (matrix_rate * 0.2 * math.sqrt(wide[index])) * ortho
+        low = high
 
 
 def fixed(shape):
@@ -714,7 +712,7 @@
     tokens, qkv_spec, att_spec, deep_spec, ff_spec = group_specs(width, ff, 0)
     wide = (groups, width, lanes)
     z1 = grid_call(
-        normal_kernel, info, 0, groups, [(tokens, block_in), (None, vec)], [(deep_spec, wide, bf16)], [],
+        normal_kernel, after(info, ub), 0, groups, [(tokens, block_in), (None, vec)], [(deep_spec, wide, bf16)], [],
         "normal", 1e9,
     )[0]
     wq_own = after(exchange(first), z1)
@@ -881,30 +879,36 @@
     gq, gpr, sq, sp, spread_a, state_a, vector_a = sums(
         got_a, mq_s, mp_s, (4 * blocks, LANES), (half, cq + cp, width), "att"
     )
+    others_b = swap(state_b)
     own_a = exchange(spread_a)
+    others_a = swap(state_a)
     pool = joined(pool, after(moved, spread_a))
     moved = gather_step(pool, bits[-2])
     dx = input_part(0, mid, dqkv, after(info, pool))
     pool = joined(pool, after(moved, dx[0]))
     moved = gather_step(pool, bits[-1])
-    dx = input_part(mid, groups, dqkv, after(info, pool), dx)
+    dx = input_part(mid, groups, dqkv, after(info, pool, others_a, others_b), dx)
     own_a = after(own_a, dx[0])
     other_a = swap(own_a)
     square = pltpu.VMEM((2, width, width), f32)
     parts = pltpu.VMEM((2, width, 3 * width), bf16)
-    mine = small_call(
+    total = cq + cp + cu + cd
+    mine, send = small_call(
         newton_kernel,
-        [((2, width + 8, width), f32)],
+        [((total, width), f32), ((total, width), f32)],
         "newton",
         scalars=1,
         scratch=[square, square, square, parts, parts, parts, parts],
-    )(jnp.stack([par, jnp.full((), cq, jnp.int32)]), own_a, other_a, pool, moved)[0]
+    )(
+        jnp.stack([par, jnp.full((), cq, jnp.int32)]),
+        own_a, other_a, pool, moved, state_a, others_a, state_b, others_b,
+    )
     uq, up, uu, ud = small_call(
         functools.partial(update_kernel, tuple(w.shape[0] * devices for w in turned)),
         [(w.shape, f32) for w in turned],
         "update",
         scalars=1,
-    )(par.reshape(1), mine, swap(mine), state_a, state_b, *turned)
+    )(par.reshape(1), mine, swap(send), *turned)
     out, dx = out[0], dx[0]
 
     vector_grad = jnp.concatenate([vector_a.reshape(4, width), vector_b[:4]], axis=0)

time: 281 us -> 281 us (level)
  Pallas kernels: 200 us -> 181 us
  starting transfers between devices: 38.3 us -> 51.8 us
  waiting for transfers between devices: 21.5 us -> 26.2 us
    pallas_call x9, Pallas kernels: 168 us -> 149 us  [grid_call(): pl.pallas_call(kernel, grid_spec=pltpu.PrefetchScalarGridSpec(num_scalar_...]
    all_to_all x5, starting transfers between devices: 32.5 us -> 39.4 us  [exchange(): return lax.all_to_all(x, 'dp', 0, 0, axis_index_groups=planes, tiled=True)]
    ppermute x7 -> x9, starting transfers between devices: 0.22 us -> 5.3 us  [swap(): return lax.ppermute(x, 'dp', pairs)]
    all_to_all x5, waiting for transfers between devices: 9.7 us -> 13.6 us  [exchange(): return lax.all_to_all(x, 'dp', 0, 0, axis_index_groups=planes, tiled=True)]
    ppermute x7 -> x9, waiting for transfers between devices: 5.79 us -> 5.91 us  [swap(): return lax.ppermute(x, 'dp', pairs)]
  transfers between devices with their start and end apart: 16 -> 18, of which waited for: 9 -> 8; matrix products, arithmetic and copies ran while one was open for 3% -> 4% of each run, Pallas kernels for 40% -> 37%
where the time goes in v7:
time: 281 us; the launch traced here: 279 us
  Pallas kernels  181 us (64%)
  starting transfers between devices  51.8 us (18%)
  waiting for transfers between devices  26.2 us (9%)
  local copies, waits for them, and re-layouts  11 us (4%)
  other arithmetic  6.97 us (2%)
    pallas_call x9, Pallas kernels, grid_call(): pl.pallas_call(kernel, grid_spec=pltpu.PrefetchScalarGridSpec(num_scalar_...  149 us
    all_to_all x5, starting transfers between devices, exchange(): return lax.all_to_all(x, 'dp', 0, 0, axis_index_groups=planes, tiled=True)  39.4 us
    pallas_call x5, Pallas kernels, call(): pl.pallas_call(kernel, in_specs=[smem] * scalars + [vmem] * (len(args) -...  31.8 us
    all_to_all x5, waiting for transfers between devices, exchange(): return lax.all_to_all(x, 'dp', 0, 0, axis_index_groups=planes, tiled=True)  13.6 us
    ppermute x4, starting transfers between devices, gather_step(): return lax.ppermute(pool, 'dp', [(i, i ^ bit) for i in range(devices)])  7.03 us
    ppermute x4, waiting for transfers between devices, gather_step(): return lax.ppermute(pool, 'dp', [(i, i ^ bit) for i in range(devices)])  6.65 us
    ppermute x9, waiting for transfers between devices, swap(): return lax.ppermute(x, 'dp', pairs)  5.91 us
  transfers between devices with their start and end apart: 18, of which 8 were waited for; matrix products, arithmetic and copies ran while one was open for 4% of the time, Pallas kernels for 37%

profile of v7, /device:TPU:0, one launch (start us, length us, event | category | flops | bytes accessed | tf_op | source)
XLA Modules:
  0.0 279.4 jit_solution(10207557284685079855)
XLA Ops:
  0.7 2.3 prep.1
  2.9 8.3 %all-to-all-start = ((bf16[16,36,384]{2,1,0:T(8,128)(2,1)}), bf16[16,36,384]{2,1,0:T(8,128)(2,1)S(1)}, u32[]{:S(2)}, u32[]{:S(2)}) async-start(bf16[16,36,384]{2,1,0:T(8,128)(2,1)} %get-tuple-element.78), calls=%async_computation | async-start | bytes 983040 | tf_op jit(solution)/shard_map/all_to_all | solution.py:697
  14.6 2.3 broadcast_in_dim.5.vec_ref
  16.9 8.6 %normal.1.z_ref = bf16[8,384,512]{2,1,0:T(8,128)(2,1)} custom-call(s32[2]{0:T(128)} %pad_add_fusion.info, bf16[4096,384]{1,0:T(8,128)(2,1)} %x_ref.7, f32[8,384,128]{2,1,0:T(8,128)} %broadcast_in_dim.5.vec_ref), custom_call_target="tpu_custom_call" | custom-call | flops 8000000000 | bytes 32000000 | tf_op jit(solution)/shard_map/normal/pallas_call | solution.py:630
  25.8 6.7 %all-to-all-start.1 = ((bf16[16,112,384]{2,1,0:T(8,128)(2,1)}), bf16[16,112,384]{2,1,0:T(8,128)(2,1)S(1)}, u32[]{:S(2)}, u32[]{:S(2)}) async-start(bf16[16,112,384]{2,1,0:T(8,128)(2,1)} %get-tuple-element.82), calls=%async_computation.1 | async-start | bytes 2752512 | tf_op jit(solution)/shard_map/all_to_all | solution.py:697
  33.3 20.4 %attend.1 = (bf16[8,1152,512]{2,1,0:T(8,128)(2,1)}, bf16[8,3072,256]{2,1,0:T(8,128)(2,1)}, bf16[8,384,512]{2,1,0:T(8,128)(2,1)}, bf16[1152,384]{1,0:T(8,128)(2,1)}) custom-call(s32[2]{0:T(128)} %pad_add_fusion.info, bf16[8,384,512]{2,1,0:T(8,128)(2,1)} %normal.1.z_ref, f32[8,384,128]{2,1,0:T(8,128)} %broadcast_in_dim.5.vec_ref, ...), custom_call_target="tpu_custom_call" | custom-call | flops 32000000000 | bytes 32000000 | tf_op jit(solution)/shard_map/attend/pallas_call | solution.py:630
  53.6 9.7 %all-to-all-done.1.own_ref = bf16[16,112,384]{2,1,0:T(8,128)(2,1)S(1)} async-done(((bf16[16,112,384]{2,1,0:T(8,128)(2,1)}), bf16[16,112,384]{2,1,0:T(8,128)(2,1)S(1)}, u32[]{:S(2)}, u32[]{:S(2)}) %all-to-all-start.1) | async-done | bytes 1376288 | tf_op jit(solution)/shard_map/all_to_all | solution.py:697
  63.4 3.3 %collective-permute-done.1.other_ref = bf16[16,112,384]{2,1,0:T(8,128)(2,1)} collective-permute-done((bf16[16,112,384]{2,1,0:T(8,128)(2,1)S(1)}, bf16[16,112,384]{2,1,0:T(8,128)(2,1)}, u32[]{:S(2)}, u32[]{:S(2)}) %collective-permute-start.1) | collective-permute-done | bytes 1376288 | tf_op jit(solution)/shard_map/ppermute | solution.py:700
  66.6 49.7 %mlp.1 = (f32[8,384,512]{2,1,0:T(8,128)}, bf16[8,1536,512]{2,1,0:T(8,128)(2,1)}, f32[8,384,512]{2,1,0:T(8,128)}, f32[384,384]{1,0:T(8,128)}, bf16[384,384]{1,0:T...) custom-call(s32[2]{0:T(128)} %pad_add_fusion.info, ...), custom_call_target="tpu_custom_call" | custom-call | flops 80000000000 | bytes 32000000 | tf_op jit(solution)/shard_map/mlp/pallas_call | solution.py:630
  116.4 4.6 %collective-permute-start.2 = (bf16[16,104,384]{2,1,0:T(8,128)(2,1)}, bf16[16,104,384]{2,1,0:T(8,128)(2,1)S(1)}, u32[]{:S(2)}, u32[]{:S(2)}) collective-permute-start(bf16[16,104,384]{2,1,0:T(8,128)(2,1)} %get-tuple-element.85), channel_id=1, source_target_pairs={{0,1},{1,0},{2,3},{3,2},{4,5},{5,4},{6,7},{7,6},{8,9},{9,8},{10,11... | collective-permute-start | bytes 3833864 | tf_op jit(solution)/shard_map/ppermute | solution.py:700
  121.0 8.6 %back.2 = (bf16[8,1152,512]{2,1,0:T(8,128)(2,1)}, f32[1152,384]{1,0:T(8,128)}, f32[3,384,128]{2,1,0:T(8,128)}) custom-call(s32[2]{0:T(128)} %pad_add_fusion.info, bf16[8,384,512]{2,1,0:T(8,128)(2,1)} %normal.1.z_ref, bf16[8,1152,512]{2,1,0:T(8,128)(2,1)} %get-tuple-element.86.qkv_ref, bf16[8,3072,256]{2,1,0:T(8,128)(2,1)} %get-tuple-element.87.att_ref, ...), custom_call_target="tpu_custom_call" | custom-call | flops 6000000000 | bytes 4000000 | tf_op jit(solution)/shard_map/back/pallas_call | solution.py:630
  129.6 1.3 add_convert_fusion
  130.9 13.7 %all-to-all-start.2 = ((bf16[16,104,384]{2,1,0:T(8,128)(2,1)}), bf16[16,104,384]{2,1,0:T(8,128)(2,1)S(1)}, u32[]{:S(2)}, u32[]{:S(2)}) async-start(bf16[16,104,384]{2,1,0:T(8,128)(2,1)} %add_convert_fusion), calls=%async_computation.2 | async-start | bytes 2555904 | tf_op jit(solution)/shard_map/all_to_all | solution.py:697
  144.6 25.2 %back.3 = (bf16[8,1152,512]{2,1,0:T(8,128)(2,1)}, f32[16,160,128]{2,1,0:T(8,128)}, bf16[16,160,128]{2,1,0:T(8,128)(2,1)}) custom-call(s32[2]{0:T(128)} %pad_add_fusion.info, bf16[8,384,512]{2,1,0:T(8,128)(2,1)} %normal.1.z_ref, bf16[8,1152,512]{2,1,0:T(8,128)(2,1)} %get-tuple-element.86.qkv_ref, ...), custom_call_target="tpu_custom_call", output_to_operand_aliasing={{0}: (11, {})} | custom-call | flops 41999998976 | bytes 28000000 | tf_op jit(solution)/shard_map/back/pallas_call | solution.py:630
  169.8 3.7 %all-to-all-done.2.got_ref = bf16[16,104,384]{2,1,0:T(8,128)(2,1)S(1)} async-done(((bf16[16,104,384]{2,1,0:T(8,128)(2,1)}), bf16[16,104,384]{2,1,0:T(8,128)(2,1)S(1)}, u32[]{:S(2)}, u32[]{:S(2)}) %all-to-all-start.2) | async-done | bytes 1277984 | tf_op jit(solution)/shard_map/all_to_all | solution.py:697
  174.1 1.6 collective-permute-done.3
  175.8 2.3 add_convert_fusion.1
  178.1 7.0 %all-to-all-start.3 = ((bf16[16,160,128]{2,1,0:T(8,128)(2,1)}), bf16[16,160,128]{2,1,0:T(8,128)(2,1)S(1)}, u32[]{:S(2)}, u32[]{:S(2)}) async-start(bf16[16,160,128]{2,1,0:T(8,128)(2,1)} %add_convert_fusion.1), calls=%async_computation.3 | async-start | bytes 1310720 | tf_op jit(solution)/shard_map/all_to_all | solution.py:697
  185.1 2.3 mlp_state.1
  190.3 2.9 %collective-permute-start.5 = (bf16[96,384]{1,0:T(8,128)(2,1)S(1)}, bf16[96,384]{1,0:T(8,128)(2,1)S(1)}, u32[]{:S(2)}, u32[]{:S(2)}) collective-permute-start(bf16[96,384]{1,0:T(8,128)(2,1)S(1)} %pad_maximum_fusion.2), channel_id=1, source_target_pairs={{0,16},{1,17},{2,18},{3,19},{4,20},{5,21},{6,22},{7,23},{8,24},{9,... | collective-permute-start | bytes 221192 | tf_op jit(solution)/shard_map/ppermute | solution.py:865
  193.2 9.0 %out.2.refs_0_ = f32[4096,384]{1,0:T(8,128)} custom-call(s32[2]{0:T(128)} %pad_add_fusion.info, f32[8,384,512]{2,1,0:T(8,128)} %get-tuple-element.105.h_ref, bf16[8,1536,512]{2,1,0:T(8,128)(2,1)} %get-tuple-element.106.act_ref, bf16[384,1536]{1,0:T(8,128)(2,1)} %get-tuple-element.107.wdn_ref, f32[8,384,128]{2,1,0:T(8,128)} %broadcast_in_dim.5.vec_ref), custom_call_target="tpu_custom_call" | custom-call | flops 6000000000 | bytes 16000000 | tf_op jit(solution)/shard_map/out/pallas_call | solution.py:630
  202.2 3.5 %collective-permute-done.5 = bf16[96,384]{1,0:T(8,128)(2,1)S(1)} collective-permute-done((bf16[96,384]{1,0:T(8,128)(2,1)S(1)}, bf16[96,384]{1,0:T(8,128)(2,1)S(1)}, u32[]{:S(2)}, u32[]{:S(2)}) %collective-permute-start.5) | collective-permute-done | bytes 73760 | tf_op jit(solution)/shard_map/ppermute | solution.py:865
  205.8 8.2 %out.3 = f32[4096,384]{1,0:T(8,128)} custom-call(s32[2]{0:T(128)} %pad_add_fusion.info, f32[8,384,512]{2,1,0:T(8,128)} %get-tuple-element.105.h_ref, bf16[8,1536,512]{2,1,0:T(8,128)(2,1)} %get-tuple-element.106.act_ref, bf16[384,1536]{1,0:T(8,128)(2,1)} %get-tuple-element.107.wdn_ref, ...), custom_call_target="tpu_custom_call", output_to_operand_aliasing={{}: (5, {})} | custom-call | flops 6000000000 | bytes 16000000 | tf_op jit(solution)/shard_map/out/pallas_call | solution.py:630
  214.8 2.1 att_state.1
  217.0 2.4 collective-permute-start.7
  219.4 3.8 %all-to-all-start.4 = ((bf16[16,48,384]{2,1,0:T(8,128)(2,1)}), bf16[16,48,384]{2,1,0:T(8,128)(2,1)S(1)}, u32[]{:S(2)}, u32[]{:S(2)}) async-start(bf16[16,48,384]{2,1,0:T(8,128)(2,1)} %get-tuple-element.111), calls=%async_computation.4 | async-start | bytes 1179648 | tf_op jit(solution)/shard_map/all_to_all | solution.py:697
  223.3 10.2 %input.2.refs_0_ = f32[4096,384]{1,0:T(8,128)} custom-call(s32[2]{0:T(128)} %pad_add_fusion.info, bf16[4096,384]{1,0:T(8,128)(2,1)} %x_ref.7, bf16[8,1152,512]{2,1,0:T(8,128)(2,1)} %get-tuple-element.114.dqkv_ref, f32[8,384,512]{2,1,0:T(8,128)} %get-tuple-element.88.dh_ref, bf16[1152,384]{1,0:T(8,128)(2,1)} %get-tuple-element.90.wq_ref, ...), custom_call_target="tpu_custom_call" | custom-call | flops 8000000000 | bytes 16000000 | tf_op jit(solution)/shard_map/input/pallas_call | solution.py:630
  233.6 1.6 collective-permute-start.11
  235.2 9.4 %input.3 = f32[4096,384]{1,0:T(8,128)} custom-call(s32[2]{0:T(128)} %pad_add_fusion.info, bf16[4096,384]{1,0:T(8,128)(2,1)} %x_ref.7, bf16[8,1152,512]{2,1,0:T(8,128)(2,1)} %get-tuple-element.114.dqkv_ref, f32[8,384,512]{2,1,0:T(8,128)} %get-tuple-element.88.dh_ref, bf16[1152,384]{1,0:T(8,128)(2,1)} %get-tuple-element.90.wq_ref, ...), custom_call_target="tpu_custom_call", output_to_operand_aliasing={{}: (6, {})} | custom-call | flops 8000000000 | bytes 16000000 | tf_op jit(solution)/shard_map/input/pallas_call | solution.py:630
  246.9 3.2 %collective-permute-done.11.moved_ref = bf16[768,384]{1,0:T(8,128)(2,1)S(1)} collective-permute-done((bf16[768,384]{1,0:T(8,128)(2,1)S(1)}, bf16[768,384]{1,0:T(8,128)(2,1)S(1)}, u32[]{:S(2)}, u32[]{:S(2)}) %collective-permute-start.11) | collective-permute-done | bytes 589856 | tf_op jit(solution)/shard_map/ppermute | solution.py:865
  251.7 23.2 %newton.1 = (f32[144,384]{1,0:T(8,128)}, f32[144,384]{1,0:T(8,128)}) custom-call(s32[2]{0:T(128)} %pad_add_fusion.1.info, bf16[16,48,384]{2,1,0:T(8,128)(2,1)} %copy-done.3, bf16[16,48,384]{2,1,0:T(8,128)(2,1)} %copy-done.7, bf16[768,384]{1,0:T(8,128)(2,1)} %copy-done.5, bf16[768,384]{1,0:T(8,128)(2,1)} %copy-done.6, f32[48,384]{1,0:T(8,128)} %get-tuple-element.116.mine_a, ...), custom_call_target="tpu_custom_call" | custom-call | tf_op jit(solution)/shard_map/newton/pallas_call | solution.py:603
  277.4 1.9 update.1
  (83 shorter events, 14.0 us)
Async XLA Ops:
  2.9 22.8 %all-to-all-start = ((bf16[16,36,384]{2,1,0:T(8,128)(2,1)}), bf16[16,36,384]{2,1,0:T(8,128)(2,1)S(1)}, u32[]{:S(2)}, u32[]{:S(2)}) async-start(bf16[16,36,384]{2,1,0:T(8,128)(2,1)} %get-tuple-element.78), calls=%async_computation | async-start | bytes 983040 | tf_op jit(solution)/shard_map/all_to_all | solution.py:697
  25.8 6.7 %copy-start.8 = (bf16[16,36,384]{2,1,0:T(8,128)(2,1)}, bf16[16,36,384]{2,1,0:T(8,128)(2,1)S(1)}, u32[]{:S(2)}) copy-start(bf16[16,36,384]{2,1,0:T(8,128)(2,1)S(1)} %all-to-all-done.refs_0_) | copy-start | bytes 1327108
  25.8 6.7 %collective-permute-start = (bf16[16,36,384]{2,1,0:T(8,128)(2,1)S(1)}, bf16[16,36,384]{2,1,0:T(8,128)(2,1)S(1)}, u32[]{:S(2)}, u32[]{:S(2)}) collective-permute-start(bf16[16,36,384]{2,1,0:T(8,128)(2,1)S(1)} %all-to-all-done.refs_0_), channel_id=1, source_target_pairs={{0,1},{1,0},{2,3},{3,2},{4,5},{5,4},{6,7},{7,6},{8,9},{9,8},{10,11... | collective-permute-start | bytes 1327112 | tf_op jit(solution)/shard_map/ppermute | solution.py:700
  25.8 37.6 %all-to-all-start.1 = ((bf16[16,112,384]{2,1,0:T(8,128)(2,1)}), bf16[16,112,384]{2,1,0:T(8,128)(2,1)S(1)}, u32[]{:S(2)}, u32[]{:S(2)}) async-start(bf16[16,112,384]{2,1,0:T(8,128)(2,1)} %get-tuple-element.82), calls=%async_computation.1 | async-start | bytes 2752512 | tf_op jit(solution)/shard_map/all_to_all | solution.py:697
  63.4 3.3 %copy-start.4 = (bf16[16,112,384]{2,1,0:T(8,128)(2,1)}, bf16[16,112,384]{2,1,0:T(8,128)(2,1)S(1)}, u32[]{:S(2)}) copy-start(bf16[16,112,384]{2,1,0:T(8,128)(2,1)S(1)} %all-to-all-done.1.own_ref) | copy-start | bytes 4128772
  63.4 3.3 %collective-permute-start.1 = (bf16[16,112,384]{2,1,0:T(8,128)(2,1)S(1)}, bf16[16,112,384]{2,1,0:T(8,128)(2,1)}, u32[]{:S(2)}, u32[]{:S(2)}) collective-permute-start(bf16[16,112,384]{2,1,0:T(8,128)(2,1)S(1)} %all-to-all-done.1.own_ref), channel_id=1, source_target_pairs={{0,1},{1,0},{2,3},{3,2},{4,5},{5,4},{6,7},{7,6},{8,9},{9,8},{10,11... | collective-permute-start | bytes 4128776 | tf_op jit(solution)/shard_map/ppermute | solution.py:700
  116.4 13.2 %collective-permute-start.2 = (bf16[16,104,384]{2,1,0:T(8,128)(2,1)}, bf16[16,104,384]{2,1,0:T(8,128)(2,1)S(1)}, u32[]{:S(2)}, u32[]{:S(2)}) collective-permute-start(bf16[16,104,384]{2,1,0:T(8,128)(2,1)} %get-tuple-element.85), channel_id=1, source_target_pairs={{0,1},{1,0},{2,3},{3,2},{4,5},{5,4},{6,7},{7,6},{8,9},{9,8},{10,11... | collective-permute-start | bytes 3833864 | tf_op jit(solution)/shard_map/ppermute | solution.py:700
  121.0 8.6 %copy-start.2 = (f32[16,104,384]{2,1,0:T(8,128)S(1)}, f32[16,104,384]{2,1,0:T(8,128)}, u32[]{:S(2)}) copy-start(f32[16,104,384]{2,1,0:T(8,128)} %get-tuple-element.84) | copy-start | bytes 7667716
  130.9 42.5 %all-to-all-start.2 = ((bf16[16,104,384]{2,1,0:T(8,128)(2,1)}), bf16[16,104,384]{2,1,0:T(8,128)(2,1)S(1)}, u32[]{:S(2)}, u32[]{:S(2)}) async-start(bf16[16,104,384]{2,1,0:T(8,128)(2,1)} %add_convert_fusion), calls=%async_computation.2 | async-start | bytes 2555904 | tf_op jit(solution)/shard_map/all_to_all | solution.py:697
  173.5 11.6 %copy-start = (bf16[16,104,384]{2,1,0:T(8,128)(2,1)}, bf16[16,104,384]{2,1,0:T(8,128)(2,1)S(1)}, u32[]{:S(2)}) copy-start(bf16[16,104,384]{2,1,0:T(8,128)(2,1)S(1)} %all-to-all-done.2.got_ref) | copy-start | bytes 3833860
  173.5 2.3 collective-permute-start.3
  178.1 35.9 %all-to-all-start.3 = ((bf16[16,160,128]{2,1,0:T(8,128)(2,1)}), bf16[16,160,128]{2,1,0:T(8,128)(2,1)S(1)}, u32[]{:S(2)}, u32[]{:S(2)}) async-start(bf16[16,160,128]{2,1,0:T(8,128)(2,1)} %add_convert_fusion.1), calls=%async_computation.3 | async-start | bytes 1310720 | tf_op jit(solution)/shard_map/all_to_all | solution.py:697
  188.9 1.4 collective-permute-start.4
  189.7 45.5 %collective-permute-start.9 = (f32[96,384]{1,0:T(8,128)}, f32[96,384]{1,0:T(8,128)S(1)}, u32[]{:S(2)}, u32[]{:S(2)}) collective-permute-start(f32[96,384]{1,0:T(8,128)} %get-tuple-element.117.mine_b), channel_id=1, source_target_pairs={{0,1},{1,0},{2,3},{3,2},{4,5},{5,4},{6,7},{7,6},{8,9},{9,8},{10,11... | collective-permute-start | bytes 442376 | tf_op jit(solution)/shard_map/ppermute | solution.py:700
  190.3 15.4 %collective-permute-start.5 = (bf16[96,384]{1,0:T(8,128)(2,1)S(1)}, bf16[96,384]{1,0:T(8,128)(2,1)S(1)}, u32[]{:S(2)}, u32[]{:S(2)}) collective-permute-start(bf16[96,384]{1,0:T(8,128)(2,1)S(1)} %pad_maximum_fusion.2), channel_id=1, source_target_pairs={{0,16},{1,17},{2,18},{3,19},{4,20},{5,21},{6,22},{7,23},{8,24},{9,... | collective-permute-start | bytes 221192 | tf_op jit(solution)/shard_map/ppermute | solution.py:865
  205.7 11.2 %collective-permute-start.6 = (bf16[192,384]{1,0:T(8,128)(2,1)S(1)}, bf16[192,384]{1,0:T(8,128)(2,1)S(1)}, u32[]{:S(2)}, u32[]{:S(2)}) collective-permute-start(bf16[192,384]{1,0:T(8,128)(2,1)S(1)} %pad_maximum_fusion.1), channel_id=1, source_target_pairs={{0,8},{1,9},{2,10},{3,11},{4,12},{5,13},{6,14},{7,15},{8,0},{9,1},... | collective-permute-start | bytes 442376 | tf_op jit(solution)/shard_map/ppermute | solution.py:865
  214.0 0.8 copy-start.1
  217.0 16.5 %collective-permute-start.7 = (bf16[384,384]{1,0:T(8,128)(2,1)S(1)}, bf16[384,384]{1,0:T(8,128)(2,1)S(1)}, u32[]{:S(2)}, u32[]{:S(2)}) collective-permute-start(bf16[384,384]{1,0:T(8,128)(2,1)S(1)} %pad_maximum_fusion), channel_id=1, source_target_pairs={{0,4},{1,5},{2,6},{3,7},{4,0},{5,1},{6,2},{7,3},{8,12},{9,13},{10,... | collective-permute-start | bytes 884744 | tf_op jit(solution)/shard_map/ppermute | solution.py:865
  219.4 25.3 %all-to-all-start.4 = ((bf16[16,48,384]{2,1,0:T(8,128)(2,1)}), bf16[16,48,384]{2,1,0:T(8,128)(2,1)S(1)}, u32[]{:S(2)}, u32[]{:S(2)}) async-start(bf16[16,48,384]{2,1,0:T(8,128)(2,1)} %get-tuple-element.111), calls=%async_computation.4 | async-start | bytes 1179648 | tf_op jit(solution)/shard_map/all_to_all | solution.py:697
  223.2 12.0 %collective-permute-start.8 = (f32[48,384]{1,0:T(8,128)}, f32[48,384]{1,0:T(8,128)S(1)}, u32[]{:S(2)}, u32[]{:S(2)}) collective-permute-start(f32[48,384]{1,0:T(8,128)} %get-tuple-element.116.mine_a), channel_id=1, source_target_pairs={{0,1},{1,0},{2,3},{3,2},{4,5},{5,4},{6,7},{7,6},{8,9},{9,8},{10,11... | collective-permute-start | bytes 221192 | tf_op jit(solution)/shard_map/ppermute | solution.py:700
  233.5 11.1 %copy-start.5 = (bf16[768,384]{1,0:T(8,128)(2,1)}, bf16[768,384]{1,0:T(8,128)(2,1)S(1)}, u32[]{:S(2)}) copy-start(bf16[768,384]{1,0:T(8,128)(2,1)S(1)} %constant_dynamic-update-slice_fusion.pool_ref) | copy-start | bytes 1769476
  233.5 12.6 %copy-start.14 = (f32[1536]{0:T(1024)S(1)}, f32[1536]{0:T(1024)}, u32[]{:S(2)}) copy-start(f32[1536]{0:T(1024)} %param.21) | copy-start | bytes 18436
  233.5 13.2 %copy-start.16 = (f32[12,128]{1,0:T(8,128)S(1)}, f32[12,128]{1,0:T(8,128)}, u32[]{:S(2)}) copy-start(f32[12,128]{1,0:T(8,128)} %get-tuple-element.123) | copy-start | bytes 18436
  233.6 16.5 %collective-permute-start.11 = (bf16[768,384]{1,0:T(8,128)(2,1)S(1)}, bf16[768,384]{1,0:T(8,128)(2,1)S(1)}, u32[]{:S(2)}, u32[]{:S(2)}) collective-permute-start(bf16[768,384]{1,0:T(8,128)(2,1)S(1)} %constant_dynamic-update-slice_fusion.pool_ref), channel_id=1, source_target_pairs={{0,2},{1,3},{2,0},{3,1},{4,6},{5,7},{6,4},{7,5},{8,10},{9,11},{10,... | collective-permute-start | bytes 1769480 | tf_op jit(solution)/shard_map/ppermute | solution.py:865
  235.2 9.4 %copy-start.10 = (f32[96,384]{1,0:T(8,128)}, f32[96,384]{1,0:T(8,128)S(1)}, u32[]{:S(2)}) copy-start(f32[96,384]{1,0:T(8,128)S(1)} %collective-permute-done.9.theirs_b) | copy-start | bytes 442372
  235.2 9.4 %copy-start.12 = (f32[48,384]{1,0:T(8,128)}, f32[48,384]{1,0:T(8,128)S(1)}, u32[]{:S(2)}) copy-start(f32[48,384]{1,0:T(8,128)S(1)} %collective-permute-done.8.theirs_a) | copy-start | bytes 221188
  244.6 30.3 %copy-start.11 = (f32[8,384]{1,0:T(8,128)S(1)}, f32[8,384]{1,0:T(8,128)}, u32[]{:S(2)}) copy-start(f32[8,384]{1,0:T(8,128)} %row_ref.3) | copy-start | bytes 36868
  244.7 5.5 %copy-start.3 = (bf16[16,48,384]{2,1,0:T(8,128)(2,1)}, bf16[16,48,384]{2,1,0:T(8,128)(2,1)S(1)}, u32[]{:S(2)}) copy-start(bf16[16,48,384]{2,1,0:T(8,128)(2,1)S(1)} %all-to-all-done.4.own_ref) | copy-start | bytes 1769476
  244.7 5.4 %collective-permute-start.10 = (bf16[16,48,384]{2,1,0:T(8,128)(2,1)S(1)}, bf16[16,48,384]{2,1,0:T(8,128)(2,1)S(1)}, u32[]{:S(2)}, u32[]{:S(2)}) collective-permute-start(bf16[16,48,384]{2,1,0:T(8,128)(2,1)S(1)} %all-to-all-done.4.own_ref), channel_id=1, source_target_pairs={{0,1},{1,0},{2,3},{3,2},{4,5},{5,4},{6,7},{7,6},{8,9},{9,8},{10,11... | collective-permute-start | bytes 1769480 | tf_op jit(solution)/shard_map/ppermute | solution.py:700
  245.5 33.8 %copy-start.15 = (f32[1536]{0:T(1024)}, f32[1536]{0:T(1024)S(1)}, u32[]{:S(2)}) copy-start(f32[1536]{0:T(1024)S(1)} %reshape.80) | copy-start | bytes 18436
  246.9 32.3 %copy-start.13 = (f32[8,384]{1,0:T(8,128)}, f32[8,384]{1,0:T(8,128)S(1)}, u32[]{:S(2)}) copy-start(f32[8,384]{1,0:T(8,128)S(1)} %get-tuple-element.137) | copy-start | bytes 36868
  275.0 1.7 collective-permute-start.12
  (4 other events, 3.1 us)
